TPU v7x, 256 devices: a whole 4x4x8 slice. The times are simulated.
256 devices in a mesh: log: 32 (over z, x), ctx: 8 (over y, core).
Axes of the slice: x: 4, y: 4, z: 8, core: 2. Of those that a mesh axis runs over, the one named last changes fastest.
Arguments:
- events: bfloat16 [8, 32, 512, 512], P('ctx', 'log'), may hold values from -6 to 6
- owner_ids: int32 [8, 32, 512, 1], P('ctx', 'log'), may hold values from 0 to 31; in each aligned block of 512 rows (0 to 511, 512 to 1023, ..., all dimensions but the last counted through in order) at most 20 rows name the same one
- elapsed: float32 [8, 32, 512], P('ctx', 'log'), may hold values from 0.25 to 4
- resets: float32 [8, 32, 512], P('ctx', 'log'), may hold values from 0 to 0.7
- decay_rates: float32 [4, 8], replicated, may hold values from 4.8828125e-06 to 0.04
- weights: bfloat16 [4, 4, 512, 512], replicated, may hold values from -0.25 to 0.25
- cotangent: bfloat16 [8, 32, 512, 512], P('ctx', 'log'), may hold values from -6 to 6
Outputs:
- encoded: bfloat16 [8, 32, 512, 512], P('ctx', 'log')
- event_grad: bfloat16 [8, 32, 512, 512], P('ctx', 'log')
Inputs may be any that keep to these rules, and one draw needn't show every extreme that they name: `owner_ids`: the 512 events of one device name at most 20 of them with one owner; some device names exactly 20 with some owner in every draw.
All inputs are finite; a program needn't handle non-finite values.
Results may differ from a plain program's by a relative error of at most 0.014.
Values may be sent and summed in bfloat16 or wider, within the bound.
No kernel may reach another device: no remote copies, remote signals or barrier semaphores. Data moves between devices by JAX's collectives and lax.ppermute only.
A program may use at most 64 MiB of HBM per device.

v0:
```python
import jax
import jax.numpy as jnp
from jax import lax
from jax.experimental import pallas as pl
from jax.experimental.pallas import tpu as pltpu
from jax.sharding import PartitionSpec as P


bf16 = jnp.bfloat16
f32 = jnp.float32
CH = 128
NN = (((1,), (0,)), ((), ()))
NT = (((1,), (1,)), ((), ()))
TN = (((0,), (0,)), ((), ()))
EXACT = lax.Precision.HIGHEST
LIMIT = 16 << 20


def dot(a, b, dims=NN, precision=None):
    return lax.dot_general(a, b, dims, preferred_element_type=f32, precision=precision)


def iota(shape, dim):
    return lax.broadcasted_iota(jnp.int32, shape, dim)


def ones_where(cond, dtype=bf16):
    return jnp.where(cond, 1.0, 0.0).astype(dtype)


VMEM = pl.BlockSpec(memory_space=pltpu.VMEM)
SMEM = pl.BlockSpec(memory_space=pltpu.SMEM)
HBM = pl.BlockSpec(memory_space=pltpu.HBM)


def call(body, outs, ins, scratch=(), spaces=None, out_hbm=()):
    ins = [
        pltpu.with_memory_space_constraint(v, pltpu.HBM) if (spaces or {}).get(i) is HBM else v
        for i, v in enumerate(ins)
    ]
    return pl.pallas_call(
        body,
        out_shape=[
            pltpu.HBM(s, d) if i in out_hbm else jax.ShapeDtypeStruct(s, d)
            for i, (s, d) in enumerate(outs)
        ],
        in_specs=[(spaces or {}).get(i, VMEM) for i in range(len(ins))],
        out_specs=[HBM if i in out_hbm else VMEM for i in range(len(outs))],
        scratch_shapes=list(scratch),
        compiler_params=pltpu.CompilerParams(vmem_limit_bytes=LIMIT),
    )(*ins)


def write_rows(scratch, rows_of, parts):
    count = scratch.shape[0] // parts
    for j in range(parts):
        scratch[pl.ds(j, count, stride=parts), :] = rows_of(j)


def write_message(message, scratch, rows_of, width):
    write_rows(scratch, rows_of, width // 128)
    owners = message.shape[0]
    per = scratch.shape[0] // owners
    message[:, 0:per, :] = scratch[...].reshape(owners, per, 128).astype(bf16)


def read_message(message, scratch, width):
    parts = width // 128
    count = scratch.shape[0] // parts
    owners = message.shape[0]
    per = scratch.shape[0] // owners
    scratch[...] = message[:, 0:per, :].astype(f32).reshape(scratch.shape)
    return [scratch[pl.ds(j, count, stride=parts), :] for j in range(parts)]


class Sender:
    def __init__(self, out, wide, narrow, sems, parts):
        self.out, self.wide, self.narrow, self.sems, self.parts = out, wide, narrow, sems, parts

    def copy(self, j):
        size = CH * self.parts
        span = pl.ds(pl.multiple_of(j * size, size), size)
        return pltpu.make_async_copy(self.narrow.at[span, :], self.out.at[span, :], self.sems.at[j])

    def put(self, j, value):
        size = CH * self.parts
        for p in range(self.parts):
            self.wide[pl.ds(p, CH, stride=self.parts), :] = value[:, 128 * p : 128 * (p + 1)]
        span = pl.ds(pl.multiple_of(j * size, size), size)
        self.narrow[span, :] = self.wide[...].astype(bf16)
        self.copy(j).start()

    def finish(self, blocks):
        for j in range(blocks):
            self.copy(j).wait()


def fetched(source, target, sem):
    copy = pltpu.make_async_copy(source, target, sem)
    copy.start()
    return copy


def expanded(fade, rows, p):
    here = fade[rows, :]
    shape = (here.shape[0], 128)
    return jnp.where(
        iota(shape, 1) < 64,
        jnp.broadcast_to(here[:, 2 * p : 2 * p + 1], shape),
        jnp.broadcast_to(here[:, 2 * p + 1 : 2 * p + 2], shape),
    )


def pack_events(
    owner_in, events_in, elapsed_in, resets_in, message, place,
    scratch, owner, events, elapsed, resets, sems,
):
    copies = [
        pltpu.make_async_copy(source, target, sems.at[i])
        for i, (source, target) in enumerate(
            (
                (owner_in, owner),
                (elapsed_in, elapsed),
                (resets_in, resets),
                (events_in, events),
            )
        )
    ]
    for copy in copies:
        copy.start()
    copies[0].wait()
    rows, width = events.shape
    owners = message.shape[0]
    slots = place.shape[0]
    cap = slots // owners
    own = owner[...]
    hit = iota((owners, rows), 0) == own
    earlier = ones_where(iota((rows, rows), 0) < iota((rows, rows), 1))
    before = dot(ones_where(hit), earlier)
    rank = jnp.sum(jnp.where(hit, before, 0.0), axis=0, keepdims=True).astype(jnp.int32)
    place[...] = ones_where(iota((slots, rows), 0) == own * cap + rank)
    for copy in copies[1:]:
        copy.wait()
    write_message(
        message,
        scratch,
        lambda j: dot(place[...], events[:, 128 * j : 128 * (j + 1)]),
        width,
    )
    lanes = iota((128, rows), 0)
    times = jnp.zeros((owners, 128), f32)
    for k, ref in enumerate((elapsed, resets)):
        value = ref[...]
        high = value.astype(bf16).astype(f32)
        for m, part in enumerate((high, value - high)):
            spot = ones_where(lanes == rank + cap * (2 * k + m))
            times += dot(jnp.where(hit, part, 0.0).astype(bf16), spot, NT)
    spread = ones_where(iota((owners * 8, owners), 0) == 8 * iota((owners * 8, owners), 1))
    extra = dot(spread, times.astype(bf16)).reshape(owners, 8, 128)
    per = scratch.shape[0] // owners
    message[:, per : per + 8, :] = extra.astype(bf16)


def pack_grads(info, place, grads, message, back, scratch):
    rows, width = grads.shape
    write_message(
        message,
        scratch,
        lambda j: dot(place[...], grads[:, 128 * j : 128 * (j + 1)]),
        width,
    )
    same = ones_where(iota((rows, rows), 0) == iota((rows, rows), 1))
    back[...] = dot(same, place[...], NT).astype(bf16)


def unpack_rows(back, message, out, scratch):
    width = out.shape[1]
    for j, part in enumerate(read_message(message, scratch, width)):
        out[:, 128 * j : 128 * (j + 1)] = dot(back[...], part.astype(bf16)).astype(bf16)


def halves():
    low = ones_where(iota((CH, 128), 1) < 64)
    return low, ones_where(iota((CH, 128), 1) >= 64)


def block_mask():
    return (iota((128, 128), 0) < 64) == (iota((128, 128), 1) < 64)


def stacked(value, low, high):
    return jnp.concatenate([value * low, value * high], axis=0)


def decay_pair(fade, fade_t, rows, j, p):
    causal = iota((CH, CH), 0) >= iota((CH, CH), 1)
    both, wide = [], []
    turned = fade_t[j]
    here = fade[rows, :]
    for h in (2 * p, 2 * p + 1):
        column = jnp.broadcast_to(here[:, h : h + 1], (CH, CH))
        wide.append(column)
        spread = column - turned[h : h + 1, :]
        both.append(jnp.exp(jnp.where(causal, spread, -1e30)))
    return jnp.concatenate(both, axis=1), jnp.where(iota((CH, CH), 1) < 64, wide[0], wide[1])


def folded(full):
    return full[0:64, :] + full[64:128, :]


def unfolded(half, mask):
    return jnp.where(mask, jnp.concatenate([half, half], axis=0), 0.0)


def write_state(send, state, last, pairs):
    for p in range(pairs):
        send[64 * p : 64 * (p + 1), :] = folded(state[p]).astype(bf16)
    write_marks(send, last, pairs)


def write_marks(send, last, pairs):
    last = jnp.broadcast_to(last, (8, 128))
    high = last.astype(bf16).astype(f32)
    lane = iota(last.shape, 1)
    send[64 * pairs : 64 * pairs + 8, :] = jnp.where(lane < 64, high, last - high).astype(bf16)


def read_marks(ref, pairs):
    marks = ref[64 * pairs : 64 * pairs + 8, :].astype(f32)
    return marks[:, 0:1] + marks[:, 64:65]


def lane_factors(log, p):
    return jnp.exp(
        jnp.where(
            iota((1, 128), 1) < 64,
            jnp.broadcast_to(log[2 * p : 2 * p + 1, :], (1, 128)),
            jnp.broadcast_to(log[2 * p + 1 : 2 * p + 2, :], (1, 128)),
        )
    )


def join_pair(near, far, out, pairs):
    log = read_marks(near, pairs)
    for p in range(pairs):
        rows = slice(64 * p, 64 * (p + 1))
        joined = near[rows, :].astype(f32) + lane_factors(log, p) * far[rows, :].astype(f32)
        out[rows, :] = joined.astype(bf16)
    write_marks(out, log + read_marks(far, pairs), pairs)


def join_ahead(info, own, other, out):
    join(info[1] == 1, own, other, out)


def join_back(info, own, other, out):
    join(info[1] == 0, own, other, out)


def join(own_is_near, own, other, out):
    pairs = own.shape[0] // 64

    @pl.when(own_is_near)
    def _():
        join_pair(own, other, out, pairs)

    @pl.when(jnp.logical_not(own_is_near))
    def _():
        join_pair(other, own, out, pairs)


def gathered_state(partner_counts, partner, received, pairs):
    log = read_marks(partner, pairs) * partner_counts
    total = [partner[64 * p : 64 * (p + 1), :].astype(f32) * partner_counts for p in range(pairs)]
    for ref in received:
        for p in range(pairs):
            total[p] += lane_factors(log, p) * ref[64 * p : 64 * (p + 1), :].astype(f32)
        log = log + read_marks(ref, pairs)
    return total


def forward_state(
    info, rates, message_in, weights,
    x_out, keys, values, keys_out, values_out, fade, fade_t, marks, send,
    scratch, memory, message, mine, x, sems,
):
    arrival = fetched(message_in, message, sems.at[0])
    fetch = fetched(weights.at[info[0], pl.ds(1, 2)], mine, sems.at[1])
    slots, width = x.shape
    pairs = width // 128
    blocks = slots // CH
    owners = message.shape[0]
    cap = slots // owners
    per = cap * pairs
    arrival.wait()
    for j, part in enumerate(read_message(message, scratch, width)):
        x[:, 128 * j : 128 * (j + 1)] = part.astype(bf16)
    stores = [fetched(x, x_out, sems.at[2])]
    times = message[:, per : per + 8, :].astype(f32).reshape(owners * 8, 128).astype(bf16)
    r = iota((slots, owners * 8), 0)
    c = iota((slots, owners * 8), 1)
    expand = ones_where(((c & 7) == 0) & (8 * r >= cap * c) & (8 * r < cap * (c + 8)))
    wide = dot(expand, times)
    row = iota((slots, 128), 0).astype(f32)
    lane = iota((slots, 128), 1).astype(f32)
    s = row - cap * jnp.floor((row + 0.5) * (1.0 / cap))
    hit = (lane == s) | (lane == s + cap) | (lane == s + 2 * cap) | (lane == s + 3 * cap)
    own = jnp.where(hit, wide, 0.0).astype(bf16)
    tri = ones_where(iota((slots, slots), 0) >= iota((slots, slots), 1))
    running = dot(tri, own)
    kind = iota((128, 128), 0)
    head = iota((128, 128), 1)
    kind_t = iota((8, 128), 1)
    head_t = iota((8, 128), 0)
    rate = jnp.zeros((128, 128), f32)
    rate_t = jnp.zeros((8, 128), f32)
    for h in range(rates.shape[1]):
        value = rates[info[0], h]
        rate = jnp.where(head == h, value, rate)
        rate_t = jnp.where(head_t == h, value, rate_t)
    to_heads = jnp.where(kind < 2 * cap, -rate, jnp.where(kind < 4 * cap, -1.0, 0.0))
    fade[...] = dot(running, to_heads, NN, EXACT)
    to_heads = jnp.where(kind_t < 2 * cap, -rate_t, jnp.where(kind_t < 4 * cap, -1.0, 0.0))
    turned = dot(to_heads, running, NT, EXACT)
    for j in range(blocks):
        fade_t[j] = turned[:, CH * j : CH * (j + 1)]
    for j in range(blocks):
        for p in range(pairs):
            if j == 0:
                marks[j, p : p + 1, :] = jnp.zeros((1, 128), f32)
            else:
                marks[j, p : p + 1, :] = expanded(fade, slice(CH * j - 1, CH * j), p)
            end = slice(CH * j + CH - 1, CH * j + CH)
            marks[j, pairs + p : pairs + p + 1, :] = expanded(fade, end, p)
    fetch.wait()
    memory[...] = jnp.zeros(memory.shape, f32)
    mask = block_mask()

    def project(j, carry):
        rows = pl.ds(pl.multiple_of(j * CH, CH), CH)
        here = x[rows, :]
        k = dot(here, mine[0]).astype(bf16)
        v = dot(here, mine[1]).astype(bf16)
        keys[rows, :] = k
        values[rows, :] = v
        for p in range(pairs):
            cols = slice(128 * p, 128 * (p + 1))
            end = marks[blocks - 1, pairs + p : pairs + p + 1, :]
            kf = (k[:, cols].astype(f32) * jnp.exp(end - expanded(fade, rows, p))).astype(bf16)
            memory[p] += jnp.where(mask, dot(kf, v[:, cols], TN), 0.0)
        return carry

    lax.fori_loop(0, blocks, project, 0)
    stores.append(fetched(keys, keys_out, sems.at[3]))
    stores.append(fetched(values, values_out, sems.at[4]))
    write_state(send, memory, turned[:, slots - 1 : slots], pairs)
    for store in stores:
        store.wait()


def project_queries(info, x_in, weights, q8, mine, x, sems):
    arrival = fetched(x_in, x, sems.at[0])
    fetched(weights.at[info[0], 0], mine, sems.at[1]).wait()
    arrival.wait()

    def project(j, carry):
        rows = pl.ds(pl.multiple_of(j * CH, CH), CH)
        q8[rows, :] = (dot(x[rows, :], mine[...]).astype(bf16).astype(f32) * 0.125).astype(bf16)
        return carry

    lax.fori_loop(0, x.shape[0] // CH, project, 0)


def attend(q8, keys, values, fade, fade_t, marks, attended, states, memory):
    slots, width = q8.shape
    pairs = width // 128
    low, high = halves()
    mask = block_mask()
    memory[...] = jnp.zeros(memory.shape, f32)

    def block(j, carry):
        rows = pl.ds(pl.multiple_of(j * CH, CH), CH)
        edge = marks[j]
        for p in range(pairs):
            cols = slice(128 * p, 128 * (p + 1))
            start, end = edge[p : p + 1, :], edge[pairs + p : pairs + p + 1, :]
            qp, kp, vp = q8[rows, cols], keys[rows, cols], values[rows, cols]
            scores = dot(qp, stacked(kp, low, high), NT)
            fading, g = decay_pair(fade, fade_t, rows, j, p)
            mix = (scores * fading).astype(bf16)
            within = dot(mix, stacked(vp, low, high))
            now = memory[p]
            states[j, p] = folded(now).astype(bf16)
            lifted = (qp.astype(f32) * jnp.exp(g - start)).astype(bf16)
            attended[rows, cols] = within + dot(lifted, now.astype(bf16))
            kf = (kp.astype(f32) * jnp.exp(end - g)).astype(bf16)
            memory[p] = jnp.exp(end - start) * now + jnp.where(mask, dot(kf, vp, TN), 0.0)
        return carry

    lax.fori_loop(0, slots // CH, block, 0)


def turn(info, q8, fade, fade_t, attended, x_in, weights, message_in, partner, *rest):
    received = rest[:-15]
    (
        encoded, grads, grad_full, incoming, send,
        scratch, message, mine, x, wide, narrow, states, memory, sems, out_sems,
    ) = rest[-15:]
    arrival = fetched(message_in, message, sems.at[0])
    fetch = fetched(weights.at[info[0], 3], mine, sems.at[1])
    rows_in = fetched(x_in, x, sems.at[2])
    slots, width = x.shape
    pairs = width // 128
    blocks = slots // CH
    mask = block_mask()
    for p, state in enumerate(gathered_state(info[1].astype(f32), partner, received, pairs)):
        incoming[p] = state
        states[p] = unfolded(state, mask).astype(bf16)
    memory[...] = jnp.zeros(memory.shape, f32)
    arrival.wait()
    for j, part in enumerate(read_message(message, scratch, width)):
        grads[:, 128 * j : 128 * (j + 1)] = part.astype(bf16)
    fetch.wait()
    rows_in.wait()
    sender = Sender(encoded, wide, narrow, out_sems, pairs)

    def block(j, carry):
        rows = pl.ds(pl.multiple_of(j * CH, CH), CH)
        values, lifts = [], []
        square = jnp.zeros((CH, 1), f32)
        for p in range(pairs):
            cols = slice(128 * p, 128 * (p + 1))
            lifted = (q8[rows, cols].astype(f32) * jnp.exp(expanded(fade, rows, p))).astype(bf16)
            lifts.append(lifted)
            value = attended[rows, cols] + dot(lifted, states[p])
            values.append(value)
            square += jnp.sum(value * value, axis=1, keepdims=True)
        here = jnp.concatenate(values, axis=1)
        scale = lax.rsqrt(square * (1.0 / width) + 1e-06)
        normed = (here * scale).astype(bf16)
        sender.put(j, x[rows, :].astype(f32) + dot(normed, mine[...]))
        grad = dot(grads[rows, :], mine[...], NT).astype(bf16).astype(f32)
        along = jnp.mean(here * grad, axis=1, keepdims=True)
        da = (scale * grad - here * (scale * scale * scale * along)).astype(bf16)
        grad_full[rows, :] = da
        for p in range(pairs):
            cols = slice(128 * p, 128 * (p + 1))
            memory[p] += jnp.where(mask, dot(lifts[p], da[:, cols], TN), 0.0)
        return carry

    lax.fori_loop(0, blocks, block, 0)
    write_state(send, memory, fade_t[blocks - 1][:, CH - 1 : CH], pairs)
    sender.finish(blocks)


def backward_local(
    q8, keys, values, fade, fade_t, marks, grad_full, states, incoming,
    grad_q, grad_keys, grad_values, memory,
):
    slots, width = q8.shape
    pairs = width // 128
    blocks = slots // CH
    low, high = halves()
    lower = iota((CH, 128), 1) < 64
    mask = block_mask()
    memory[...] = jnp.zeros(memory.shape, f32)

    def block(i, carry):
        j = blocks - 1 - i
        rows = pl.ds(pl.multiple_of(j * CH, CH), CH)
        edge = marks[j]
        for p in range(pairs):
            cols = slice(128 * p, 128 * (p + 1))
            start, end = edge[p : p + 1, :], edge[pairs + p : pairs + p + 1, :]
            qp, kp, vp = q8[rows, cols], keys[rows, cols], values[rows, cols]
            da = grad_full[rows, cols]
            ks, vs = stacked(kp, low, high), stacked(vp, low, high)
            fading, g = decay_pair(fade, fade_t, rows, j, p)
            mix = (dot(qp, ks, NT) * fading).astype(bf16)
            grad_scores = (dot(da, vs, NT) * fading).astype(bf16)
            lift = jnp.exp(g - start)
            fall = jnp.exp(end - g)
            state = states[j, p].astype(f32) + jnp.exp(start) * incoming[p]
            state = unfolded(state, mask).astype(bf16)
            grad_q[rows, cols] = (
                0.125 * (dot(grad_scores, ks) + lift * dot(da, state, NT))
            ).astype(bf16)
            gk = dot(grad_scores, qp, TN)
            gv = dot(mix, da, TN)
            now = memory[p]
            narrow = now.astype(bf16)
            kf = (kp.astype(f32) * fall).astype(bf16)
            grad_keys[rows, cols] = jnp.where(lower, gk[0:CH], gk[CH:]) + fall * dot(vp, narrow, NT)
            grad_values[rows, cols] = jnp.where(lower, gv[0:CH], gv[CH:]) + dot(kf, narrow)
            lifted = (qp.astype(f32) * lift).astype(bf16)
            memory[p] = jnp.exp(end - start) * now + jnp.where(mask, dot(lifted, da, TN), 0.0)
        return carry

    lax.fori_loop(0, blocks, block, 0)


def project_back(info, grads, grad_q, weights, partial, mine, sem):
    fetched(weights.at[info[0], 0], mine, sem).wait()

    def project(j, carry):
        rows = pl.ds(pl.multiple_of(j * CH, CH), CH)
        partial[rows, :] = grads[rows, :].astype(f32) + dot(grad_q[rows, :], mine[...], NT)
        return carry

    lax.fori_loop(0, grads.shape[0] // CH, project, 0)


def backward_finish(
    info, partial, grad_keys, grad_values, keys, values, fade, marks, weights, partner, *rest
):
    received = rest[:-9]
    out, mine, wide, narrow, states, gk, gv, sem, out_sems = rest[-9:]
    fetch = fetched(weights.at[info[0], pl.ds(1, 2)], mine, sem)
    slots, width = partial.shape
    pairs = width // 128
    blocks = slots // CH
    mask = block_mask()
    arrived = gathered_state((1 - info[1]).astype(f32), partner, received, pairs)
    for p, state in enumerate(arrived):
        states[p] = unfolded(state, mask).astype(bf16)
    sender = Sender(out, wide, narrow, out_sems, pairs)
    fetch.wait()

    def block(j, carry):
        rows = pl.ds(pl.multiple_of(j * CH, CH), CH)
        for p in range(pairs):
            cols = slice(128 * p, 128 * (p + 1))
            end = marks[blocks - 1, pairs + p : pairs + p + 1, :]
            fall = jnp.exp(end - expanded(fade, rows, p))
            kf = (keys[rows, cols].astype(f32) * fall).astype(bf16)
            state = states[p]
            gk[:, cols] = (grad_keys[rows, cols] + fall * dot(values[rows, cols], state, NT)).astype(bf16)
            gv[:, cols] = (grad_values[rows, cols] + dot(kf, state)).astype(bf16)
        sender.put(j, partial[rows, :] + dot(gk[...], mine[0], NT) + dot(gv[...], mine[1], NT))
        return carry

    lax.fori_loop(0, blocks, block, 0)
    sender.finish(blocks)


def swapped(value, axis):
    return lax.ppermute(value, axis, [(i, i ^ 1) for i in range(lax.axis_size(axis))])


def exchange(value, axis, sign):
    count = lax.axis_size(axis)
    return [
        lax.ppermute(
            value, axis, [(i, i + sign * k) for i in range(count) if 0 <= i + sign * k < count]
        )
        for k in range(2, count, 2)
    ]


def regroup(value):
    return lax.all_to_all(value, "log", split_axis=0, concat_axis=0, tiled=True)


def shards(events, owner_ids, elapsed, resets, decay_rates, weights, cotangent):
    rows, width = events.shape[2:]
    owners = lax.axis_size("log")
    cap = 5 * rows // (4 * owners)
    slots = owners * cap
    pairs = width // 128
    blocks = slots // CH
    per = cap * pairs
    flat = pltpu.VMEM((slots * pairs, 128), f32)
    state_vmem = pltpu.VMEM((pairs, 128, 128), f32)
    state_msg = ((64 * pairs + 8, 128), bf16)
    wide_msg = ((owners, per, 128), bf16)
    wide16, wide32 = ((slots, width), bf16), ((slots, width), f32)

    tower = lax.axis_index("log") // (owners // decay_rates.shape[0])
    info = jnp.stack([tower, lax.axis_index("ctx") % 2]).astype(jnp.int32)

    message, place = call(
        pack_events,
        [((owners, per + 8, 128), bf16), ((slots, rows), bf16)],
        [
            owner_ids.reshape(1, rows),
            events.reshape(rows, width),
            elapsed.reshape(1, rows),
            resets.reshape(1, rows),
        ],
        [
            flat,
            pltpu.VMEM((1, rows), jnp.int32),
            pltpu.VMEM((rows, width), bf16),
            pltpu.VMEM((1, rows), f32),
            pltpu.VMEM((1, rows), f32),
            pltpu.SemaphoreType.DMA((4,)),
        ],
        {0: HBM, 1: HBM, 2: HBM, 3: HBM},
    )
    events_in = regroup(message)
    message, back = call(
        pack_grads,
        [wide_msg, ((rows, slots), bf16)],
        [info, place, cotangent.reshape(rows, width)],
        [flat],
        {0: SMEM},
    )
    grads_in = regroup(message)
    one = pltpu.VMEM((width, width), bf16)
    two = pltpu.VMEM((2, width, width), bf16)
    sem = pltpu.SemaphoreType.DMA
    half_states = ((pairs, 64, 128), f32)
    flat_msg = ((slots * pairs, 128), bf16)
    block_wide = pltpu.VMEM((CH * pairs, 128), f32)
    flat_narrow = pltpu.VMEM(*flat_msg)
    rows16 = pltpu.VMEM(*wide16)
    narrow_states = pltpu.VMEM((pairs, 128, 128), bf16)
    x, keys, values, keys_far, values_far, fade, fade_t, marks, send = call(
        forward_state,
        [
            wide16, wide16, wide16, wide16, wide16, ((slots, 128), f32), ((blocks, 8, 128), f32),
            ((blocks, 2 * pairs, 128), f32), state_msg,
        ],
        [info, decay_rates, events_in, weights],
        [flat, state_vmem, pltpu.VMEM((owners, per + 8, 128), bf16), two, rows16, sem((5,))],
        {0: SMEM, 1: SMEM, 2: HBM, 3: HBM},
        (0, 3, 4),
    )
    partner = swapped(send, "ctx")
    (q8,) = call(
        project_queries,
        [wide16],
        [info, x, weights],
        [one, rows16, sem((2,))],
        {0: SMEM, 1: HBM, 2: HBM},
    )
    (joined,) = call(join_ahead, [state_msg], [info, send, partner], (), {0: SMEM})
    received = exchange(joined, "ctx", 1)
    attended, kept = call(
        attend,
        [wide32, ((blocks, pairs, 64, 128), bf16)],
        [q8, keys, values, fade, fade_t, marks],
        [state_vmem],
    )
    message, grads, grad_full, incoming, send = call(
        turn,
        [flat_msg, wide16, wide16, half_states, state_msg],
        [info, q8, fade, fade_t, attended, x, weights, grads_in, partner, *received],
        [
            flat, pltpu.VMEM(*wide_msg), one, rows16, block_wide, flat_narrow, narrow_states,
            state_vmem, sem((3,)), sem((blocks,)),
        ],
        {0: SMEM, 5: HBM, 6: HBM, 7: HBM},
        (0,),
    )
    partner = swapped(send, "ctx")
    encoded_in = regroup(message.reshape(owners, per, 128))
    grad_q, grad_keys, grad_values = call(
        backward_local,
        [wide16, wide32, wide32],
        [q8, keys_far, values_far, fade, fade_t, marks, grad_full, kept, incoming],
        [state_vmem],
    )
    (joined,) = call(join_back, [state_msg], [info, send, partner], (), {0: SMEM})
    received = exchange(joined, "ctx", -1)
    (partial,) = call(
        project_back, [wide32], [info, grads, grad_q, weights], [one, sem], {0: SMEM, 3: HBM}
    )
    (message,) = call(
        backward_finish,
        [flat_msg],
        [
            info, partial, grad_keys, grad_values, keys_far, values_far, fade, marks, weights,
            partner, *received,
        ],
        [
            two, block_wide, flat_narrow, narrow_states,
            pltpu.VMEM((CH, width), bf16), pltpu.VMEM((CH, width), bf16), sem, sem((blocks,)),
        ],
        {0: SMEM, 8: HBM},
        (0,),
    )
    grad_in = regroup(message.reshape(owners, per, 128))
    (encoded,) = call(unpack_rows, [((rows, width), bf16)], [back, encoded_in], [flat])
    (grad,) = call(unpack_rows, [((rows, width), bf16)], [back, grad_in], [flat])
    return encoded.reshape(events.shape), grad.reshape(events.shape)


def solution(mesh):
    wide = P("ctx", "log", None, None)
    flat = P("ctx", "log", None)
    return jax.shard_map(
        shards,
        mesh=mesh,
        in_specs=(wide, wide, flat, flat, P(), P(), wide),
        out_specs=(wide, wide),
        check_vma=False,
    )
```

profile of v0, /device:TPU:24, one launch (start us, length us, event | category | flops | bytes accessed | tf_op | source)
XLA Modules:
  0.0 150.6 jit_solution(10063887386587054816)
XLA Ops:
  0.6 3.3 %shard_map.86 = (bf16[32,88,128]{2,1,0:T(8,128)(2,1)}, bf16[640,512]{1,0:T(8,128)(2,1)S(1)}) custom-call(s32[1,512]{1,0:T(1,128)} %bitcast.17, bf16[512,512]{1,0:T(8,128)(2,1)} %bitcast.16, f32[1,512]{1,0:T(1,128)} %bitcast.18, f32[1,512]{1,0:T(1,128)} %bitcast.19), custom_call_target="tpu_custom_call" | custom-call | tf_op jit(solution)/shard_map/pallas_call | solution.py:41
  4.0 11.3 %all-to-all-start = ((bf16[32,88,128]{2,1,0:T(8,128)(2,1)}), bf16[32,88,128]{2,1,0:T(8,128)(2,1)S(1)}, u32[]{:S(2)}, u32[]{:S(2)}) async-start(bf16[32,88,128]{2,1,0:T(8,128)(2,1)} %get-tuple-element.27), calls=%async_computation | async-start | bytes 1441792 | tf_op jit(solution)/shard_map/all_to_all | solution.py:562
  15.4 2.4 %shard_map.87 = (bf16[32,80,128]{2,1,0:T(8,128)(2,1)}, bf16[512,640]{1,0:T(8,128)(2,1)S(1)}) custom-call(s32[2]{0:T(128)S(1)} %pad_add_fusion.info, bf16[640,512]{1,0:T(8,128)(2,1)S(1)} %get-tuple-element.25.place, bf16[512,512]{1,0:T(8,128)(2,1)S(1)} %bitcast.11), custom_call_target="tpu_custom_call" | custom-call | tf_op jit(solution)/shard_map/pallas_call | solution.py:41
  17.9 19.1 %all-to-all-done.message_in = bf16[32,88,128]{2,1,0:T(8,128)(2,1)S(1)} async-done(((bf16[32,88,128]{2,1,0:T(8,128)(2,1)}), bf16[32,88,128]{2,1,0:T(8,128)(2,1)S(1)}, u32[]{:S(2)}, u32[]{:S(2)}) %all-to-all-start) | async-done | bytes 720928 | tf_op jit(solution)/shard_map/all_to_all | solution.py:562
  36.9 5.1 %all-to-all-start.1 = ((bf16[32,80,128]{2,1,0:T(8,128)(2,1)}), bf16[32,80,128]{2,1,0:T(8,128)(2,1)}, u32[]{:S(2)}, u32[]{:S(2)}) async-start(bf16[32,80,128]{2,1,0:T(8,128)(2,1)} %get-tuple-element.35), calls=%async_computation.1 | async-start | bytes 1310720 | tf_op jit(solution)/shard_map/all_to_all | solution.py:562
  42.1 6.5 %shard_map.88 = (bf16[640,512]{1,0:T(8,128)(2,1)}, bf16[640,512]{1,0:T(8,128)(2,1)S(1)}, bf16[640,512]{1,0:T(8,128)(2,1)S(1)}, bf16[640,512]{1,0:T(8,128)(2,1)},...) custom-call(s32[2]{0:T(128)S(1)} %pad_add_fusion.info, ...), custom_call_target="tpu_custom_call" | custom-call | tf_op jit(solution)/shard_map/pallas_call | solution.py:41
  49.9 1.3 shard_map.91
  52.5 1.3 collective-permute-start.2
  53.8 1.3 collective-permute-start.3
  55.1 3.0 %shard_map.89.q8 = bf16[640,512]{1,0:T(8,128)(2,1)S(1)} custom-call(s32[2]{0:T(128)S(1)} %pad_add_fusion.info, bf16[640,512]{1,0:T(8,128)(2,1)} %get-tuple-element.28.x_in, bf16[4,4,512,512]{3,2,1,0:T(8,128)(2,1)} %weights.9), custom_call_target="tpu_custom_call" | custom-call | tf_op jit(solution)/shard_map/pallas_call | solution.py:41
  58.1 4.0 %shard_map.90 = (f32[640,512]{1,0:T(8,128)S(1)}, bf16[5,4,64,128]{3,2,1,0:T(8,128)(2,1)S(1)}) custom-call(bf16[640,512]{1,0:T(8,128)(2,1)S(1)} %shard_map.89.q8, bf16[640,512]{1,0:T(8,128)(2,1)S(1)} %get-tuple-element.31.keys, bf16[640,512]{1,0:T(8,128)(2,1)S(1)} %get-tuple-element.32.values, f32[640,128]{1,0:T(8,128)S(1)} %get-tuple-element.29.fade, ...), custom_call_target="tpu_custom_call" | custom-call | tf_op jit(solution)/shard_map/pallas_call | solution.py:41
  65.4 8.2 %shard_map.92 = (bf16[2560,128]{1,0:T(8,128)(2,1)}, bf16[640,512]{1,0:T(8,128)(2,1)S(1)}, bf16[640,512]{1,0:T(8,128)(2,1)S(1)}, f32[4,64,128]{2,1,0:T(8,128)S(1)}, bf16[264,128]{1,0:T(8,128)(2,1)S(1)}) custom-call(s32[2]{0:T(128)S(1)} %pad_add_fusion.info, bf16[640,512]{1,0:T(8,128)(2,1)S(1)} %shard_map.89.q8, f32[640,128]{1,0:T(8,128)S(1)} %get-tuple-element.29.fade, ...), custom_call_target="tpu_custom_call" | custom-call | tf_op jit(solution)/shard_map/pallas_call | solution.py:41
  75.9 10.0 %all-to-all-start.2 = ((bf16[32,80,128]{2,1,0:T(8,128)(2,1)}), bf16[32,80,128]{2,1,0:T(8,128)(2,1)}, u32[]{:S(2)}, u32[]{:S(2)}) async-start(bf16[32,80,128]{2,1,0:T(8,128)(2,1)} %bitcast.13), calls=%async_computation.2 | async-start | bytes 1310720 | tf_op jit(solution)/shard_map/all_to_all | solution.py:562
  86.0 1.5 collective-permute-done.4.other.partner
  89.0 4.4 %collective-permute-start.5 = (bf16[264,128]{1,0:T(8,128)(2,1)S(1)}, bf16[264,128]{1,0:T(8,128)(2,1)S(1)}, u32[]{:S(2)}, u32[]{:S(2)}) collective-permute-start(bf16[264,128]{1,0:T(8,128)(2,1)S(1)} %shard_map.96), channel_id=1, source_target_pairs={{2,0},{3,1},{4,2},{5,3},{6,4},{7,5},{10,8},{11,9},{12,10},{13,11},... | collective-permute-start | bytes 202760 | tf_op jit(solution)/shard_map/ppermute | solution.py:554
  93.4 7.3 %collective-permute-start.6 = (bf16[264,128]{1,0:T(8,128)(2,1)S(1)}, bf16[264,128]{1,0:T(8,128)(2,1)S(1)}, u32[]{:S(2)}, u32[]{:S(2)}) collective-permute-start(bf16[264,128]{1,0:T(8,128)(2,1)S(1)} %shard_map.96), channel_id=1, source_target_pairs={{4,0},{5,1},{6,2},{7,3},{12,8},{13,9},{14,10},{15,11},{20,16},{21,... | collective-permute-start | bytes 202760 | tf_op jit(solution)/shard_map/ppermute | solution.py:554
  100.7 1.3 collective-permute-start.7
  103.1 6.6 %shard_map.94 = (bf16[640,512]{1,0:T(8,128)(2,1)S(1)}, f32[640,512]{1,0:T(8,128)S(1)}, f32[640,512]{1,0:T(8,128)S(1)}) custom-call(bf16[640,512]{1,0:T(8,128)(2,1)S(1)} %shard_map.89.q8, bf16[640,512]{1,0:T(8,128)(2,1)S(1)} %copy-done, bf16[640,512]{1,0:T(8,128)(2,1)S(1)} %copy-done.1, f32[640,128]{1,0:T(8,128)S(1)} %get-tuple-element.29.fade, ...), custom_call_target="tpu_custom_call" | custom-call | tf_op jit(solution)/shard_map/pallas_call | solution.py:41
  109.8 3.1 %shard_map.95.partial = f32[640,512]{1,0:T(8,128)S(1)} custom-call(s32[2]{0:T(128)S(1)} %pad_add_fusion.info, bf16[640,512]{1,0:T(8,128)(2,1)S(1)} %copy-done.3, bf16[640,512]{1,0:T(8,128)(2,1)S(1)} %get-tuple-element.44.grad_q, bf16[4,4,512,512]{3,2,1,0:T(8,128)(2,1)} %weights.9), custom_call_target="tpu_custom_call" | custom-call | tf_op jit(solution)/shard_map/pallas_call | solution.py:41
  113.0 6.2 %shard_map.97 = bf16[2560,128]{1,0:T(8,128)(2,1)} custom-call(s32[2]{0:T(128)S(1)} %pad_add_fusion.info, f32[640,512]{1,0:T(8,128)S(1)} %shard_map.95.partial, f32[640,512]{1,0:T(8,128)S(1)} %get-tuple-element.45.grad_keys, f32[640,512]{1,0:T(8,128)S(1)} %get-tuple-element.46.grad_values, bf16[640,512]{1,0:T(8,128)(2,1)S(1)} %copy-done, ...), custom_call_target="tpu_custom_call" | custom-call | tf_op jit(solution)/shard_map/pallas_call | solution.py:41
  119.2 9.7 %all-to-all-start.3 = ((bf16[32,80,128]{2,1,0:T(8,128)(2,1)}), bf16[32,80,128]{2,1,0:T(8,128)(2,1)S(1)}, u32[]{:S(2)}, u32[]{:S(2)}) async-start(bf16[32,80,128]{2,1,0:T(8,128)(2,1)} %bitcast.12), calls=%async_computation.3 | async-start | bytes 1310720 | tf_op jit(solution)/shard_map/all_to_all | solution.py:562
  128.9 2.8 %shard_map.93 = bf16[512,512]{1,0:T(8,128)(2,1)} custom-call(bf16[512,640]{1,0:T(8,128)(2,1)S(1)} %get-tuple-element.26.back, bf16[32,80,128]{2,1,0:T(8,128)(2,1)} %all-to-all-done.2.message), custom_call_target="tpu_custom_call" | custom-call | tf_op jit(solution)/shard_map/pallas_call | solution.py:41
  131.7 17.2 %all-to-all-done.3.message = bf16[32,80,128]{2,1,0:T(8,128)(2,1)S(1)} async-done(((bf16[32,80,128]{2,1,0:T(8,128)(2,1)}), bf16[32,80,128]{2,1,0:T(8,128)(2,1)S(1)}, u32[]{:S(2)}, u32[]{:S(2)}) %all-to-all-start.3) | async-done | bytes 655392 | tf_op jit(solution)/shard_map/all_to_all | solution.py:562
  148.9 1.7 %shard_map.98 = bf16[512,512]{1,0:T(8,128)(2,1)} custom-call(bf16[512,640]{1,0:T(8,128)(2,1)S(1)} %get-tuple-element.26.back, bf16[32,80,128]{2,1,0:T(8,128)(2,1)S(1)} %all-to-all-done.3.message), custom_call_target="tpu_custom_call" | custom-call | tf_op jit(solution)/shard_map/pallas_call | solution.py:41
  (44 shorter events, 11.0 us)
Async XLA Ops:
  0.6 14.8 %copy-start.6 = (bf16[1,1,512,512]{3,2,1,0:T(8,128)(2,1)S(1)}, bf16[1,1,512,512]{3,2,1,0:T(8,128)(2,1)}, u32[]{:S(2)}) copy-start(bf16[1,1,512,512]{3,2,1,0:T(8,128)(2,1)} %param.13) | copy-start | bytes 1572868
  4.0 33.0 %all-to-all-start = ((bf16[32,88,128]{2,1,0:T(8,128)(2,1)}), bf16[32,88,128]{2,1,0:T(8,128)(2,1)S(1)}, u32[]{:S(2)}, u32[]{:S(2)}) async-start(bf16[32,88,128]{2,1,0:T(8,128)(2,1)} %get-tuple-element.27), calls=%async_computation | async-start | bytes 1441792 | tf_op jit(solution)/shard_map/all_to_all | solution.py:562
  15.3 26.7 %copy-start.13 = (f32[4,8]{1,0:T(4,128)S(1)}, f32[4,8]{1,0:T(4,128)}, u32[]{:S(2)}) copy-start(f32[4,8]{1,0:T(4,128)} %rates.1) | copy-start | bytes 388
  36.9 5.1 %copy-start.14 = (bf16[32,88,128]{2,1,0:T(8,128)(2,1)}, bf16[32,88,128]{2,1,0:T(8,128)(2,1)S(1)}, u32[]{:S(2)}) copy-start(bf16[32,88,128]{2,1,0:T(8,128)(2,1)S(1)} %all-to-all-done.message_in) | copy-start | bytes 2162692
  36.9 25.2 %all-to-all-start.1 = ((bf16[32,80,128]{2,1,0:T(8,128)(2,1)}), bf16[32,80,128]{2,1,0:T(8,128)(2,1)}, u32[]{:S(2)}, u32[]{:S(2)}) async-start(bf16[32,80,128]{2,1,0:T(8,128)(2,1)} %get-tuple-element.35), calls=%async_computation.1 | async-start | bytes 1310720 | tf_op jit(solution)/shard_map/all_to_all | solution.py:562
  48.5 1.3 collective-permute-start
  51.2 10.9 %collective-permute-start.1 = (bf16[264,128]{1,0:T(8,128)(2,1)}, bf16[264,128]{1,0:T(8,128)(2,1)S(1)}, u32[]{:S(2)}, u32[]{:S(2)}) collective-permute-start(bf16[264,128]{1,0:T(8,128)(2,1)} %shard_map.91), channel_id=1, source_target_pairs={{0,2},{1,3},{2,4},{3,5},{4,6},{5,7},{8,10},{9,11},{10,12},{11,13},... | collective-permute-start | bytes 202760 | tf_op jit(solution)/shard_map/ppermute | solution.py:554
  52.5 10.3 %collective-permute-start.2 = (bf16[264,128]{1,0:T(8,128)(2,1)}, bf16[264,128]{1,0:T(8,128)(2,1)S(1)}, u32[]{:S(2)}, u32[]{:S(2)}) collective-permute-start(bf16[264,128]{1,0:T(8,128)(2,1)} %shard_map.91), channel_id=1, source_target_pairs={{0,4},{1,5},{2,6},{3,7},{8,12},{9,13},{10,14},{11,15},{16,20},{17,... | collective-permute-start | bytes 202760 | tf_op jit(solution)/shard_map/ppermute | solution.py:554
  53.8 9.8 %collective-permute-start.3 = (bf16[264,128]{1,0:T(8,128)(2,1)}, bf16[264,128]{1,0:T(8,128)(2,1)}, u32[]{:S(2)}, u32[]{:S(2)}) collective-permute-start(bf16[264,128]{1,0:T(8,128)(2,1)} %shard_map.91), channel_id=1, source_target_pairs={{0,6},{1,7},{8,14},{9,15},{16,22},{17,23},{24,30},{25,31},{32,38},... | collective-permute-start | bytes 202760 | tf_op jit(solution)/shard_map/ppermute | solution.py:554
  63.6 0.9 copy-start.8
  64.5 0.9 copy-start.10
  73.6 0.9 copy-start.2
  74.4 0.8 copy-start.4
  75.9 26.1 %copy-start = (bf16[640,512]{1,0:T(8,128)(2,1)S(1)}, bf16[640,512]{1,0:T(8,128)(2,1)}, u32[]{:S(2)}) copy-start(bf16[640,512]{1,0:T(8,128)(2,1)} %get-tuple-element.39.keys) | copy-start | bytes 1966084
  75.9 26.1 %copy-start.1 = (bf16[640,512]{1,0:T(8,128)(2,1)S(1)}, bf16[640,512]{1,0:T(8,128)(2,1)}, u32[]{:S(2)}) copy-start(bf16[640,512]{1,0:T(8,128)(2,1)} %get-tuple-element.40.values) | copy-start | bytes 1966084
  75.9 43.3 %all-to-all-start.2 = ((bf16[32,80,128]{2,1,0:T(8,128)(2,1)}), bf16[32,80,128]{2,1,0:T(8,128)(2,1)}, u32[]{:S(2)}, u32[]{:S(2)}) async-start(bf16[32,80,128]{2,1,0:T(8,128)(2,1)} %bitcast.13), calls=%async_computation.2 | async-start | bytes 1310720 | tf_op jit(solution)/shard_map/all_to_all | solution.py:562
  85.9 1.6 %collective-permute-start.4 = (bf16[264,128]{1,0:T(8,128)(2,1)}, bf16[264,128]{1,0:T(8,128)(2,1)S(1)}, u32[]{:S(2)}, u32[]{:S(2)}) collective-permute-start(bf16[264,128]{1,0:T(8,128)(2,1)} %copy-done.11), channel_id=1, source_target_pairs={{0,1},{1,0},{2,3},{3,2},{4,5},{5,4},{6,7},{7,6},{8,9},{9,8},{10,11... | collective-permute-start | bytes 202760 | tf_op jit(solution)/shard_map/ppermute | solution.py:548
  87.4 0.9 copy-start.12
  89.0 23.9 %collective-permute-start.5 = (bf16[264,128]{1,0:T(8,128)(2,1)S(1)}, bf16[264,128]{1,0:T(8,128)(2,1)S(1)}, u32[]{:S(2)}, u32[]{:S(2)}) collective-permute-start(bf16[264,128]{1,0:T(8,128)(2,1)S(1)} %shard_map.96), channel_id=1, source_target_pairs={{2,0},{3,1},{4,2},{5,3},{6,4},{7,5},{10,8},{11,9},{12,10},{13,11},... | collective-permute-start | bytes 202760 | tf_op jit(solution)/shard_map/ppermute | solution.py:554
  93.4 19.5 %collective-permute-start.6 = (bf16[264,128]{1,0:T(8,128)(2,1)S(1)}, bf16[264,128]{1,0:T(8,128)(2,1)S(1)}, u32[]{:S(2)}, u32[]{:S(2)}) collective-permute-start(bf16[264,128]{1,0:T(8,128)(2,1)S(1)} %shard_map.96), channel_id=1, source_target_pairs={{4,0},{5,1},{6,2},{7,3},{12,8},{13,9},{14,10},{15,11},{20,16},{21,... | collective-permute-start | bytes 202760 | tf_op jit(solution)/shard_map/ppermute | solution.py:554
  100.7 12.2 %collective-permute-start.7 = (bf16[264,128]{1,0:T(8,128)(2,1)S(1)}, bf16[264,128]{1,0:T(8,128)(2,1)S(1)}, u32[]{:S(2)}, u32[]{:S(2)}) collective-permute-start(bf16[264,128]{1,0:T(8,128)(2,1)S(1)} %shard_map.96), channel_id=1, source_target_pairs={{6,0},{7,1},{14,8},{15,9},{22,16},{23,17},{30,24},{31,25},{38,32},... | collective-permute-start | bytes 202760 | tf_op jit(solution)/shard_map/ppermute | solution.py:554
  102.0 1.1 copy-start.5
  103.1 6.6 %copy-start.3 = (bf16[640,512]{1,0:T(8,128)(2,1)S(1)}, bf16[640,512]{1,0:T(8,128)(2,1)}, u32[]{:S(2)}) copy-start(bf16[640,512]{1,0:T(8,128)(2,1)} %copy-done.2) | copy-start | bytes 1966084
  119.2 29.7 %all-to-all-start.3 = ((bf16[32,80,128]{2,1,0:T(8,128)(2,1)}), bf16[32,80,128]{2,1,0:T(8,128)(2,1)S(1)}, u32[]{:S(2)}, u32[]{:S(2)}) async-start(bf16[32,80,128]{2,1,0:T(8,128)(2,1)} %bitcast.12), calls=%async_computation.3 | async-start | bytes 1310720 | tf_op jit(solution)/shard_map/all_to_all | solution.py:562
  (3 other events, 1.9 us)
where the time goes:
time: 152 us; the launch traced here: 151 us
  starting transfers between devices  53.1 us (35%)
  Pallas kernels  50 us (33%)
  waiting for transfers between devices  39.2 us (26%)
  local copies, waits for them, and re-layouts  7.32 us (5%)
    pallas_call x13, Pallas kernels, call(): pl.pallas_call(body, out_shape=[pltpu.HBM(s, d) if i in out_hbm else jax....  50 us
    all_to_all x4, waiting for transfers between devices, regroup(): return lax.all_to_all(value, 'log', split_axis=0, concat_axis=0, tiled=True)  36.3 us
    all_to_all x4, starting transfers between devices, regroup(): return lax.all_to_all(value, 'log', split_axis=0, concat_axis=0, tiled=True)  36.1 us
    ppermute x6, starting transfers between devices, exchange(): lax.ppermute(value, axis, [(i, i + sign * k) for i in range(count) if 0 <...  16.8 us
    unnamed x30, local copies, waits for them, and re-layouts  7.32 us
  transfers between devices with their start and end apart: 12, of which 5 were waited for; matrix products, arithmetic and copies ran while one was open for 0% of the time, Pallas kernels for 24%

commit v1 on v0

--- a/solution.py
+++ b/solution.py
@@ -14,6 +14,7 @@
 TN = (((0,), (0,)), ((), ()))
 EXACT = lax.Precision.HIGHEST
 LIMIT = 16 << 20
+NX = 4
 
 
 def dot(a, b, dims=NN, precision=None):
@@ -31,6 +32,7 @@
 VMEM = pl.BlockSpec(memory_space=pltpu.VMEM)
 SMEM = pl.BlockSpec(memory_space=pltpu.SMEM)
 HBM = pl.BlockSpec(memory_space=pltpu.HBM)
+ANY = pl.BlockSpec(memory_space=pl.ANY)
 
 
 def call(body, outs, ins, scratch=(), spaces=None, out_hbm=()):
@@ -101,6 +103,11 @@
     return copy
 
 
+def rows_copy(source, target, sems, j):
+    rows = pl.ds(pl.multiple_of(j * CH, CH), CH)
+    return pltpu.make_async_copy(source.at[rows, :], target.at[rows, :], sems.at[j])
+
+
 def expanded(fade, rows, p):
     here = fade[rows, :]
     shape = (here.shape[0], 128)
@@ -112,8 +119,8 @@
 
 
 def pack_events(
-    owner_in, events_in, elapsed_in, resets_in, message, place,
-    scratch, owner, events, elapsed, resets, sems,
+    owner_in, events_in, elapsed_in, resets_in, message, spots,
+    scratch, place, owner, events, elapsed, resets, sems,
 ):
     copies = [
         pltpu.make_async_copy(source, target, sems.at[i])
@@ -138,6 +145,8 @@
     earlier = ones_where(iota((rows, rows), 0) < iota((rows, rows), 1))
     before = dot(ones_where(hit), earlier)
     rank = jnp.sum(jnp.where(hit, before, 0.0), axis=0, keepdims=True).astype(jnp.int32)
+    spots[0:1, :] = own
+    spots[1:2, :] = rank
     place[...] = ones_where(iota((slots, rows), 0) == own * cap + rank)
     for copy in copies[1:]:
         copy.wait()
@@ -161,16 +170,59 @@
     message[:, per : per + 8, :] = extra.astype(bf16)
 
 
-def pack_grads(info, place, grads, message, back, scratch):
+def pack_grads(info, spots, grads, *rest):
+    pieces, (back, back_far, scratch, narrow, turned, turned_far, sems) = rest[:NX], rest[NX:]
     rows, width = grads.shape
-    write_message(
-        message,
-        scratch,
-        lambda j: dot(place[...], grads[:, 128 * j : 128 * (j + 1)]),
-        width,
-    )
+    slots = turned.shape[1]
+    own, rank = spots[0:1, :], spots[1:2, :]
+    count = pieces[0].shape[0]
+    cap = slots // (count * NX)
+    z, x = own >> (NX.bit_length() - 1), own & (NX - 1)
+    place = ones_where(iota((slots, rows), 0) == (((x - info[2]) & (NX - 1)) * count + z) * cap + rank)
+    write_rows(
+        scratch, lambda j: dot(place, grads[:, 128 * j : 128 * (j + 1)]), width // 128
+    )
+    narrow[...] = scratch[...].reshape(narrow.shape).astype(bf16)
+    copies = [
+        fetched(narrow.at[k], pieces[k], sems.at[k]) for k in range(NX)
+    ]
     same = ones_where(iota((rows, rows), 0) == iota((rows, rows), 1))
-    back[...] = dot(same, place[...], NT).astype(bf16)
+    place = ones_where(iota((slots, rows), 0) == own * cap + rank)
+    turned[...] = dot(same, place, NT).astype(bf16)
+    copies.append(fetched(turned, back, sems.at[NX]))
+    place = ones_where(iota((slots, rows), 0) == (((info[2] - x) & (NX - 1)) * count + z) * cap + rank)
+    turned_far[...] = dot(same, place, NT).astype(bf16)
+    copies.append(fetched(turned_far, back_far, sems.at[NX + 1]))
+    for copy in copies:
+        copy.wait()
+
+
+def merge_pieces(*rest):
+    pieces, (out, sems) = rest[:NX], rest[NX:]
+    copies = [fetched(pieces[k], out.at[:, k], sems.at[k]) for k in range(NX)]
+    for copy in copies:
+        copy.wait()
+
+
+def split_pieces(info, merged, *rest):
+    pieces, sems = rest[:NX], rest[NX]
+    copies = [
+        fetched(merged.at[:, (info[2] + k) & (NX - 1)], pieces[k], sems.at[k]) for k in range(NX)
+    ]
+    for copy in copies:
+        copy.wait()
+
+
+def unpack_pieces(back, *rest):
+    pieces, (out, scratch) = rest[:NX], rest[NX:]
+    width = out.shape[1]
+    parts = width // 128
+    size = scratch.shape[0] // NX
+    for k in range(NX):
+        scratch[size * k : size * (k + 1), :] = pieces[k][...].astype(f32).reshape(size, 128)
+    for j in range(parts):
+        part = scratch[pl.ds(j, scratch.shape[0] // parts, stride=parts), :].astype(bf16)
+        out[:, 128 * j : 128 * (j + 1)] = dot(back[...], part).astype(bf16)
 
 
 def unpack_rows(back, message, out, scratch):
@@ -372,7 +424,9 @@
     lax.fori_loop(0, x.shape[0] // CH, project, 0)
 
 
-def attend(q8, keys, values, fade, fade_t, marks, attended, states, memory):
+def attend(
+    q8, keys, values, fade, fade_t, marks, attended_out, states, memory, attended, sems
+):
     slots, width = q8.shape
     pairs = width // 128
     low, high = halves()
@@ -396,20 +450,28 @@
             attended[rows, cols] = within + dot(lifted, now.astype(bf16))
             kf = (kp.astype(f32) * jnp.exp(end - g)).astype(bf16)
             memory[p] = jnp.exp(end - start) * now + jnp.where(mask, dot(kf, vp, TN), 0.0)
+        rows_copy(attended, attended_out, sems, j).start()
         return carry
 
     lax.fori_loop(0, slots // CH, block, 0)
-
-
-def turn(info, q8, fade, fade_t, attended, x_in, weights, message_in, partner, *rest):
-    received = rest[:-15]
+    for j in range(slots // CH):
+        rows_copy(attended, attended_out, sems, j).wait()
+
+
+def turn(info, q8, fade, fade_t, attended_in, x_in, weights, message_in, partner, *rest):
+    received = rest[:-17]
     (
-        encoded, grads, grad_full, incoming, send,
-        scratch, message, mine, x, wide, narrow, states, memory, sems, out_sems,
-    ) = rest[-15:]
-    arrival = fetched(message_in, message, sems.at[0])
-    fetch = fetched(weights.at[info[0], 3], mine, sems.at[1])
-    rows_in = fetched(x_in, x, sems.at[2])
+        encoded, grads_out, grad_full, incoming, send,
+        scratch, message, mine, x, attended, grads,
+        wide, narrow, states, memory, sems, out_sems,
+    ) = rest[-17:]
+    arrivals = [
+        fetched(message_in.at[:, (info[2] - k) & (NX - 1)], message.at[:, k], sems.at[2 + k])
+        for k in range(NX)
+    ]
+    fetch = fetched(weights.at[info[0], 3], mine, sems.at[0])
+    rows_in = fetched(x_in, x, sems.at[1])
+    attended_here = fetched(attended_in, attended, sems.at[2 + NX])
     slots, width = x.shape
     pairs = width // 128
     blocks = slots // CH
@@ -418,11 +480,16 @@
         incoming[p] = state
         states[p] = unfolded(state, mask).astype(bf16)
     memory[...] = jnp.zeros(memory.shape, f32)
-    arrival.wait()
-    for j, part in enumerate(read_message(message, scratch, width)):
+    for arrival in arrivals:
+        arrival.wait()
+    scratch[...] = message[...].astype(f32).reshape(scratch.shape)
+    for j in range(pairs):
+        part = scratch[pl.ds(j, slots, stride=pairs), :]
         grads[:, 128 * j : 128 * (j + 1)] = part.astype(bf16)
     fetch.wait()
     rows_in.wait()
+    attended_here.wait()
+    store = fetched(grads, grads_out, sems.at[3 + NX])
     sender = Sender(encoded, wide, narrow, out_sems, pairs)
 
     def block(j, carry):
@@ -452,6 +519,7 @@
     lax.fori_loop(0, blocks, block, 0)
     write_state(send, memory, fade_t[blocks - 1][:, CH - 1 : CH], pairs)
     sender.finish(blocks)
+    store.wait()
 
 
 def backward_local(
@@ -500,8 +568,10 @@
     lax.fori_loop(0, blocks, block, 0)
 
 
-def project_back(info, grads, grad_q, weights, partial, mine, sem):
-    fetched(weights.at[info[0], 0], mine, sem).wait()
+def project_back(info, grads_in, grad_q, weights, partial, mine, grads, sems):
+    arrival = fetched(grads_in, grads, sems.at[0])
+    fetched(weights.at[info[0], 0], mine, sems.at[1]).wait()
+    arrival.wait()
 
     def project(j, carry):
         rows = pl.ds(pl.multiple_of(j * CH, CH), CH)
@@ -573,15 +643,32 @@
     flat = pltpu.VMEM((slots * pairs, 128), f32)
     state_vmem = pltpu.VMEM((pairs, 128, 128), f32)
     state_msg = ((64 * pairs + 8, 128), bf16)
-    wide_msg = ((owners, per, 128), bf16)
     wide16, wide32 = ((slots, width), bf16), ((slots, width), f32)
 
     tower = lax.axis_index("log") // (owners // decay_rates.shape[0])
-    info = jnp.stack([tower, lax.axis_index("ctx") % 2]).astype(jnp.int32)
-
-    message, place = call(
+    place_x = lax.axis_index("log") % NX
+    info = jnp.stack([tower, lax.axis_index("ctx") % 2, place_x]).astype(jnp.int32)
+    depth = owners // NX
+    piece = ((depth, per, 128), bf16)
+    sem = pltpu.SemaphoreType.DMA
+    along_x = [
+        [(i, i // NX * NX + (i + k) % NX) for i in range(owners)] for k in range(NX)
+    ]
+    along_z = [[z * NX + i for z in range(depth)] for i in range(NX)]
+
+    def over_x(pieces):
+        return [pieces[0]] + [lax.ppermute(pieces[k], "log", along_x[k]) for k in range(1, NX)]
+
+    def over_z(value):
+        moved = lax.all_to_all(
+            value.reshape(depth, NX * per, 128), "log", split_axis=0, concat_axis=0,
+            axis_index_groups=along_z, tiled=True,
+        )
+        return moved.reshape(depth, NX, per, 128)
+
+    message, spots = call(
         pack_events,
-        [((owners, per + 8, 128), bf16), ((slots, rows), bf16)],
+        [((owners, per + 8, 128), bf16), ((2, rows), jnp.int32)],
         [
             owner_ids.reshape(1, rows),
             events.reshape(rows, width),
@@ -590,6 +677,7 @@
         ],
         [
             flat,
+            pltpu.VMEM((slots, rows), bf16),
             pltpu.VMEM((1, rows), jnp.int32),
             pltpu.VMEM((rows, width), bf16),
             pltpu.VMEM((1, rows), f32),
@@ -599,22 +687,36 @@
         {0: HBM, 1: HBM, 2: HBM, 3: HBM},
     )
     events_in = regroup(message)
-    message, back = call(
+    *pieces, back, back_far = call(
         pack_grads,
-        [wide_msg, ((rows, slots), bf16)],
-        [info, place, cotangent.reshape(rows, width)],
-        [flat],
+        [piece] * NX + [((rows, slots), bf16)] * 2,
+        [info, spots, cotangent.reshape(rows, width)],
+        [
+            flat,
+            pltpu.VMEM((NX, depth, per, 128), bf16),
+            pltpu.VMEM((rows, slots), bf16),
+            pltpu.VMEM((rows, slots), bf16),
+            sem((NX + 2,)),
+        ],
         {0: SMEM},
-    )
-    grads_in = regroup(message)
+        range(NX + 2),
+    )
+    (merged,) = call(
+        merge_pieces,
+        [((depth, NX, per, 128), bf16)],
+        over_x(pieces),
+        [sem((NX,))],
+        {k: HBM for k in range(NX)},
+        (0,),
+    )
+    grads_in = over_z(merged)
     one = pltpu.VMEM((width, width), bf16)
     two = pltpu.VMEM((2, width, width), bf16)
-    sem = pltpu.SemaphoreType.DMA
     half_states = ((pairs, 64, 128), f32)
     flat_msg = ((slots * pairs, 128), bf16)
     block_wide = pltpu.VMEM((CH * pairs, 128), f32)
     flat_narrow = pltpu.VMEM(*flat_msg)
-    rows16 = pltpu.VMEM(*wide16)
+    rows16, rows32 = pltpu.VMEM(*wide16), pltpu.VMEM(*wide32)
     narrow_states = pltpu.VMEM((pairs, 128, 128), bf16)
     x, keys, values, keys_far, values_far, fade, fade_t, marks, send = call(
         forward_state,
@@ -641,21 +743,23 @@
         attend,
         [wide32, ((blocks, pairs, 64, 128), bf16)],
         [q8, keys, values, fade, fade_t, marks],
-        [state_vmem],
+        [state_vmem, rows32, sem((blocks,))],
+        None,
+        (0,),
     )
     message, grads, grad_full, incoming, send = call(
         turn,
         [flat_msg, wide16, wide16, half_states, state_msg],
         [info, q8, fade, fade_t, attended, x, weights, grads_in, partner, *received],
         [
-            flat, pltpu.VMEM(*wide_msg), one, rows16, block_wide, flat_narrow, narrow_states,
-            state_vmem, sem((3,)), sem((blocks,)),
+            flat, pltpu.VMEM((depth, NX, per, 128), bf16), one, rows16, rows32, rows16,
+            block_wide, flat_narrow, narrow_states, state_vmem, sem((4 + NX,)), sem((blocks,)),
         ],
-        {0: SMEM, 5: HBM, 6: HBM, 7: HBM},
-        (0,),
+        {0: SMEM, 4: HBM, 5: HBM, 6: HBM, 7: ANY},
+        (0, 1),
     )
     partner = swapped(send, "ctx")
-    encoded_in = regroup(message.reshape(owners, per, 128))
+    encoded_in = over_z(message)
     grad_q, grad_keys, grad_values = call(
         backward_local,
         [wide16, wide32, wide32],
@@ -665,7 +769,11 @@
     (joined,) = call(join_back, [state_msg], [info, send, partner], (), {0: SMEM})
     received = exchange(joined, "ctx", -1)
     (partial,) = call(
-        project_back, [wide32], [info, grads, grad_q, weights], [one, sem], {0: SMEM, 3: HBM}
+        project_back,
+        [wide32],
+        [info, grads, grad_q, weights],
+        [one, rows16, sem((2,))],
+        {0: SMEM, 1: HBM, 3: HBM},
     )
     (message,) = call(
         backward_finish,
@@ -682,7 +790,17 @@
         (0,),
     )
     grad_in = regroup(message.reshape(owners, per, 128))
-    (encoded,) = call(unpack_rows, [((rows, width), bf16)], [back, encoded_in], [flat])
+    pieces = call(
+        split_pieces,
+        [piece] * NX,
+        [info, encoded_in],
+        [sem((NX,))],
+        {0: SMEM, 1: HBM},
+        range(NX),
+    )
+    (encoded,) = call(
+        unpack_pieces, [((rows, width), bf16)], [back_far, *over_x(pieces)], [flat]
+    )
     (grad,) = call(unpack_rows, [((rows, width), bf16)], [back, grad_in], [flat])
     return encoded.reshape(events.shape), grad.reshape(events.shape)
 

time: 152 us -> 176 us (1.16)
  Pallas kernels: 50 us -> 92.4 us
  waiting for transfers between devices: 39.2 us -> 19.1 us
  starting transfers between devices: 53.1 us -> 60.7 us
  local copies, waits for them, and re-layouts: 7.32 us -> 1.67 us
    pallas_call x13 -> x15, Pallas kernels: 50 us -> 92.4 us  [call(): pl.pallas_call(body, out_shape=[pltpu.HBM(s, d) if i in out_hbm else jax....]
    all_to_all x4 -> x2, waiting for transfers between devices: 36.3 us -> 0.01 us  [regroup(): return lax.all_to_all(value, 'log', split_axis=0, concat_axis=0, tiled=True)]
    ppermute x0 -> x6, waiting for transfers between devices: none -> 16.6 us  [over_x(): lax.ppermute(pieces[k], 'log', along_x[k])]
    all_to_all x4 -> x2, starting transfers between devices: 36.1 us -> 20.2 us  [regroup(): return lax.all_to_all(value, 'log', split_axis=0, concat_axis=0, tiled=True)]
    all_to_all x0 -> x2, starting transfers between devices: none -> 13 us  [over_z(): lax.all_to_all(value.reshape(depth, NX * per, 128), 'log', split_axis=0,...]
    ppermute x0 -> x6, starting transfers between devices: none -> 12 us  [over_x(): lax.ppermute(pieces[k], 'log', along_x[k])]
    unnamed x30 -> x22, local copies, waits for them, and re-layouts: 7.32 us -> 1.67 us
  transfers between devices with their start and end apart: 12 -> 18, of which waited for: 5 -> 6; matrix products, arithmetic and copies ran while one was open for 0% -> 0% of each run, Pallas kernels for 24% -> 45%
where the time goes in v1:
time: 176 us; the launch traced here: 175 us
  Pallas kernels  92.4 us (52%)
  starting transfers between devices  60.7 us (34%)
  waiting for transfers between devices  19.1 us (11%)
    pallas_call x15, Pallas kernels, call(): pl.pallas_call(body, out_shape=[pltpu.HBM(s, d) if i in out_hbm else jax....  92.4 us
    all_to_all x2, starting transfers between devices, regroup(): return lax.all_to_all(value, 'log', split_axis=0, concat_axis=0, tiled=True)  20.2 us
    ppermute x6, waiting for transfers between devices, over_x(): lax.ppermute(pieces[k], 'log', along_x[k])  16.6 us
    ppermute x6, starting transfers between devices, exchange(): lax.ppermute(value, axis, [(i, i + sign * k) for i in range(count) if 0 <...  15.3 us
    all_to_all x2, starting transfers between devices, over_z(): lax.all_to_all(value.reshape(depth, NX * per, 128), 'log', split_axis=0,...  13 us
    ppermute x6, starting transfers between devices, over_x(): lax.ppermute(pieces[k], 'log', along_x[k])  12 us
  transfers between devices with their start and end apart: 18, of which 6 were waited for; matrix products, arithmetic and copies ran while one was open for 0% of the time, Pallas kernels for 45%

profile of v1, /device:TPU:24, one launch (start us, length us, event | category | flops | bytes accessed | tf_op | source)
XLA Modules:
  0.0 175.0 jit_solution(3524448679523229727)
XLA Ops:
  0.6 3.3 %shard_map.86 = (bf16[32,88,128]{2,1,0:T(8,128)(2,1)}, s32[2,512]{1,0:T(2,128)S(1)}) custom-call(s32[1,512]{1,0:T(1,128)} %bitcast.23, bf16[512,512]{1,0:T(8,128)(2,1)} %bitcast.22, f32[1,512]{1,0:T(1,128)} %bitcast.24, f32[1,512]{1,0:T(1,128)} %bitcast.25), custom_call_target="tpu_custom_call" | custom-call | tf_op jit(solution)/shard_map/pallas_call | solution.py:43
  3.9 11.3 %all-to-all-start = ((bf16[32,88,128]{2,1,0:T(8,128)(2,1)}), bf16[32,88,128]{2,1,0:T(8,128)(2,1)S(1)}, u32[]{:S(2)}, u32[]{:S(2)}) async-start(bf16[32,88,128]{2,1,0:T(8,128)(2,1)} %get-tuple-element.35), calls=%async_computation | async-start | bytes 1441792 | tf_op jit(solution)/shard_map/all_to_all | solution.py:632
  15.3 3.2 %shard_map.87 = (bf16[8,80,128]{2,1,0:T(8,128)(2,1)}, bf16[8,80,128]{2,1,0:T(8,128)(2,1)}, bf16[8,80,128]{2,1,0:T(8,128)(2,1)}, bf16[8,80,128]{2,1,0:T(8,128)(2,...) custom-call(s32[3]{0:T(128)S(1)} %pad_add_fusion.info, s32[2,512]{1,0:T(2,128)S(1)} %get-tuple-element.33.spots, ...), custom_call_target="tpu_custom_call" | custom-call | tf_op jit(solution)/shard_map/pallas_call | solution.py:43
  18.5 1.9 %collective-permute-start = (bf16[8,80,128]{2,1,0:T(8,128)(2,1)}, bf16[8,80,128]{2,1,0:T(8,128)(2,1)S(1)}, u32[]{:S(2)}, u32[]{:S(2)}) collective-permute-start(bf16[8,80,128]{2,1,0:T(8,128)(2,1)} %get-tuple-element.44), channel_id=1, source_target_pairs={{0,8},{8,16},{16,24},{24,0},{32,40},{40,48},{48,56},{56,32},{64,72... | collective-permute-start | bytes 491528 | tf_op jit(solution)/shard_map/ppermute | solution.py:660
  20.4 2.7 %collective-permute-start.1 = (bf16[8,80,128]{2,1,0:T(8,128)(2,1)}, bf16[8,80,128]{2,1,0:T(8,128)(2,1)S(1)}, u32[]{:S(2)}, u32[]{:S(2)}) collective-permute-start(bf16[8,80,128]{2,1,0:T(8,128)(2,1)} %get-tuple-element.45), channel_id=1, source_target_pairs={{0,16},{8,24},{16,0},{24,8},{32,48},{40,56},{48,32},{56,40},{64,80... | collective-permute-start | bytes 491528 | tf_op jit(solution)/shard_map/ppermute | solution.py:660
  24.5 6.3 %collective-permute-done.rest_1_ = bf16[8,80,128]{2,1,0:T(8,128)(2,1)S(1)} collective-permute-done((bf16[8,80,128]{2,1,0:T(8,128)(2,1)}, bf16[8,80,128]{2,1,0:T(8,128)(2,1)S(1)}, u32[]{:S(2)}, u32[]{:S(2)}) %collective-permute-start) | collective-permute-done | bytes 163872 | tf_op jit(solution)/shard_map/ppermute | solution.py:660
  30.8 5.0 %collective-permute-done.1.rest_2_ = bf16[8,80,128]{2,1,0:T(8,128)(2,1)S(1)} collective-permute-done((bf16[8,80,128]{2,1,0:T(8,128)(2,1)}, bf16[8,80,128]{2,1,0:T(8,128)(2,1)S(1)}, u32[]{:S(2)}, u32[]{:S(2)}) %collective-permute-start.1) | collective-permute-done | bytes 163872 | tf_op jit(solution)/shard_map/ppermute | solution.py:660
  36.5 21.0 %shard_map.91 = bf16[8,4,80,128]{3,2,1,0:T(8,128)(2,1)} custom-call(bf16[8,80,128]{2,1,0:T(8,128)(2,1)} %get-tuple-element.43.rest_0_, bf16[8,80,128]{2,1,0:T(8,128)(2,1)} %copy-done.8, bf16[8,80,128]{2,1,0:T(8,128)(2,1)} %copy-done.9, bf16[8,80,128]{2,1,0:T(8,128)(2,1)} %copy-done.10), custom_call_target="tpu_custom_call" | custom-call | tf_op jit(solution)/shard_map/pallas_call | solution.py:43
  57.5 5.6 %all-to-all-start.1 = ((bf16[8,320,128]{2,1,0:T(8,128)(2,1)}), bf16[8,320,128]{2,1,0:T(8,128)(2,1)S(1)}, u32[]{:S(2)}, u32[]{:S(2)}) async-start(bf16[8,320,128]{2,1,0:T(8,128)(2,1)} %bitcast.18), calls=%async_computation.1 | async-start | bytes 1310720 | tf_op jit(solution)/shard_map/all_to_all | solution.py:663
  63.2 6.4 %shard_map.88 = (bf16[640,512]{1,0:T(8,128)(2,1)}, bf16[640,512]{1,0:T(8,128)(2,1)S(1)}, bf16[640,512]{1,0:T(8,128)(2,1)S(1)}, bf16[640,512]{1,0:T(8,128)(2,1)},...) custom-call(s32[3]{0:T(128)S(1)} %pad_add_fusion.info, ...), custom_call_target="tpu_custom_call" | custom-call | tf_op jit(solution)/shard_map/pallas_call | solution.py:43
  75.6 3.0 %shard_map.89.q8 = bf16[640,512]{1,0:T(8,128)(2,1)S(1)} custom-call(s32[3]{0:T(128)S(1)} %pad_add_fusion.info, bf16[640,512]{1,0:T(8,128)(2,1)} %get-tuple-element.36.x_in, bf16[4,4,512,512]{3,2,1,0:T(8,128)(2,1)} %weights.9), custom_call_target="tpu_custom_call" | custom-call | tf_op jit(solution)/shard_map/pallas_call | solution.py:43
  78.6 4.8 %shard_map.90 = (f32[640,512]{1,0:T(8,128)}, bf16[5,4,64,128]{3,2,1,0:T(8,128)(2,1)S(1)}) custom-call(bf16[640,512]{1,0:T(8,128)(2,1)S(1)} %shard_map.89.q8, bf16[640,512]{1,0:T(8,128)(2,1)S(1)} %get-tuple-element.39.keys, bf16[640,512]{1,0:T(8,128)(2,1)S(1)} %get-tuple-element.40.values, f32[640,128]{1,0:T(8,128)S(1)} %get-tuple-element.37.fade, ...), custom_call_target="tpu_custom_call" | custom-call | tf_op jit(solution)/shard_map/pallas_call | solution.py:43
  83.4 8.3 %shard_map.93 = (bf16[2560,128]{1,0:T(8,128)(2,1)}, bf16[640,512]{1,0:T(8,128)(2,1)}, bf16[640,512]{1,0:T(8,128)(2,1)S(1)}, f32[4,64,128]{2,1,0:T(8,128)S(1)}, bf16[264,128]{1,0:T(8,128)(2,1)S(1)}) custom-call(s32[3]{0:T(128)S(1)} %pad_add_fusion.info, bf16[640,512]{1,0:T(8,128)(2,1)S(1)} %shard_map.89.q8, f32[640,128]{1,0:T(8,128)S(1)} %get-tuple-element.37.fade, ...), custom_call_target="tpu_custom_call" | custom-call | tf_op jit(solution)/shard_map/pallas_call | solution.py:43
  91.8 7.3 %all-to-all-start.2 = ((bf16[8,320,128]{2,1,0:T(8,128)(2,1)}), bf16[8,320,128]{2,1,0:T(8,128)(2,1)}, u32[]{:S(2)}, u32[]{:S(2)}) async-start(bf16[8,320,128]{2,1,0:T(8,128)(2,1)} %bitcast.19), calls=%async_computation.2 | async-start | bytes 1310720 | tf_op jit(solution)/shard_map/all_to_all | solution.py:663
  101.1 7.2 %collective-permute-start.13 = (bf16[264,128]{1,0:T(8,128)(2,1)S(1)}, bf16[264,128]{1,0:T(8,128)(2,1)S(1)}, u32[]{:S(2)}, u32[]{:S(2)}) collective-permute-start(bf16[264,128]{1,0:T(8,128)(2,1)S(1)} %shard_map.98), channel_id=1, source_target_pairs={{6,0},{7,1},{14,8},{15,9},{22,16},{23,17},{30,24},{31,25},{38,32},... | collective-permute-start | bytes 202760 | tf_op jit(solution)/shard_map/ppermute | solution.py:624
  109.6 2.9 %collective-permute-start.11 = (bf16[264,128]{1,0:T(8,128)(2,1)S(1)}, bf16[264,128]{1,0:T(8,128)(2,1)S(1)}, u32[]{:S(2)}, u32[]{:S(2)}) collective-permute-start(bf16[264,128]{1,0:T(8,128)(2,1)S(1)} %shard_map.98), channel_id=1, source_target_pairs={{2,0},{3,1},{4,2},{5,3},{6,4},{7,5},{10,8},{11,9},{12,10},{13,11},... | collective-permute-start | bytes 202760 | tf_op jit(solution)/shard_map/ppermute | solution.py:624
  112.6 6.6 %shard_map.96 = (bf16[640,512]{1,0:T(8,128)(2,1)S(1)}, f32[640,512]{1,0:T(8,128)S(1)}, f32[640,512]{1,0:T(8,128)S(1)}) custom-call(bf16[640,512]{1,0:T(8,128)(2,1)S(1)} %shard_map.89.q8, bf16[640,512]{1,0:T(8,128)(2,1)S(1)} %copy-done, bf16[640,512]{1,0:T(8,128)(2,1)S(1)} %copy-done.1, f32[640,128]{1,0:T(8,128)S(1)} %get-tuple-element.37.fade, ...), custom_call_target="tpu_custom_call" | custom-call | tf_op jit(solution)/shard_map/pallas_call | solution.py:43
  119.2 3.3 %shard_map.97.partial = f32[640,512]{1,0:T(8,128)S(1)} custom-call(s32[3]{0:T(128)S(1)} %pad_add_fusion.info, bf16[640,512]{1,0:T(8,128)(2,1)} %get-tuple-element.54.grads_in, bf16[640,512]{1,0:T(8,128)(2,1)S(1)} %get-tuple-element.60.grad_q, bf16[4,4,512,512]{3,2,1,0:T(8,128)(2,1)} %weights.9), custom_call_target="tpu_custom_call" | custom-call | tf_op jit(solution)/shard_map/pallas_call | solution.py:43
  122.6 6.2 %shard_map.99 = bf16[2560,128]{1,0:T(8,128)(2,1)} custom-call(s32[3]{0:T(128)S(1)} %pad_add_fusion.info, f32[640,512]{1,0:T(8,128)S(1)} %shard_map.97.partial, f32[640,512]{1,0:T(8,128)S(1)} %get-tuple-element.61.grad_keys, f32[640,512]{1,0:T(8,128)S(1)} %get-tuple-element.62.grad_values, bf16[640,512]{1,0:T(8,128)(2,1)S(1)} %copy-done, ...), custom_call_target="tpu_custom_call" | custom-call | tf_op jit(solution)/shard_map/pallas_call | solution.py:43
  128.9 8.9 %all-to-all-start.3 = ((bf16[32,80,128]{2,1,0:T(8,128)(2,1)}), bf16[32,80,128]{2,1,0:T(8,128)(2,1)S(1)}, u32[]{:S(2)}, u32[]{:S(2)}) async-start(bf16[32,80,128]{2,1,0:T(8,128)(2,1)} %bitcast.17), calls=%async_computation.3 | async-start | bytes 1310720 | tf_op jit(solution)/shard_map/all_to_all | solution.py:632
  137.8 21.5 %shard_map.94 = (bf16[8,80,128]{2,1,0:T(8,128)(2,1)}, bf16[8,80,128]{2,1,0:T(8,128)(2,1)}, bf16[8,80,128]{2,1,0:T(8,128)(2,1)}, bf16[8,80,128]{2,1,0:T(8,128)(2,1)}) custom-call(s32[3]{0:T(128)S(1)} %pad_add_fusion.info, bf16[8,4,80,128]{3,2,1,0:T(8,128)(2,1)} %bitcast.11.merged), custom_call_target="tpu_custom_call" | custom-call | tf_op jit(solution)/shard_map/pallas_call | solution.py:43
  161.2 2.7 %collective-permute-start.8 = (bf16[8,80,128]{2,1,0:T(8,128)(2,1)}, bf16[8,80,128]{2,1,0:T(8,128)(2,1)S(1)}, u32[]{:S(2)}, u32[]{:S(2)}) collective-permute-start(bf16[8,80,128]{2,1,0:T(8,128)(2,1)} %get-tuple-element.51), channel_id=1, source_target_pairs={{0,16},{8,24},{16,0},{24,8},{32,48},{40,56},{48,32},{56,40},{64,80... | collective-permute-start | bytes 491528 | tf_op jit(solution)/shard_map/ppermute | solution.py:660
  165.3 1.9 %collective-permute-done.7.rest_1_ = bf16[8,80,128]{2,1,0:T(8,128)(2,1)S(1)} collective-permute-done((bf16[8,80,128]{2,1,0:T(8,128)(2,1)}, bf16[8,80,128]{2,1,0:T(8,128)(2,1)S(1)}, u32[]{:S(2)}, u32[]{:S(2)}) %collective-permute-start.7) | collective-permute-done | bytes 163872 | tf_op jit(solution)/shard_map/ppermute | solution.py:660
  167.2 3.5 %collective-permute-done.8.rest_2_ = bf16[8,80,128]{2,1,0:T(8,128)(2,1)S(1)} collective-permute-done((bf16[8,80,128]{2,1,0:T(8,128)(2,1)}, bf16[8,80,128]{2,1,0:T(8,128)(2,1)S(1)}, u32[]{:S(2)}, u32[]{:S(2)}) %collective-permute-start.8) | collective-permute-done | bytes 163872 | tf_op jit(solution)/shard_map/ppermute | solution.py:660
  (50 shorter events, 19.1 us)
Async XLA Ops:
  0.6 14.7 %copy-start.4 = (bf16[1,1,512,512]{3,2,1,0:T(8,128)(2,1)S(1)}, bf16[1,1,512,512]{3,2,1,0:T(8,128)(2,1)}, u32[]{:S(2)}) copy-start(bf16[1,1,512,512]{3,2,1,0:T(8,128)(2,1)} %param.13) | copy-start | bytes 1572868
  3.9 53.6 %all-to-all-start = ((bf16[32,88,128]{2,1,0:T(8,128)(2,1)}), bf16[32,88,128]{2,1,0:T(8,128)(2,1)S(1)}, u32[]{:S(2)}, u32[]{:S(2)}) async-start(bf16[32,88,128]{2,1,0:T(8,128)(2,1)} %get-tuple-element.35), calls=%async_computation | async-start | bytes 1441792 | tf_op jit(solution)/shard_map/all_to_all | solution.py:632
  18.5 12.3 %collective-permute-start = (bf16[8,80,128]{2,1,0:T(8,128)(2,1)}, bf16[8,80,128]{2,1,0:T(8,128)(2,1)S(1)}, u32[]{:S(2)}, u32[]{:S(2)}) collective-permute-start(bf16[8,80,128]{2,1,0:T(8,128)(2,1)} %get-tuple-element.44), channel_id=1, source_target_pairs={{0,8},{8,16},{16,24},{24,0},{32,40},{40,48},{48,56},{56,32},{64,72... | collective-permute-start | bytes 491528 | tf_op jit(solution)/shard_map/ppermute | solution.py:660
  20.4 15.4 %collective-permute-start.1 = (bf16[8,80,128]{2,1,0:T(8,128)(2,1)}, bf16[8,80,128]{2,1,0:T(8,128)(2,1)S(1)}, u32[]{:S(2)}, u32[]{:S(2)}) collective-permute-start(bf16[8,80,128]{2,1,0:T(8,128)(2,1)} %get-tuple-element.45), channel_id=1, source_target_pairs={{0,16},{8,24},{16,0},{24,8},{32,48},{40,56},{48,32},{56,40},{64,80... | collective-permute-start | bytes 491528 | tf_op jit(solution)/shard_map/ppermute | solution.py:660
  23.1 12.7 %collective-permute-start.2 = (bf16[8,80,128]{2,1,0:T(8,128)(2,1)}, bf16[8,80,128]{2,1,0:T(8,128)(2,1)S(1)}, u32[]{:S(2)}, u32[]{:S(2)}) collective-permute-start(bf16[8,80,128]{2,1,0:T(8,128)(2,1)} %get-tuple-element.46), channel_id=1, source_target_pairs={{0,24},{8,0},{16,8},{24,16},{32,56},{40,32},{48,40},{56,48},{64,88... | collective-permute-start | bytes 491528 | tf_op jit(solution)/shard_map/ppermute | solution.py:660
  36.5 26.7 %copy-start.6 = (f32[4,8]{1,0:T(4,128)S(1)}, f32[4,8]{1,0:T(4,128)}, u32[]{:S(2)}) copy-start(f32[4,8]{1,0:T(4,128)} %rates.1) | copy-start | bytes 388
  57.5 25.9 %all-to-all-start.1 = ((bf16[8,320,128]{2,1,0:T(8,128)(2,1)}), bf16[8,320,128]{2,1,0:T(8,128)(2,1)S(1)}, u32[]{:S(2)}, u32[]{:S(2)}) async-start(bf16[8,320,128]{2,1,0:T(8,128)(2,1)} %bitcast.18), calls=%async_computation.1 | async-start | bytes 1310720 | tf_op jit(solution)/shard_map/all_to_all | solution.py:663
  69.7 1.3 collective-permute-start.3
  71.7 11.7 %collective-permute-start.6 = (bf16[264,128]{1,0:T(8,128)(2,1)S(1)}, bf16[264,128]{1,0:T(8,128)(2,1)S(1)}, u32[]{:S(2)}, u32[]{:S(2)}) collective-permute-start(bf16[264,128]{1,0:T(8,128)(2,1)S(1)} %shard_map.92), channel_id=1, source_target_pairs={{0,6},{1,7},{8,14},{9,15},{16,22},{17,23},{24,30},{25,31},{32,38},... | collective-permute-start | bytes 202760 | tf_op jit(solution)/shard_map/ppermute | solution.py:624
  73.0 10.4 %collective-permute-start.5 = (bf16[264,128]{1,0:T(8,128)(2,1)S(1)}, bf16[264,128]{1,0:T(8,128)(2,1)S(1)}, u32[]{:S(2)}, u32[]{:S(2)}) collective-permute-start(bf16[264,128]{1,0:T(8,128)(2,1)S(1)} %shard_map.92), channel_id=1, source_target_pairs={{0,4},{1,5},{2,6},{3,7},{8,12},{9,13},{10,14},{11,15},{16,20},{17,... | collective-permute-start | bytes 202760 | tf_op jit(solution)/shard_map/ppermute | solution.py:624
  74.3 9.1 %collective-permute-start.4 = (bf16[264,128]{1,0:T(8,128)(2,1)S(1)}, bf16[264,128]{1,0:T(8,128)(2,1)S(1)}, u32[]{:S(2)}, u32[]{:S(2)}) collective-permute-start(bf16[264,128]{1,0:T(8,128)(2,1)S(1)} %shard_map.92), channel_id=1, source_target_pairs={{0,2},{1,3},{2,4},{3,5},{4,6},{5,7},{8,10},{9,11},{10,12},{11,13},... | collective-permute-start | bytes 202760 | tf_op jit(solution)/shard_map/ppermute | solution.py:624
  91.7 20.8 %copy-start = (bf16[640,512]{1,0:T(8,128)(2,1)S(1)}, bf16[640,512]{1,0:T(8,128)(2,1)}, u32[]{:S(2)}) copy-start(bf16[640,512]{1,0:T(8,128)(2,1)} %get-tuple-element.55.keys) | copy-start | bytes 1966084
  91.8 20.8 %copy-start.1 = (bf16[640,512]{1,0:T(8,128)(2,1)S(1)}, bf16[640,512]{1,0:T(8,128)(2,1)}, u32[]{:S(2)}) copy-start(bf16[640,512]{1,0:T(8,128)(2,1)} %get-tuple-element.56.values) | copy-start | bytes 1966084
  91.8 37.1 %all-to-all-start.2 = ((bf16[8,320,128]{2,1,0:T(8,128)(2,1)}), bf16[8,320,128]{2,1,0:T(8,128)(2,1)}, u32[]{:S(2)}, u32[]{:S(2)}) async-start(bf16[8,320,128]{2,1,0:T(8,128)(2,1)} %bitcast.19), calls=%async_computation.2 | async-start | bytes 1310720 | tf_op jit(solution)/shard_map/all_to_all | solution.py:663
  99.1 1.3 collective-permute-start.10
  101.1 21.5 %collective-permute-start.13 = (bf16[264,128]{1,0:T(8,128)(2,1)S(1)}, bf16[264,128]{1,0:T(8,128)(2,1)S(1)}, u32[]{:S(2)}, u32[]{:S(2)}) collective-permute-start(bf16[264,128]{1,0:T(8,128)(2,1)S(1)} %shard_map.98), channel_id=1, source_target_pairs={{6,0},{7,1},{14,8},{15,9},{22,16},{23,17},{30,24},{31,25},{38,32},... | collective-permute-start | bytes 202760 | tf_op jit(solution)/shard_map/ppermute | solution.py:624
  108.3 14.3 %collective-permute-start.12 = (bf16[264,128]{1,0:T(8,128)(2,1)S(1)}, bf16[264,128]{1,0:T(8,128)(2,1)S(1)}, u32[]{:S(2)}, u32[]{:S(2)}) collective-permute-start(bf16[264,128]{1,0:T(8,128)(2,1)S(1)} %shard_map.98), channel_id=1, source_target_pairs={{4,0},{5,1},{6,2},{7,3},{12,8},{13,9},{14,10},{15,11},{20,16},{21,... | collective-permute-start | bytes 202760 | tf_op jit(solution)/shard_map/ppermute | solution.py:624
  109.6 13.0 %collective-permute-start.11 = (bf16[264,128]{1,0:T(8,128)(2,1)S(1)}, bf16[264,128]{1,0:T(8,128)(2,1)S(1)}, u32[]{:S(2)}, u32[]{:S(2)}) collective-permute-start(bf16[264,128]{1,0:T(8,128)(2,1)S(1)} %shard_map.98), channel_id=1, source_target_pairs={{2,0},{3,1},{4,2},{5,3},{6,4},{7,5},{10,8},{11,9},{12,10},{13,11},... | collective-permute-start | bytes 202760 | tf_op jit(solution)/shard_map/ppermute | solution.py:624
  128.8 41.9 %copy-start.3 = (bf16[512,640]{1,0:T(8,128)(2,1)S(1)}, bf16[512,640]{1,0:T(8,128)(2,1)}, u32[]{:S(2)}) copy-start(bf16[512,640]{1,0:T(8,128)(2,1)} %get-tuple-element.34.back) | copy-start | bytes 1966084
  128.9 44.4 %all-to-all-start.3 = ((bf16[32,80,128]{2,1,0:T(8,128)(2,1)}), bf16[32,80,128]{2,1,0:T(8,128)(2,1)S(1)}, u32[]{:S(2)}, u32[]{:S(2)}) async-start(bf16[32,80,128]{2,1,0:T(8,128)(2,1)} %bitcast.17), calls=%async_computation.3 | async-start | bytes 1310720 | tf_op jit(solution)/shard_map/all_to_all | solution.py:632
  137.8 35.5 %copy-start.2 = (bf16[512,640]{1,0:T(8,128)(2,1)S(1)}, bf16[512,640]{1,0:T(8,128)(2,1)}, u32[]{:S(2)}) copy-start(bf16[512,640]{1,0:T(8,128)(2,1)} %get-tuple-element.53.back) | copy-start | bytes 1966084
  159.3 7.9 %collective-permute-start.7 = (bf16[8,80,128]{2,1,0:T(8,128)(2,1)}, bf16[8,80,128]{2,1,0:T(8,128)(2,1)S(1)}, u32[]{:S(2)}, u32[]{:S(2)}) collective-permute-start(bf16[8,80,128]{2,1,0:T(8,128)(2,1)} %get-tuple-element.50), channel_id=1, source_target_pairs={{0,8},{8,16},{16,24},{24,0},{32,40},{40,48},{48,56},{56,32},{64,72... | collective-permute-start | bytes 491528 | tf_op jit(solution)/shard_map/ppermute | solution.py:660
  161.2 9.5 %collective-permute-start.8 = (bf16[8,80,128]{2,1,0:T(8,128)(2,1)}, bf16[8,80,128]{2,1,0:T(8,128)(2,1)S(1)}, u32[]{:S(2)}, u32[]{:S(2)}) collective-permute-start(bf16[8,80,128]{2,1,0:T(8,128)(2,1)} %get-tuple-element.51), channel_id=1, source_target_pairs={{0,16},{8,24},{16,0},{24,8},{32,48},{40,56},{48,32},{56,40},{64,80... | collective-permute-start | bytes 491528 | tf_op jit(solution)/shard_map/ppermute | solution.py:660
  163.8 6.8 %collective-permute-start.9 = (bf16[8,80,128]{2,1,0:T(8,128)(2,1)}, bf16[8,80,128]{2,1,0:T(8,128)(2,1)S(1)}, u32[]{:S(2)}, u32[]{:S(2)}) collective-permute-start(bf16[8,80,128]{2,1,0:T(8,128)(2,1)} %get-tuple-element.52), channel_id=1, source_target_pairs={{0,24},{8,0},{16,8},{24,16},{32,56},{40,32},{48,40},{56,48},{64,88... | collective-permute-start | bytes 491528 | tf_op jit(solution)/shard_map/ppermute | solution.py:660
  (5 other events, 12.9 us)

commit v2 on v0

--- a/solution.py
+++ b/solution.py
@@ -14,6 +14,7 @@
 TN = (((0,), (0,)), ((), ()))
 EXACT = lax.Precision.HIGHEST
 LIMIT = 16 << 20
+WIDE = 256
 
 
 def dot(a, b, dims=NN, precision=None):
@@ -31,6 +32,7 @@
 VMEM = pl.BlockSpec(memory_space=pltpu.VMEM)
 SMEM = pl.BlockSpec(memory_space=pltpu.SMEM)
 HBM = pl.BlockSpec(memory_space=pltpu.HBM)
+ANY = pl.BlockSpec(memory_space=pl.ANY)
 
 
 def call(body, outs, ins, scratch=(), spaces=None, out_hbm=()):
@@ -101,6 +103,11 @@
     return copy
 
 
+def rows_copy(source, target, sems, j):
+    rows = pl.ds(pl.multiple_of(j * CH, CH), CH)
+    return pltpu.make_async_copy(source.at[rows, :], target.at[rows, :], sems.at[j])
+
+
 def expanded(fade, rows, p):
     here = fade[rows, :]
     shape = (here.shape[0], 128)
@@ -112,8 +119,8 @@
 
 
 def pack_events(
-    owner_in, events_in, elapsed_in, resets_in, message, place,
-    scratch, owner, events, elapsed, resets, sems,
+    owner_in, events_in, elapsed_in, resets_in, message, spots,
+    scratch, place, owner, events, elapsed, resets, sems,
 ):
     copies = [
         pltpu.make_async_copy(source, target, sems.at[i])
@@ -138,6 +145,8 @@
     earlier = ones_where(iota((rows, rows), 0) < iota((rows, rows), 1))
     before = dot(ones_where(hit), earlier)
     rank = jnp.sum(jnp.where(hit, before, 0.0), axis=0, keepdims=True).astype(jnp.int32)
+    spots[0:1, :] = own
+    spots[1:2, :] = own * cap + rank
     place[...] = ones_where(iota((slots, rows), 0) == own * cap + rank)
     for copy in copies[1:]:
         copy.wait()
@@ -161,16 +170,18 @@
     message[:, per : per + 8, :] = extra.astype(bf16)
 
 
-def pack_grads(info, place, grads, message, back, scratch):
+def pack_grads(info, spots, grads, message, back, scratch, narrow, turned, sems):
     rows, width = grads.shape
-    write_message(
-        message,
-        scratch,
-        lambda j: dot(place[...], grads[:, 128 * j : 128 * (j + 1)]),
-        width,
-    )
+    slots = turned.shape[1]
+    place = ones_where(iota((slots, rows), 0) == spots[1:2, :])
+    write_rows(scratch, lambda j: dot(place, grads[:, 128 * j : 128 * (j + 1)]), width // 128)
+    narrow[...] = scratch[...].astype(bf16)
+    copies = [fetched(narrow, message, sems.at[0])]
     same = ones_where(iota((rows, rows), 0) == iota((rows, rows), 1))
-    back[...] = dot(same, place[...], NT).astype(bf16)
+    turned[...] = dot(same, place, NT).astype(bf16)
+    copies.append(fetched(turned, back, sems.at[1]))
+    for copy in copies:
+        copy.wait()
 
 
 def unpack_rows(back, message, out, scratch):
@@ -334,24 +345,17 @@
             end = slice(CH * j + CH - 1, CH * j + CH)
             marks[j, pairs + p : pairs + p + 1, :] = expanded(fade, end, p)
     fetch.wait()
-    memory[...] = jnp.zeros(memory.shape, f32)
     mask = block_mask()
-
-    def project(j, carry):
-        rows = pl.ds(pl.multiple_of(j * CH, CH), CH)
-        here = x[rows, :]
-        k = dot(here, mine[0]).astype(bf16)
-        v = dot(here, mine[1]).astype(bf16)
-        keys[rows, :] = k
-        values[rows, :] = v
-        for p in range(pairs):
-            cols = slice(128 * p, 128 * (p + 1))
-            end = marks[blocks - 1, pairs + p : pairs + p + 1, :]
-            kf = (k[:, cols].astype(f32) * jnp.exp(end - expanded(fade, rows, p))).astype(bf16)
-            memory[p] += jnp.where(mask, dot(kf, v[:, cols], TN), 0.0)
-        return carry
-
-    lax.fori_loop(0, blocks, project, 0)
+    for n in range(0, width, WIDE):
+        cols = slice(n, n + WIDE)
+        keys[:, cols] = dot(x[...], mine[0, :, cols]).astype(bf16)
+        values[:, cols] = dot(x[...], mine[1, :, cols]).astype(bf16)
+    every = slice(0, slots)
+    for p in range(pairs):
+        cols = slice(128 * p, 128 * (p + 1))
+        end = marks[blocks - 1, pairs + p : pairs + p + 1, :]
+        kf = (keys[:, cols].astype(f32) * jnp.exp(end - expanded(fade, every, p))).astype(bf16)
+        memory[p] = jnp.where(mask, dot(kf, values[:, cols], TN), 0.0)
     stores.append(fetched(keys, keys_out, sems.at[3]))
     stores.append(fetched(values, values_out, sems.at[4]))
     write_state(send, memory, turned[:, slots - 1 : slots], pairs)
@@ -359,20 +363,19 @@
         store.wait()
 
 
-def project_queries(info, x_in, weights, q8, mine, x, sems):
-    arrival = fetched(x_in, x, sems.at[0])
-    fetched(weights.at[info[0], 0], mine, sems.at[1]).wait()
+def attend(
+    info, x_in, weights, keys, values, fade, fade_t, marks,
+    q8, attended_out, states,
+    memory, attended, x, mine, in_sems, sems,
+):
+    arrival = fetched(x_in, x, in_sems.at[0])
+    fetch = fetched(weights.at[info[0], 0], mine, in_sems.at[1])
     arrival.wait()
-
-    def project(j, carry):
-        rows = pl.ds(pl.multiple_of(j * CH, CH), CH)
-        q8[rows, :] = (dot(x[rows, :], mine[...]).astype(bf16).astype(f32) * 0.125).astype(bf16)
-        return carry
-
-    lax.fori_loop(0, x.shape[0] // CH, project, 0)
-
-
-def attend(q8, keys, values, fade, fade_t, marks, attended, states, memory):
+    fetch.wait()
+    for n in range(0, x.shape[1], WIDE):
+        cols = slice(n, n + WIDE)
+        query = dot(x[...], mine[:, cols]).astype(bf16).astype(f32)
+        q8[:, cols] = (query * 0.125).astype(bf16)
     slots, width = q8.shape
     pairs = width // 128
     low, high = halves()
@@ -396,20 +399,25 @@
             attended[rows, cols] = within + dot(lifted, now.astype(bf16))
             kf = (kp.astype(f32) * jnp.exp(end - g)).astype(bf16)
             memory[p] = jnp.exp(end - start) * now + jnp.where(mask, dot(kf, vp, TN), 0.0)
+        rows_copy(attended, attended_out, sems, j).start()
         return carry
 
     lax.fori_loop(0, slots // CH, block, 0)
-
-
-def turn(info, q8, fade, fade_t, attended, x_in, weights, message_in, partner, *rest):
-    received = rest[:-15]
+    for j in range(slots // CH):
+        rows_copy(attended, attended_out, sems, j).wait()
+
+
+def turn(info, q8, fade, fade_t, attended_in, x_in, weights, message_in, partner, *rest):
+    received = rest[:-20]
     (
-        encoded, grads, grad_full, incoming, send,
-        scratch, message, mine, x, wide, narrow, states, memory, sems, out_sems,
-    ) = rest[-15:]
-    arrival = fetched(message_in, message, sems.at[0])
-    fetch = fetched(weights.at[info[0], 3], mine, sems.at[1])
-    rows_in = fetched(x_in, x, sems.at[2])
+        encoded, grads_out, grad_full, incoming, send,
+        scratch, message, mine, x, attended, grads, grad_normed, normed, lifts,
+        wide, narrow, states, memory, sems, out_sems,
+    ) = rest[-20:]
+    arrival = fetched(message_in, message, sems.at[2])
+    fetch = fetched(weights.at[info[0], 3], mine, sems.at[0])
+    rows_in = fetched(x_in, x, sems.at[1])
+    attended_here = fetched(attended_in, attended, sems.at[3])
     slots, width = x.shape
     pairs = width // 128
     blocks = slots // CH
@@ -417,47 +425,66 @@
     for p, state in enumerate(gathered_state(info[1].astype(f32), partner, received, pairs)):
         incoming[p] = state
         states[p] = unfolded(state, mask).astype(bf16)
-    memory[...] = jnp.zeros(memory.shape, f32)
     arrival.wait()
     for j, part in enumerate(read_message(message, scratch, width)):
         grads[:, 128 * j : 128 * (j + 1)] = part.astype(bf16)
+    store = fetched(grads, grads_out, sems.at[4])
     fetch.wait()
-    rows_in.wait()
-    sender = Sender(encoded, wide, narrow, out_sems, pairs)
+    for n in range(0, width, WIDE):
+        cols = slice(n, n + WIDE)
+        grad_normed[:, cols] = dot(grads[...], mine[cols, :], NT).astype(bf16)
+    attended_here.wait()
 
     def block(j, carry):
         rows = pl.ds(pl.multiple_of(j * CH, CH), CH)
-        values, lifts = [], []
+        values = []
         square = jnp.zeros((CH, 1), f32)
         for p in range(pairs):
             cols = slice(128 * p, 128 * (p + 1))
             lifted = (q8[rows, cols].astype(f32) * jnp.exp(expanded(fade, rows, p))).astype(bf16)
-            lifts.append(lifted)
+            lifts[rows, cols] = lifted
             value = attended[rows, cols] + dot(lifted, states[p])
             values.append(value)
             square += jnp.sum(value * value, axis=1, keepdims=True)
         here = jnp.concatenate(values, axis=1)
         scale = lax.rsqrt(square * (1.0 / width) + 1e-06)
-        normed = (here * scale).astype(bf16)
-        sender.put(j, x[rows, :].astype(f32) + dot(normed, mine[...]))
-        grad = dot(grads[rows, :], mine[...], NT).astype(bf16).astype(f32)
+        normed[rows, :] = (here * scale).astype(bf16)
+        grad = grad_normed[rows, :].astype(f32)
         along = jnp.mean(here * grad, axis=1, keepdims=True)
-        da = (scale * grad - here * (scale * scale * scale * along)).astype(bf16)
-        grad_full[rows, :] = da
-        for p in range(pairs):
-            cols = slice(128 * p, 128 * (p + 1))
-            memory[p] += jnp.where(mask, dot(lifts[p], da[:, cols], TN), 0.0)
+        grad_full[rows, :] = (scale * grad - here * (scale * scale * scale * along)).astype(bf16)
         return carry
 
     lax.fori_loop(0, blocks, block, 0)
+    for p in range(pairs):
+        cols = slice(128 * p, 128 * (p + 1))
+        memory[p] = jnp.where(mask, dot(lifts[:, cols], grad_full[:, cols], TN), 0.0)
     write_state(send, memory, fade_t[blocks - 1][:, CH - 1 : CH], pairs)
+    rows_in.wait()
+    for n in range(0, width, WIDE):
+        cols = slice(n, n + WIDE)
+        attended[:, cols] = x[:, cols].astype(f32) + dot(normed[...], mine[:, cols])
+    sender = Sender(encoded, wide, narrow, out_sems, pairs)
+
+    def put(j, carry):
+        sender.put(j, attended[pl.ds(pl.multiple_of(j * CH, CH), CH), :])
+        return carry
+
+    lax.fori_loop(0, blocks, put, 0)
     sender.finish(blocks)
+    store.wait()
 
 
 def backward_local(
-    q8, keys, values, fade, fade_t, marks, grad_full, states, incoming,
-    grad_q, grad_keys, grad_values, memory,
+    info, q8, keys_in, values_in, fade, fade_t, marks, grad_full, states, incoming, grads_in,
+    weights,
+    grad_keys, grad_values, partial,
+    memory, grad_q, grads, mine, keys, values, sems, key_sems, value_sems,
 ):
+    for j in reversed(range(q8.shape[0] // CH)):
+        rows_copy(keys_in, keys, key_sems, j).start()
+        rows_copy(values_in, values, value_sems, j).start()
+    arrival = fetched(grads_in, grads, sems.at[0])
+    fetch = fetched(weights.at[info[0], 0], mine, sems.at[1])
     slots, width = q8.shape
     pairs = width // 128
     blocks = slots // CH
@@ -468,6 +495,8 @@
 
     def block(i, carry):
         j = blocks - 1 - i
+        rows_copy(keys_in, keys, key_sems, j).wait()
+        rows_copy(values_in, values, value_sems, j).wait()
         rows = pl.ds(pl.multiple_of(j * CH, CH), CH)
         edge = marks[j]
         for p in range(pairs):
@@ -498,25 +527,21 @@
         return carry
 
     lax.fori_loop(0, blocks, block, 0)
-
-
-def project_back(info, grads, grad_q, weights, partial, mine, sem):
-    fetched(weights.at[info[0], 0], mine, sem).wait()
-
-    def project(j, carry):
-        rows = pl.ds(pl.multiple_of(j * CH, CH), CH)
-        partial[rows, :] = grads[rows, :].astype(f32) + dot(grad_q[rows, :], mine[...], NT)
-        return carry
-
-    lax.fori_loop(0, grads.shape[0] // CH, project, 0)
+    arrival.wait()
+    fetch.wait()
+    for n in range(0, width, WIDE):
+        cols = slice(n, n + WIDE)
+        partial[:, cols] = grads[:, cols].astype(f32) + dot(grad_q[...], mine[cols, :], NT)
 
 
 def backward_finish(
-    info, partial, grad_keys, grad_values, keys, values, fade, marks, weights, partner, *rest
+    info, partial, grad_keys, grad_values, keys_in, values_in, fade, marks, weights, partner, *rest
 ):
-    received = rest[:-9]
-    out, mine, wide, narrow, states, gk, gv, sem, out_sems = rest[-9:]
-    fetch = fetched(weights.at[info[0], pl.ds(1, 2)], mine, sem)
+    received = rest[:-12]
+    out, mine, wide, narrow, states, gk, gv, total, keys, values, sems, out_sems = rest[-12:]
+    keys_here = fetched(keys_in, keys, sems.at[1])
+    values_here = fetched(values_in, values, sems.at[2])
+    fetch = fetched(weights.at[info[0], pl.ds(1, 2)], mine, sems.at[0])
     slots, width = partial.shape
     pairs = width // 128
     blocks = slots // CH
@@ -524,23 +549,30 @@
     arrived = gathered_state((1 - info[1]).astype(f32), partner, received, pairs)
     for p, state in enumerate(arrived):
         states[p] = unfolded(state, mask).astype(bf16)
+    every = slice(0, slots)
+    keys_here.wait()
+    values_here.wait()
+    for p in range(pairs):
+        cols = slice(128 * p, 128 * (p + 1))
+        end = marks[blocks - 1, pairs + p : pairs + p + 1, :]
+        fall = jnp.exp(end - expanded(fade, every, p))
+        kf = (keys[:, cols].astype(f32) * fall).astype(bf16)
+        state = states[p]
+        gk[:, cols] = (grad_keys[:, cols] + fall * dot(values[:, cols], state, NT)).astype(bf16)
+        gv[:, cols] = (grad_values[:, cols] + dot(kf, state)).astype(bf16)
+    fetch.wait()
+    for n in range(0, width, WIDE):
+        cols = slice(n, n + WIDE)
+        total[:, cols] = (
+            partial[:, cols] + dot(gk[...], mine[0, cols, :], NT) + dot(gv[...], mine[1, cols, :], NT)
+        )
     sender = Sender(out, wide, narrow, out_sems, pairs)
-    fetch.wait()
-
-    def block(j, carry):
-        rows = pl.ds(pl.multiple_of(j * CH, CH), CH)
-        for p in range(pairs):
-            cols = slice(128 * p, 128 * (p + 1))
-            end = marks[blocks - 1, pairs + p : pairs + p + 1, :]
-            fall = jnp.exp(end - expanded(fade, rows, p))
-            kf = (keys[rows, cols].astype(f32) * fall).astype(bf16)
-            state = states[p]
-            gk[:, cols] = (grad_keys[rows, cols] + fall * dot(values[rows, cols], state, NT)).astype(bf16)
-            gv[:, cols] = (grad_values[rows, cols] + dot(kf, state)).astype(bf16)
-        sender.put(j, partial[rows, :] + dot(gk[...], mine[0], NT) + dot(gv[...], mine[1], NT))
+
+    def put(j, carry):
+        sender.put(j, total[pl.ds(pl.multiple_of(j * CH, CH), CH), :])
         return carry
 
-    lax.fori_loop(0, blocks, block, 0)
+    lax.fori_loop(0, blocks, put, 0)
     sender.finish(blocks)
 
 
@@ -573,15 +605,15 @@
     flat = pltpu.VMEM((slots * pairs, 128), f32)
     state_vmem = pltpu.VMEM((pairs, 128, 128), f32)
     state_msg = ((64 * pairs + 8, 128), bf16)
-    wide_msg = ((owners, per, 128), bf16)
     wide16, wide32 = ((slots, width), bf16), ((slots, width), f32)
 
     tower = lax.axis_index("log") // (owners // decay_rates.shape[0])
     info = jnp.stack([tower, lax.axis_index("ctx") % 2]).astype(jnp.int32)
-
-    message, place = call(
+    sem = pltpu.SemaphoreType.DMA
+
+    message, spots = call(
         pack_events,
-        [((owners, per + 8, 128), bf16), ((slots, rows), bf16)],
+        [((owners, per + 8, 128), bf16), ((2, rows), jnp.int32)],
         [
             owner_ids.reshape(1, rows),
             events.reshape(rows, width),
@@ -590,6 +622,7 @@
         ],
         [
             flat,
+            pltpu.VMEM((slots, rows), bf16),
             pltpu.VMEM((1, rows), jnp.int32),
             pltpu.VMEM((rows, width), bf16),
             pltpu.VMEM((1, rows), f32),
@@ -599,22 +632,22 @@
         {0: HBM, 1: HBM, 2: HBM, 3: HBM},
     )
     events_in = regroup(message)
+    flat_msg = ((slots * pairs, 128), bf16)
     message, back = call(
         pack_grads,
-        [wide_msg, ((rows, slots), bf16)],
-        [info, place, cotangent.reshape(rows, width)],
-        [flat],
+        [flat_msg, ((rows, slots), bf16)],
+        [info, spots, cotangent.reshape(rows, width)],
+        [flat, pltpu.VMEM(*flat_msg), pltpu.VMEM((rows, slots), bf16), sem((2,))],
         {0: SMEM},
-    )
-    grads_in = regroup(message)
+        (0, 1),
+    )
+    grads_in = regroup(message.reshape(owners, per, 128))
     one = pltpu.VMEM((width, width), bf16)
     two = pltpu.VMEM((2, width, width), bf16)
-    sem = pltpu.SemaphoreType.DMA
     half_states = ((pairs, 64, 128), f32)
-    flat_msg = ((slots * pairs, 128), bf16)
     block_wide = pltpu.VMEM((CH * pairs, 128), f32)
     flat_narrow = pltpu.VMEM(*flat_msg)
-    rows16 = pltpu.VMEM(*wide16)
+    rows16, rows32 = pltpu.VMEM(*wide16), pltpu.VMEM(*wide32)
     narrow_states = pltpu.VMEM((pairs, 128, 128), bf16)
     x, keys, values, keys_far, values_far, fade, fade_t, marks, send = call(
         forward_state,
@@ -628,45 +661,44 @@
         (0, 3, 4),
     )
     partner = swapped(send, "ctx")
-    (q8,) = call(
-        project_queries,
-        [wide16],
-        [info, x, weights],
-        [one, rows16, sem((2,))],
-        {0: SMEM, 1: HBM, 2: HBM},
-    )
     (joined,) = call(join_ahead, [state_msg], [info, send, partner], (), {0: SMEM})
     received = exchange(joined, "ctx", 1)
-    attended, kept = call(
+    q8, attended, kept = call(
         attend,
-        [wide32, ((blocks, pairs, 64, 128), bf16)],
-        [q8, keys, values, fade, fade_t, marks],
-        [state_vmem],
+        [wide16, wide32, ((blocks, pairs, 64, 128), bf16)],
+        [info, x, weights, keys, values, fade, fade_t, marks],
+        [state_vmem, rows32, rows16, one, sem((2,)), sem((blocks,))],
+        {0: SMEM, 1: HBM, 2: HBM},
+        (1,),
     )
     message, grads, grad_full, incoming, send = call(
         turn,
         [flat_msg, wide16, wide16, half_states, state_msg],
         [info, q8, fade, fade_t, attended, x, weights, grads_in, partner, *received],
         [
-            flat, pltpu.VMEM(*wide_msg), one, rows16, block_wide, flat_narrow, narrow_states,
-            state_vmem, sem((3,)), sem((blocks,)),
-        ],
-        {0: SMEM, 5: HBM, 6: HBM, 7: HBM},
-        (0,),
+            flat, pltpu.VMEM((owners, per, 128), bf16), one, rows16, rows32, rows16, rows16, rows16,
+            rows16, block_wide, flat_narrow, narrow_states, state_vmem, sem((5,)), sem((blocks,)),
+        ],
+        {0: SMEM, 4: HBM, 5: HBM, 6: HBM, 7: ANY},
+        (0, 1),
     )
     partner = swapped(send, "ctx")
     encoded_in = regroup(message.reshape(owners, per, 128))
-    grad_q, grad_keys, grad_values = call(
+    grad_keys, grad_values, partial = call(
         backward_local,
-        [wide16, wide32, wide32],
-        [q8, keys_far, values_far, fade, fade_t, marks, grad_full, kept, incoming],
-        [state_vmem],
+        [wide32, wide32, wide32],
+        [
+            info, q8, keys_far, values_far, fade, fade_t, marks, grad_full, kept, incoming, grads,
+            weights,
+        ],
+        [
+            state_vmem, rows16, rows16, one, rows16, rows16, sem((2,)), sem((blocks,)),
+            sem((blocks,)),
+        ],
+        {0: SMEM, 2: HBM, 3: HBM, 10: HBM, 11: HBM},
     )
     (joined,) = call(join_back, [state_msg], [info, send, partner], (), {0: SMEM})
     received = exchange(joined, "ctx", -1)
-    (partial,) = call(
-        project_back, [wide32], [info, grads, grad_q, weights], [one, sem], {0: SMEM, 3: HBM}
-    )
     (message,) = call(
         backward_finish,
         [flat_msg],
@@ -676,9 +708,9 @@
         ],
         [
             two, block_wide, flat_narrow, narrow_states,
-            pltpu.VMEM((CH, width), bf16), pltpu.VMEM((CH, width), bf16), sem, sem((blocks,)),
-        ],
-        {0: SMEM, 8: HBM},
+            rows16, rows16, rows32, rows16, rows16, sem((3,)), sem((blocks,)),
+        ],
+        {0: SMEM, 4: HBM, 5: HBM, 8: HBM},
         (0,),
     )
     grad_in = regroup(message.reshape(owners, per, 128))

time: 152 us -> 139 us (0.914)
  local copies, waits for them, and re-layouts: 7.32 us -> 0.02 us
  Pallas kernels: 50 us -> 44.6 us
    unnamed x30 -> x8, local copies, waits for them, and re-layouts: 7.32 us -> 0.02 us
    pallas_call x13 -> x11, Pallas kernels: 50 us -> 44.6 us  [call(): pl.pallas_call(body, out_shape=[pltpu.HBM(s, d) if i in out_hbm else jax....]
    all_to_all x4, waiting for transfers between devices: 36.3 us -> 37.8 us  [regroup(): return lax.all_to_all(value, 'log', split_axis=0, concat_axis=0, tiled=True)]
  transfers between devices with their start and end apart: 12 -> 12, of which waited for: 5 -> 6; matrix products, arithmetic and copies ran while one was open for 0% -> 0% of each run, Pallas kernels for 24% -> 23%
where the time goes in v2:
time: 139 us; the launch traced here: 138 us
  starting transfers between devices  51.7 us (37%)
  Pallas kernels  44.6 us (32%)
  waiting for transfers between devices  40.6 us (29%)
    pallas_call x11, Pallas kernels, call(): pl.pallas_call(body, out_shape=[pltpu.HBM(s, d) if i in out_hbm else jax....  44.6 us
    all_to_all x4, waiting for transfers between devices, regroup(): return lax.all_to_all(value, 'log', split_axis=0, concat_axis=0, tiled=True)  37.8 us
    all_to_all x4, starting transfers between devices, regroup(): return lax.all_to_all(value, 'log', split_axis=0, concat_axis=0, tiled=True)  36 us
    ppermute x6, starting transfers between devices, exchange(): lax.ppermute(value, axis, [(i, i + sign * k) for i in range(count) if 0 <...  15.5 us
  transfers between devices with their start and end apart: 12, of which 6 were waited for; matrix products, arithmetic and copies ran while one was open for 0% of the time, Pallas kernels for 23%

profile of v2, /device:TPU:24, one launch (start us, length us, event | category | flops | bytes accessed | tf_op | source)
XLA Modules:
  0.0 137.9 jit_solution(8845901703402995586)
XLA Ops:
  0.6 3.2 %shard_map.86 = (bf16[32,88,128]{2,1,0:T(8,128)(2,1)}, s32[2,512]{1,0:T(2,128)S(1)}) custom-call(s32[1,512]{1,0:T(1,128)} %bitcast.19, bf16[512,512]{1,0:T(8,128)(2,1)} %bitcast.18, f32[1,512]{1,0:T(1,128)} %bitcast.20, f32[1,512]{1,0:T(1,128)} %bitcast.21), custom_call_target="tpu_custom_call" | custom-call | tf_op jit(solution)/shard_map/pallas_call | solution.py:43
  3.9 11.3 %all-to-all-start = ((bf16[32,88,128]{2,1,0:T(8,128)(2,1)}), bf16[32,88,128]{2,1,0:T(8,128)(2,1)S(1)}, u32[]{:S(2)}, u32[]{:S(2)}) async-start(bf16[32,88,128]{2,1,0:T(8,128)(2,1)} %get-tuple-element.28), calls=%async_computation | async-start | bytes 1441792 | tf_op jit(solution)/shard_map/all_to_all | solution.py:594
  15.3 2.8 %shard_map.87 = (bf16[2560,128]{1,0:T(8,128)(2,1)}, bf16[512,640]{1,0:T(8,128)(2,1)}) custom-call(s32[2]{0:T(128)S(1)} %pad_add_fusion.info, s32[2,512]{1,0:T(2,128)S(1)} %get-tuple-element.26.spots, bf16[512,512]{1,0:T(8,128)(2,1)S(1)} %bitcast.12), custom_call_target="tpu_custom_call" | custom-call | tf_op jit(solution)/shard_map/pallas_call | solution.py:43
  18.1 18.7 %all-to-all-done.message_in = bf16[32,88,128]{2,1,0:T(8,128)(2,1)S(1)} async-done(((bf16[32,88,128]{2,1,0:T(8,128)(2,1)}), bf16[32,88,128]{2,1,0:T(8,128)(2,1)S(1)}, u32[]{:S(2)}, u32[]{:S(2)}) %all-to-all-start) | async-done | bytes 720928 | tf_op jit(solution)/shard_map/all_to_all | solution.py:594
  36.8 5.0 %all-to-all-start.1 = ((bf16[32,80,128]{2,1,0:T(8,128)(2,1)}), bf16[32,80,128]{2,1,0:T(8,128)(2,1)S(1)}, u32[]{:S(2)}, u32[]{:S(2)}) async-start(bf16[32,80,128]{2,1,0:T(8,128)(2,1)} %bitcast.15), calls=%async_computation.1 | async-start | bytes 1310720 | tf_op jit(solution)/shard_map/all_to_all | solution.py:594
  41.9 5.4 %shard_map.88 = (bf16[640,512]{1,0:T(8,128)(2,1)}, bf16[640,512]{1,0:T(8,128)(2,1)S(1)}, bf16[640,512]{1,0:T(8,128)(2,1)S(1)}, bf16[640,512]{1,0:T(8,128)(2,1)},...) custom-call(s32[2]{0:T(128)S(1)} %pad_add_fusion.info, ...), custom_call_target="tpu_custom_call" | custom-call | tf_op jit(solution)/shard_map/pallas_call | solution.py:43
  47.4 1.2 collective-permute-done.other.partner
  49.3 1.3 collective-permute-start.1
  50.6 1.3 collective-permute-start.2
  51.9 1.3 collective-permute-start.3
  53.2 7.1 %shard_map.89 = (bf16[640,512]{1,0:T(8,128)(2,1)S(1)}, f32[640,512]{1,0:T(8,128)}, bf16[5,4,64,128]{3,2,1,0:T(8,128)(2,1)S(1)}) custom-call(s32[2]{0:T(128)S(1)} %pad_add_fusion.info, bf16[640,512]{1,0:T(8,128)(2,1)} %get-tuple-element.29.x_in, bf16[4,4,512,512]{3,2,1,0:T(8,128)(2,1)} %weights.9, bf16[640,512]{1,0:T(8,128)(2,1)S(1)} %get-tuple-element.30.keys, ...), custom_call_target="tpu_custom_call" | custom-call | tf_op jit(solution)/shard_map/pallas_call | solution.py:43
  60.3 0.8 all-to-all-done.1.message_in
  61.4 7.8 %shard_map.91 = (bf16[2560,128]{1,0:T(8,128)(2,1)}, bf16[640,512]{1,0:T(8,128)(2,1)}, bf16[640,512]{1,0:T(8,128)(2,1)S(1)}, f32[4,64,128]{2,1,0:T(8,128)S(1)}, bf16[264,128]{1,0:T(8,128)(2,1)S(1)}) custom-call(s32[2]{0:T(128)S(1)} %pad_add_fusion.info, bf16[640,512]{1,0:T(8,128)(2,1)S(1)} %get-tuple-element.35.q8, f32[640,128]{1,0:T(8,128)S(1)} %get-tuple-element.32.fade, ...), custom_call_target="tpu_custom_call" | custom-call | tf_op jit(solution)/shard_map/pallas_call | solution.py:43
  69.2 9.8 %all-to-all-start.2 = ((bf16[32,80,128]{2,1,0:T(8,128)(2,1)}), bf16[32,80,128]{2,1,0:T(8,128)(2,1)S(1)}, u32[]{:S(2)}, u32[]{:S(2)}) async-start(bf16[32,80,128]{2,1,0:T(8,128)(2,1)} %bitcast.14), calls=%async_computation.2 | async-start | bytes 1310720 | tf_op jit(solution)/shard_map/all_to_all | solution.py:594
  79.1 1.2 collective-permute-done.4.other.partner
  81.1 2.9 %collective-permute-start.5 = (bf16[264,128]{1,0:T(8,128)(2,1)S(1)}, bf16[264,128]{1,0:T(8,128)(2,1)S(1)}, u32[]{:S(2)}, u32[]{:S(2)}) collective-permute-start(bf16[264,128]{1,0:T(8,128)(2,1)S(1)} %shard_map.94), channel_id=1, source_target_pairs={{2,0},{3,1},{4,2},{5,3},{6,4},{7,5},{10,8},{11,9},{12,10},{13,11},... | collective-permute-start | bytes 202760 | tf_op jit(solution)/shard_map/ppermute | solution.py:586
  84.0 7.3 %collective-permute-start.6 = (bf16[264,128]{1,0:T(8,128)(2,1)S(1)}, bf16[264,128]{1,0:T(8,128)(2,1)S(1)}, u32[]{:S(2)}, u32[]{:S(2)}) collective-permute-start(bf16[264,128]{1,0:T(8,128)(2,1)S(1)} %shard_map.94), channel_id=1, source_target_pairs={{4,0},{5,1},{6,2},{7,3},{12,8},{13,9},{14,10},{15,11},{20,16},{21,... | collective-permute-start | bytes 202760 | tf_op jit(solution)/shard_map/ppermute | solution.py:586
  91.3 1.5 %collective-permute-start.7 = (bf16[264,128]{1,0:T(8,128)(2,1)S(1)}, bf16[264,128]{1,0:T(8,128)(2,1)S(1)}, u32[]{:S(2)}, u32[]{:S(2)}) collective-permute-start(bf16[264,128]{1,0:T(8,128)(2,1)S(1)} %shard_map.94), channel_id=1, source_target_pairs={{6,0},{7,1},{14,8},{15,9},{22,16},{23,17},{30,24},{31,25},{38,32},... | collective-permute-start | bytes 202760 | tf_op jit(solution)/shard_map/ppermute | solution.py:586
  92.8 8.8 %shard_map.93 = (f32[640,512]{1,0:T(8,128)S(1)}, f32[640,512]{1,0:T(8,128)S(1)}, f32[640,512]{1,0:T(8,128)S(1)}) custom-call(s32[2]{0:T(128)S(1)} %pad_add_fusion.info, bf16[640,512]{1,0:T(8,128)(2,1)S(1)} %get-tuple-element.35.q8, bf16[640,512]{1,0:T(8,128)(2,1)} %get-tuple-element.40.keys_in, bf16[640,512]{1,0:T(8,128)(2,1)} %get-tuple-element.41.values_in, ...), custom_call_target="tpu_custom_call" | custom-call | tf_op jit(solution)/shard_map/pallas_call | solution.py:43
  101.6 4.7 %shard_map.95 = bf16[2560,128]{1,0:T(8,128)(2,1)} custom-call(s32[2]{0:T(128)S(1)} %pad_add_fusion.info, f32[640,512]{1,0:T(8,128)S(1)} %get-tuple-element.46.partial, f32[640,512]{1,0:T(8,128)S(1)} %get-tuple-element.47.grad_keys, f32[640,512]{1,0:T(8,128)S(1)} %get-tuple-element.48.grad_values, bf16[640,512]{1,0:T(8,128)(2,1)} %get-tuple-element.40.keys_in, ...), custom_call_target="tpu_custom_call" | custom-call | tf_op jit(solution)/shard_map/pallas_call | solution.py:43
  106.3 9.9 %all-to-all-start.3 = ((bf16[32,80,128]{2,1,0:T(8,128)(2,1)}), bf16[32,80,128]{2,1,0:T(8,128)(2,1)S(1)}, u32[]{:S(2)}, u32[]{:S(2)}) async-start(bf16[32,80,128]{2,1,0:T(8,128)(2,1)} %bitcast.13), calls=%async_computation.3 | async-start | bytes 1310720 | tf_op jit(solution)/shard_map/all_to_all | solution.py:594
  116.3 1.7 %shard_map.92 = bf16[512,512]{1,0:T(8,128)(2,1)} custom-call(bf16[512,640]{1,0:T(8,128)(2,1)S(1)} %copy-done, bf16[32,80,128]{2,1,0:T(8,128)(2,1)S(1)} %all-to-all-done.2.message), custom_call_target="tpu_custom_call" | custom-call | tf_op jit(solution)/shard_map/pallas_call | solution.py:43
  118.0 18.3 %all-to-all-done.3.message = bf16[32,80,128]{2,1,0:T(8,128)(2,1)S(1)} async-done(((bf16[32,80,128]{2,1,0:T(8,128)(2,1)}), bf16[32,80,128]{2,1,0:T(8,128)(2,1)S(1)}, u32[]{:S(2)}, u32[]{:S(2)}) %all-to-all-start.3) | async-done | bytes 655392 | tf_op jit(solution)/shard_map/all_to_all | solution.py:594
  136.2 1.7 %shard_map.96 = bf16[512,512]{1,0:T(8,128)(2,1)} custom-call(bf16[512,640]{1,0:T(8,128)(2,1)S(1)} %copy-done, bf16[32,80,128]{2,1,0:T(8,128)(2,1)S(1)} %all-to-all-done.3.message), custom_call_target="tpu_custom_call" | custom-call | tf_op jit(solution)/shard_map/pallas_call | solution.py:43
  (20 shorter events, 2.0 us)
Async XLA Ops:
  0.6 14.7 %copy-start.1 = (bf16[1,1,512,512]{3,2,1,0:T(8,128)(2,1)S(1)}, bf16[1,1,512,512]{3,2,1,0:T(8,128)(2,1)}, u32[]{:S(2)}) copy-start(bf16[1,1,512,512]{3,2,1,0:T(8,128)(2,1)} %param.13) | copy-start | bytes 1572868
  3.9 33.0 %all-to-all-start = ((bf16[32,88,128]{2,1,0:T(8,128)(2,1)}), bf16[32,88,128]{2,1,0:T(8,128)(2,1)S(1)}, u32[]{:S(2)}, u32[]{:S(2)}) async-start(bf16[32,88,128]{2,1,0:T(8,128)(2,1)} %get-tuple-element.28), calls=%async_computation | async-start | bytes 1441792 | tf_op jit(solution)/shard_map/all_to_all | solution.py:594
  15.2 26.6 %copy-start.2 = (f32[4,8]{1,0:T(4,128)S(1)}, f32[4,8]{1,0:T(4,128)}, u32[]{:S(2)}) copy-start(f32[4,8]{1,0:T(4,128)} %rates.1) | copy-start | bytes 388
  36.8 5.0 %copy-start.3 = (bf16[32,88,128]{2,1,0:T(8,128)(2,1)}, bf16[32,88,128]{2,1,0:T(8,128)(2,1)S(1)}, u32[]{:S(2)}) copy-start(bf16[32,88,128]{2,1,0:T(8,128)(2,1)S(1)} %all-to-all-done.message_in) | copy-start | bytes 2162692
  36.8 24.3 %all-to-all-start.1 = ((bf16[32,80,128]{2,1,0:T(8,128)(2,1)}), bf16[32,80,128]{2,1,0:T(8,128)(2,1)S(1)}, u32[]{:S(2)}, u32[]{:S(2)}) async-start(bf16[32,80,128]{2,1,0:T(8,128)(2,1)} %bitcast.15), calls=%async_computation.1 | async-start | bytes 1310720 | tf_op jit(solution)/shard_map/all_to_all | solution.py:594
  47.3 1.3 collective-permute-start
  49.3 11.8 %collective-permute-start.1 = (bf16[264,128]{1,0:T(8,128)(2,1)S(1)}, bf16[264,128]{1,0:T(8,128)(2,1)S(1)}, u32[]{:S(2)}, u32[]{:S(2)}) collective-permute-start(bf16[264,128]{1,0:T(8,128)(2,1)S(1)} %shard_map.90), channel_id=1, source_target_pairs={{0,2},{1,3},{2,4},{3,5},{4,6},{5,7},{8,10},{9,11},{10,12},{11,13},... | collective-permute-start | bytes 202760 | tf_op jit(solution)/shard_map/ppermute | solution.py:586
  50.6 10.5 %collective-permute-start.2 = (bf16[264,128]{1,0:T(8,128)(2,1)S(1)}, bf16[264,128]{1,0:T(8,128)(2,1)S(1)}, u32[]{:S(2)}, u32[]{:S(2)}) collective-permute-start(bf16[264,128]{1,0:T(8,128)(2,1)S(1)} %shard_map.90), channel_id=1, source_target_pairs={{0,4},{1,5},{2,6},{3,7},{8,12},{9,13},{10,14},{11,15},{16,20},{17,... | collective-permute-start | bytes 202760 | tf_op jit(solution)/shard_map/ppermute | solution.py:586
  51.9 9.5 %collective-permute-start.3 = (bf16[264,128]{1,0:T(8,128)(2,1)S(1)}, bf16[264,128]{1,0:T(8,128)(2,1)S(1)}, u32[]{:S(2)}, u32[]{:S(2)}) collective-permute-start(bf16[264,128]{1,0:T(8,128)(2,1)S(1)} %shard_map.90), channel_id=1, source_target_pairs={{0,6},{1,7},{8,14},{9,15},{16,22},{17,23},{24,30},{25,31},{32,38},... | collective-permute-start | bytes 202760 | tf_op jit(solution)/shard_map/ppermute | solution.py:586
  69.2 37.1 %all-to-all-start.2 = ((bf16[32,80,128]{2,1,0:T(8,128)(2,1)}), bf16[32,80,128]{2,1,0:T(8,128)(2,1)S(1)}, u32[]{:S(2)}, u32[]{:S(2)}) async-start(bf16[32,80,128]{2,1,0:T(8,128)(2,1)} %bitcast.14), calls=%async_computation.2 | async-start | bytes 1310720 | tf_op jit(solution)/shard_map/all_to_all | solution.py:594
  79.0 1.3 collective-permute-start.4
  81.1 20.5 %collective-permute-start.5 = (bf16[264,128]{1,0:T(8,128)(2,1)S(1)}, bf16[264,128]{1,0:T(8,128)(2,1)S(1)}, u32[]{:S(2)}, u32[]{:S(2)}) collective-permute-start(bf16[264,128]{1,0:T(8,128)(2,1)S(1)} %shard_map.94), channel_id=1, source_target_pairs={{2,0},{3,1},{4,2},{5,3},{6,4},{7,5},{10,8},{11,9},{12,10},{13,11},... | collective-permute-start | bytes 202760 | tf_op jit(solution)/shard_map/ppermute | solution.py:586
  84.0 17.6 %collective-permute-start.6 = (bf16[264,128]{1,0:T(8,128)(2,1)S(1)}, bf16[264,128]{1,0:T(8,128)(2,1)S(1)}, u32[]{:S(2)}, u32[]{:S(2)}) collective-permute-start(bf16[264,128]{1,0:T(8,128)(2,1)S(1)} %shard_map.94), channel_id=1, source_target_pairs={{4,0},{5,1},{6,2},{7,3},{12,8},{13,9},{14,10},{15,11},{20,16},{21,... | collective-permute-start | bytes 202760 | tf_op jit(solution)/shard_map/ppermute | solution.py:586
  91.3 10.3 %collective-permute-start.7 = (bf16[264,128]{1,0:T(8,128)(2,1)S(1)}, bf16[264,128]{1,0:T(8,128)(2,1)S(1)}, u32[]{:S(2)}, u32[]{:S(2)}) collective-permute-start(bf16[264,128]{1,0:T(8,128)(2,1)S(1)} %shard_map.94), channel_id=1, source_target_pairs={{6,0},{7,1},{14,8},{15,9},{22,16},{23,17},{30,24},{31,25},{38,32},... | collective-permute-start | bytes 202760 | tf_op jit(solution)/shard_map/ppermute | solution.py:586
  106.3 9.9 %copy-start = (bf16[512,640]{1,0:T(8,128)(2,1)S(1)}, bf16[512,640]{1,0:T(8,128)(2,1)}, u32[]{:S(2)}) copy-start(bf16[512,640]{1,0:T(8,128)(2,1)} %get-tuple-element.27.back) | copy-start | bytes 1966084
  106.3 29.9 %all-to-all-start.3 = ((bf16[32,80,128]{2,1,0:T(8,128)(2,1)}), bf16[32,80,128]{2,1,0:T(8,128)(2,1)S(1)}, u32[]{:S(2)}, u32[]{:S(2)}) async-start(bf16[32,80,128]{2,1,0:T(8,128)(2,1)} %bitcast.13), calls=%async_computation.3 | async-start | bytes 1310720 | tf_op jit(solution)/shard_map/all_to_all | solution.py:594

commit v3 on v2

--- a/solution.py
+++ b/solution.py
@@ -108,14 +108,19 @@
     return pltpu.make_async_copy(source.at[rows, :], target.at[rows, :], sems.at[j])
 
 
-def expanded(fade, rows, p):
-    here = fade[rows, :]
-    shape = (here.shape[0], 128)
-    return jnp.where(
-        iota(shape, 1) < 64,
-        jnp.broadcast_to(here[:, 2 * p : 2 * p + 1], shape),
-        jnp.broadcast_to(here[:, 2 * p + 1 : 2 * p + 2], shape),
-    )
+def parts_of(value, count):
+    group = iota(value.shape, 1) >> 3
+    out = jnp.zeros(value.shape, f32)
+    for n in range(count):
+        part = value.astype(bf16).astype(f32)
+        out = jnp.where(group == n, part, out)
+        value = value - part
+    return out.astype(bf16)
+
+
+def spread_all(count, width):
+    q, c = iota((128, width), 0), iota((128, width), 1)
+    return ones_where((q < 8 * count) & ((q & 7) == (c >> 6)))
 
 
 def pack_events(
@@ -170,7 +175,7 @@
     message[:, per : per + 8, :] = extra.astype(bf16)
 
 
-def pack_grads(info, spots, grads, message, back, scratch, narrow, turned, sems):
+def pack_grads(info, spots, grads, message, back, expand, mine, scratch, narrow, turned, sems):
     rows, width = grads.shape
     slots = turned.shape[1]
     place = ones_where(iota((slots, rows), 0) == spots[1:2, :])
@@ -180,6 +185,13 @@
     same = ones_where(iota((rows, rows), 0) == iota((rows, rows), 1))
     turned[...] = dot(same, place, NT).astype(bf16)
     copies.append(fetched(turned, back, sems.at[1]))
+    cap = slots * 8 // expand.shape[1]
+    r, c = iota(expand.shape, 0), iota(expand.shape, 1)
+    expand[...] = ones_where(((c & 7) == 0) & (8 * r >= cap * c) & (8 * r < cap * (c + 8)))
+    row, lane = iota(mine.shape, 0).astype(f32), iota(mine.shape, 1).astype(f32)
+    s = row - cap * jnp.floor((row + 0.5) * (1.0 / cap))
+    hit = (lane == s) | (lane == s + cap) | (lane == s + 2 * cap) | (lane == s + 3 * cap)
+    mine[...] = ones_where(hit)
     for copy in copies:
         copy.wait()
 
@@ -292,8 +304,8 @@
 
 
 def forward_state(
-    info, rates, message_in, weights,
-    x_out, keys, values, keys_out, values_out, fade, fade_t, marks, send,
+    info, rates, message_in, weights, expand, own_lanes,
+    x_out, keys, values, keys_out, values_out, fade, fade_t, marks, fall, send,
     scratch, memory, message, mine, x, sems,
 ):
     arrival = fetched(message_in, message, sems.at[0])
@@ -309,67 +321,61 @@
         x[:, 128 * j : 128 * (j + 1)] = part.astype(bf16)
     stores = [fetched(x, x_out, sems.at[2])]
     times = message[:, per : per + 8, :].astype(f32).reshape(owners * 8, 128).astype(bf16)
-    r = iota((slots, owners * 8), 0)
-    c = iota((slots, owners * 8), 1)
-    expand = ones_where(((c & 7) == 0) & (8 * r >= cap * c) & (8 * r < cap * (c + 8)))
-    wide = dot(expand, times)
-    row = iota((slots, 128), 0).astype(f32)
-    lane = iota((slots, 128), 1).astype(f32)
-    s = row - cap * jnp.floor((row + 0.5) * (1.0 / cap))
-    hit = (lane == s) | (lane == s + cap) | (lane == s + 2 * cap) | (lane == s + 3 * cap)
-    own = jnp.where(hit, wide, 0.0).astype(bf16)
-    tri = ones_where(iota((slots, slots), 0) >= iota((slots, slots), 1))
-    running = dot(tri, own)
-    kind = iota((128, 128), 0)
-    head = iota((128, 128), 1)
-    kind_t = iota((8, 128), 1)
-    head_t = iota((8, 128), 0)
+    own = dot(expand[...], times).astype(bf16) * own_lanes[...]
+    kind, head = iota((128, 128), 0), iota((128, 128), 1) & 7
     rate = jnp.zeros((128, 128), f32)
-    rate_t = jnp.zeros((8, 128), f32)
     for h in range(rates.shape[1]):
-        value = rates[info[0], h]
-        rate = jnp.where(head == h, value, rate)
-        rate_t = jnp.where(head_t == h, value, rate_t)
+        rate = jnp.where(head == h, rates[info[0], h], rate)
     to_heads = jnp.where(kind < 2 * cap, -rate, jnp.where(kind < 4 * cap, -1.0, 0.0))
-    fade[...] = dot(running, to_heads, NN, EXACT)
-    to_heads = jnp.where(kind_t < 2 * cap, -rate_t, jnp.where(kind_t < 4 * cap, -1.0, 0.0))
-    turned = dot(to_heads, running, NT, EXACT)
+    tri = ones_where(iota((CH, CH), 0) >= iota((CH, CH), 1))
+    before = jnp.zeros((1, 128), f32)
+    start = jnp.zeros((1, 128), f32)
+    ends = []
     for j in range(blocks):
-        fade_t[j] = turned[:, CH * j : CH * (j + 1)]
+        running = dot(tri, own[CH * j : CH * (j + 1), :]) + before
+        before = running[CH - 1 : CH, :]
+        here = dot(running, to_heads, NN, EXACT)
+        fade[CH * j : CH * (j + 1), :] = here
+        fade_t[j] = here.T[0:8, :]
+        start = here[CH - 1 : CH, :]
+        ends.append(start)
+    ends = jnp.concatenate(ends + [jnp.zeros((8 - blocks, 128), f32)], axis=0)
+    wide_ends = dot(parts_of(ends, 3), spread_all(3, width))
     for j in range(blocks):
         for p in range(pairs):
+            cols = slice(128 * p, 128 * (p + 1))
+            marks[j, pairs + p : pairs + p + 1, :] = wide_ends[j : j + 1, cols]
             if j == 0:
                 marks[j, p : p + 1, :] = jnp.zeros((1, 128), f32)
             else:
-                marks[j, p : p + 1, :] = expanded(fade, slice(CH * j - 1, CH * j), p)
-            end = slice(CH * j + CH - 1, CH * j + CH)
-            marks[j, pairs + p : pairs + p + 1, :] = expanded(fade, end, p)
+                marks[j, p : p + 1, :] = wide_ends[j - 1 : j, cols]
+    fall[...] = parts_of(jnp.exp(start - fade[...]), 2)
     fetch.wait()
     mask = block_mask()
     for n in range(0, width, WIDE):
         cols = slice(n, n + WIDE)
         keys[:, cols] = dot(x[...], mine[0, :, cols]).astype(bf16)
         values[:, cols] = dot(x[...], mine[1, :, cols]).astype(bf16)
-    every = slice(0, slots)
+    hot = spread_all(2, width)
     for p in range(pairs):
         cols = slice(128 * p, 128 * (p + 1))
-        end = marks[blocks - 1, pairs + p : pairs + p + 1, :]
-        kf = (keys[:, cols].astype(f32) * jnp.exp(end - expanded(fade, every, p))).astype(bf16)
+        kf = (keys[:, cols].astype(f32) * dot(fall[...], hot[:, cols])).astype(bf16)
         memory[p] = jnp.where(mask, dot(kf, values[:, cols], TN), 0.0)
     stores.append(fetched(keys, keys_out, sems.at[3]))
     stores.append(fetched(values, values_out, sems.at[4]))
-    write_state(send, memory, turned[:, slots - 1 : slots], pairs)
+    write_state(send, memory, fade_t[blocks - 1][:, CH - 1 : CH], pairs)
     for store in stores:
         store.wait()
 
 
 def attend(
     info, x_in, weights, keys, values, fade, fade_t, marks,
-    q8, attended_out, states,
+    q8, attended_out, states, lift,
     memory, attended, x, mine, in_sems, sems,
 ):
     arrival = fetched(x_in, x, in_sems.at[0])
     fetch = fetched(weights.at[info[0], 0], mine, in_sems.at[1])
+    lift[...] = parts_of(jnp.exp(fade[...]), 2)
     arrival.wait()
     fetch.wait()
     for n in range(0, x.shape[1], WIDE):
@@ -402,12 +408,12 @@
         rows_copy(attended, attended_out, sems, j).start()
         return carry
 
-    lax.fori_loop(0, slots // CH, block, 0)
+    lax.fori_loop(0, slots // CH, block, 0, unroll=True)
     for j in range(slots // CH):
         rows_copy(attended, attended_out, sems, j).wait()
 
 
-def turn(info, q8, fade, fade_t, attended_in, x_in, weights, message_in, partner, *rest):
+def turn(info, q8, lift, fade_t, attended_in, x_in, weights, message_in, partner, *rest):
     received = rest[:-20]
     (
         encoded, grads_out, grad_full, incoming, send,
@@ -435,13 +441,16 @@
         grad_normed[:, cols] = dot(grads[...], mine[cols, :], NT).astype(bf16)
     attended_here.wait()
 
+    hot = spread_all(2, width)
+
     def block(j, carry):
         rows = pl.ds(pl.multiple_of(j * CH, CH), CH)
+        factors = dot(lift[rows, :], hot)
         values = []
         square = jnp.zeros((CH, 1), f32)
         for p in range(pairs):
             cols = slice(128 * p, 128 * (p + 1))
-            lifted = (q8[rows, cols].astype(f32) * jnp.exp(expanded(fade, rows, p))).astype(bf16)
+            lifted = (q8[rows, cols].astype(f32) * factors[:, cols]).astype(bf16)
             lifts[rows, cols] = lifted
             value = attended[rows, cols] + dot(lifted, states[p])
             values.append(value)
@@ -454,7 +463,7 @@
         grad_full[rows, :] = (scale * grad - here * (scale * scale * scale * along)).astype(bf16)
         return carry
 
-    lax.fori_loop(0, blocks, block, 0)
+    lax.fori_loop(0, blocks, block, 0, unroll=True)
     for p in range(pairs):
         cols = slice(128 * p, 128 * (p + 1))
         memory[p] = jnp.where(mask, dot(lifts[:, cols], grad_full[:, cols], TN), 0.0)
@@ -475,8 +484,8 @@
 
 
 def backward_local(
-    info, q8, keys_in, values_in, fade, fade_t, marks, grad_full, states, incoming, grads_in,
-    weights,
+    info, q8, keys_in, values_in, fade, fade_t, marks, grad_full, states, incoming,
+    grads_in, weights,
     grad_keys, grad_values, partial,
     memory, grad_q, grads, mine, keys, values, sems, key_sems, value_sems,
 ):
@@ -526,7 +535,7 @@
             memory[p] = jnp.exp(end - start) * now + jnp.where(mask, dot(lifted, da, TN), 0.0)
         return carry
 
-    lax.fori_loop(0, blocks, block, 0)
+    lax.fori_loop(0, blocks, block, 0, unroll=True)
     arrival.wait()
     fetch.wait()
     for n in range(0, width, WIDE):
@@ -535,7 +544,7 @@
 
 
 def backward_finish(
-    info, partial, grad_keys, grad_values, keys_in, values_in, fade, marks, weights, partner, *rest
+    info, partial, grad_keys, grad_values, keys_in, values_in, fall, weights, partner, *rest
 ):
     received = rest[:-12]
     out, mine, wide, narrow, states, gk, gv, total, keys, values, sems, out_sems = rest[-12:]
@@ -549,16 +558,15 @@
     arrived = gathered_state((1 - info[1]).astype(f32), partner, received, pairs)
     for p, state in enumerate(arrived):
         states[p] = unfolded(state, mask).astype(bf16)
-    every = slice(0, slots)
+    hot = spread_all(2, width)
     keys_here.wait()
     values_here.wait()
     for p in range(pairs):
         cols = slice(128 * p, 128 * (p + 1))
-        end = marks[blocks - 1, pairs + p : pairs + p + 1, :]
-        fall = jnp.exp(end - expanded(fade, every, p))
-        kf = (keys[:, cols].astype(f32) * fall).astype(bf16)
+        factor = dot(fall[...], hot[:, cols])
+        kf = (keys[:, cols].astype(f32) * factor).astype(bf16)
         state = states[p]
-        gk[:, cols] = (grad_keys[:, cols] + fall * dot(values[:, cols], state, NT)).astype(bf16)
+        gk[:, cols] = (grad_keys[:, cols] + factor * dot(values[:, cols], state, NT)).astype(bf16)
         gv[:, cols] = (grad_values[:, cols] + dot(kf, state)).astype(bf16)
     fetch.wait()
     for n in range(0, width, WIDE):
@@ -633,9 +641,11 @@
     )
     events_in = regroup(message)
     flat_msg = ((slots * pairs, 128), bf16)
-    message, back = call(
+    message, back, expand, own_lanes = call(
         pack_grads,
-        [flat_msg, ((rows, slots), bf16)],
+        [
+            flat_msg, ((rows, slots), bf16), ((slots, owners * 8), bf16), ((slots, 128), bf16),
+        ],
         [info, spots, cotangent.reshape(rows, width)],
         [flat, pltpu.VMEM(*flat_msg), pltpu.VMEM((rows, slots), bf16), sem((2,))],
         {0: SMEM},
@@ -649,13 +659,13 @@
     flat_narrow = pltpu.VMEM(*flat_msg)
     rows16, rows32 = pltpu.VMEM(*wide16), pltpu.VMEM(*wide32)
     narrow_states = pltpu.VMEM((pairs, 128, 128), bf16)
-    x, keys, values, keys_far, values_far, fade, fade_t, marks, send = call(
+    x, keys, values, keys_far, values_far, fade, fade_t, marks, fall, send = call(
         forward_state,
         [
             wide16, wide16, wide16, wide16, wide16, ((slots, 128), f32), ((blocks, 8, 128), f32),
-            ((blocks, 2 * pairs, 128), f32), state_msg,
-        ],
-        [info, decay_rates, events_in, weights],
+            ((blocks, 2 * pairs, 128), f32), ((slots, 128), bf16), state_msg,
+        ],
+        [info, decay_rates, events_in, weights, expand, own_lanes],
         [flat, state_vmem, pltpu.VMEM((owners, per + 8, 128), bf16), two, rows16, sem((5,))],
         {0: SMEM, 1: SMEM, 2: HBM, 3: HBM},
         (0, 3, 4),
@@ -663,9 +673,9 @@
     partner = swapped(send, "ctx")
     (joined,) = call(join_ahead, [state_msg], [info, send, partner], (), {0: SMEM})
     received = exchange(joined, "ctx", 1)
-    q8, attended, kept = call(
+    q8, attended, kept, lift = call(
         attend,
-        [wide16, wide32, ((blocks, pairs, 64, 128), bf16)],
+        [wide16, wide32, ((blocks, pairs, 64, 128), bf16), ((slots, 128), bf16)],
         [info, x, weights, keys, values, fade, fade_t, marks],
         [state_vmem, rows32, rows16, one, sem((2,)), sem((blocks,))],
         {0: SMEM, 1: HBM, 2: HBM},
@@ -674,7 +684,7 @@
     message, grads, grad_full, incoming, send = call(
         turn,
         [flat_msg, wide16, wide16, half_states, state_msg],
-        [info, q8, fade, fade_t, attended, x, weights, grads_in, partner, *received],
+        [info, q8, lift, fade_t, attended, x, weights, grads_in, partner, *received],
         [
             flat, pltpu.VMEM((owners, per, 128), bf16), one, rows16, rows32, rows16, rows16, rows16,
             rows16, block_wide, flat_narrow, narrow_states, state_vmem, sem((5,)), sem((blocks,)),
@@ -703,14 +713,14 @@
         backward_finish,
         [flat_msg],
         [
-            info, partial, grad_keys, grad_values, keys_far, values_far, fade, marks, weights,
-            partner, *received,
+            info, partial, grad_keys, grad_values, keys_far, values_far, fall, weights, partner,
+            *received,
         ],
         [
             two, block_wide, flat_narrow, narrow_states,
             rows16, rows16, rows32, rows16, rows16, sem((3,)), sem((blocks,)),
         ],
-        {0: SMEM, 4: HBM, 5: HBM, 8: HBM},
+        {0: SMEM, 4: HBM, 5: HBM, 7: HBM},
         (0,),
     )
     grad_in = regroup(message.reshape(owners, per, 128))

time: 139 us -> 136 us (0.978)
  Pallas kernels: 44.6 us -> 41.2 us
    pallas_call x11, Pallas kernels: 44.6 us -> 41.2 us  [call(): pl.pallas_call(body, out_shape=[pltpu.HBM(s, d) if i in out_hbm else jax....]
  transfers between devices with their start and end apart: 12 -> 12, of which waited for: 6 -> 5; matrix products, arithmetic and copies ran while one was open for 0% -> 0% of each run, Pallas kernels for 23% -> 23%
where the time goes in v3:
time: 136 us; the launch traced here: 135 us
  starting transfers between devices  51.1 us (38%)
  Pallas kernels  41.2 us (30%)
  waiting for transfers between devices  41.2 us (30%)
    pallas_call x11, Pallas kernels, call(): pl.pallas_call(body, out_shape=[pltpu.HBM(s, d) if i in out_hbm else jax....  41.2 us
    all_to_all x4, waiting for transfers between devices, regroup(): return lax.all_to_all(value, 'log', split_axis=0, concat_axis=0, tiled=True)  38.7 us
    all_to_all x4, starting transfers between devices, regroup(): return lax.all_to_all(value, 'log', split_axis=0, concat_axis=0, tiled=True)  35.8 us
    ppermute x6, starting transfers between devices, exchange(): lax.ppermute(value, axis, [(i, i + sign * k) for i in range(count) if 0 <...  15.1 us
  transfers between devices with their start and end apart: 12, of which 5 were waited for; matrix products, arithmetic and copies ran while one was open for 0% of the time, Pallas kernels for 23%

profile of v3, /device:TPU:24, one launch (start us, length us, event | category | flops | bytes accessed | tf_op | source)
XLA Modules:
  0.0 135.3 jit_solution(3357398819758840625)
XLA Ops:
  0.6 3.2 %shard_map.86 = (bf16[32,88,128]{2,1,0:T(8,128)(2,1)}, s32[2,512]{1,0:T(2,128)S(1)}) custom-call(s32[1,512]{1,0:T(1,128)} %bitcast.19, bf16[512,512]{1,0:T(8,128)(2,1)} %bitcast.18, f32[1,512]{1,0:T(1,128)} %bitcast.20, f32[1,512]{1,0:T(1,128)} %bitcast.21), custom_call_target="tpu_custom_call" | custom-call | tf_op jit(solution)/shard_map/pallas_call | solution.py:43
  3.9 11.3 %all-to-all-start = ((bf16[32,88,128]{2,1,0:T(8,128)(2,1)}), bf16[32,88,128]{2,1,0:T(8,128)(2,1)S(1)}, u32[]{:S(2)}, u32[]{:S(2)}) async-start(bf16[32,88,128]{2,1,0:T(8,128)(2,1)} %get-tuple-element.32), calls=%async_computation | async-start | bytes 1441792 | tf_op jit(solution)/shard_map/all_to_all | solution.py:602
  15.3 3.0 %shard_map.87 = (bf16[2560,128]{1,0:T(8,128)(2,1)}, bf16[512,640]{1,0:T(8,128)(2,1)}, bf16[640,256]{1,0:T(8,128)(2,1)S(1)}, bf16[640,128]{1,0:T(8,128)(2,1)S(1)}) custom-call(s32[2]{0:T(128)S(1)} %pad_add_fusion.info, s32[2,512]{1,0:T(2,128)S(1)} %get-tuple-element.30.spots, bf16[512,512]{1,0:T(8,128)(2,1)S(1)} %bitcast.12), custom_call_target="tpu_custom_call" | custom-call | tf_op jit(solution)/shard_map/pallas_call | solution.py:43
  18.3 18.5 %all-to-all-done.message_in = bf16[32,88,128]{2,1,0:T(8,128)(2,1)S(1)} async-done(((bf16[32,88,128]{2,1,0:T(8,128)(2,1)}), bf16[32,88,128]{2,1,0:T(8,128)(2,1)S(1)}, u32[]{:S(2)}, u32[]{:S(2)}) %all-to-all-start) | async-done | bytes 720928 | tf_op jit(solution)/shard_map/all_to_all | solution.py:602
  37.7 5.0 %all-to-all-start.1 = ((bf16[32,80,128]{2,1,0:T(8,128)(2,1)}), bf16[32,80,128]{2,1,0:T(8,128)(2,1)S(1)}, u32[]{:S(2)}, u32[]{:S(2)}) async-start(bf16[32,80,128]{2,1,0:T(8,128)(2,1)} %bitcast.15), calls=%async_computation.1 | async-start | bytes 1310720 | tf_op jit(solution)/shard_map/all_to_all | solution.py:602
  42.7 5.0 %shard_map.88 = (bf16[640,512]{1,0:T(8,128)(2,1)}, bf16[640,512]{1,0:T(8,128)(2,1)S(1)}, bf16[640,512]{1,0:T(8,128)(2,1)S(1)}, bf16[640,512]{1,0:T(8,128)(2,1)},...) custom-call(s32[2]{0:T(128)S(1)} %pad_add_fusion.info, ...), custom_call_target="tpu_custom_call" | custom-call | tf_op jit(solution)/shard_map/pallas_call | solution.py:43
  47.8 1.2 collective-permute-done.other.partner
  49.8 1.3 collective-permute-start.1
  51.1 1.3 collective-permute-start.2
  52.4 1.5 %collective-permute-start.3 = (bf16[264,128]{1,0:T(8,128)(2,1)S(1)}, bf16[264,128]{1,0:T(8,128)(2,1)S(1)}, u32[]{:S(2)}, u32[]{:S(2)}) collective-permute-start(bf16[264,128]{1,0:T(8,128)(2,1)S(1)} %shard_map.90), channel_id=1, source_target_pairs={{0,6},{1,7},{8,14},{9,15},{16,22},{17,23},{24,30},{25,31},{32,38},... | collective-permute-start | bytes 202760 | tf_op jit(solution)/shard_map/ppermute | solution.py:594
  53.9 6.3 %shard_map.89 = (bf16[640,512]{1,0:T(8,128)(2,1)S(1)}, f32[640,512]{1,0:T(8,128)}, bf16[5,4,64,128]{3,2,1,0:T(8,128)(2,1)S(1)}, bf16[640,128]{1,0:T(8,128)(2,1)S(1)}) custom-call(s32[2]{0:T(128)S(1)} %pad_add_fusion.info, bf16[640,512]{1,0:T(8,128)(2,1)} %get-tuple-element.35.x_in, bf16[4,4,512,512]{3,2,1,0:T(8,128)(2,1)} %weights.9, ...), custom_call_target="tpu_custom_call" | custom-call | tf_op jit(solution)/shard_map/pallas_call | solution.py:43
  60.1 1.9 %all-to-all-done.1.message_in = bf16[32,80,128]{2,1,0:T(8,128)(2,1)S(1)} async-done(((bf16[32,80,128]{2,1,0:T(8,128)(2,1)}), bf16[32,80,128]{2,1,0:T(8,128)(2,1)S(1)}, u32[]{:S(2)}, u32[]{:S(2)}) %all-to-all-start.1) | async-done | bytes 655392 | tf_op jit(solution)/shard_map/all_to_all | solution.py:602
  62.0 5.7 %shard_map.91 = (bf16[2560,128]{1,0:T(8,128)(2,1)}, bf16[640,512]{1,0:T(8,128)(2,1)}, bf16[640,512]{1,0:T(8,128)(2,1)S(1)}, f32[4,64,128]{2,1,0:T(8,128)S(1)}, bf16[264,128]{1,0:T(8,128)(2,1)S(1)}) custom-call(s32[2]{0:T(128)S(1)} %pad_add_fusion.info, bf16[640,512]{1,0:T(8,128)(2,1)S(1)} %get-tuple-element.41.q8, ...), custom_call_target="tpu_custom_call" | custom-call | tf_op jit(solution)/shard_map/pallas_call | solution.py:43
  67.8 9.6 %all-to-all-start.2 = ((bf16[32,80,128]{2,1,0:T(8,128)(2,1)}), bf16[32,80,128]{2,1,0:T(8,128)(2,1)S(1)}, u32[]{:S(2)}, u32[]{:S(2)}) async-start(bf16[32,80,128]{2,1,0:T(8,128)(2,1)} %bitcast.14), calls=%async_computation.2 | async-start | bytes 1310720 | tf_op jit(solution)/shard_map/all_to_all | solution.py:602
  77.5 1.2 collective-permute-done.4.other.partner
  79.4 2.2 %collective-permute-start.5 = (bf16[264,128]{1,0:T(8,128)(2,1)S(1)}, bf16[264,128]{1,0:T(8,128)(2,1)S(1)}, u32[]{:S(2)}, u32[]{:S(2)}) collective-permute-start(bf16[264,128]{1,0:T(8,128)(2,1)S(1)} %shard_map.94), channel_id=1, source_target_pairs={{2,0},{3,1},{4,2},{5,3},{6,4},{7,5},{10,8},{11,9},{12,10},{13,11},... | collective-permute-start | bytes 202760 | tf_op jit(solution)/shard_map/ppermute | solution.py:594
  81.7 7.3 %collective-permute-start.6 = (bf16[264,128]{1,0:T(8,128)(2,1)S(1)}, bf16[264,128]{1,0:T(8,128)(2,1)S(1)}, u32[]{:S(2)}, u32[]{:S(2)}) collective-permute-start(bf16[264,128]{1,0:T(8,128)(2,1)S(1)} %shard_map.94), channel_id=1, source_target_pairs={{4,0},{5,1},{6,2},{7,3},{12,8},{13,9},{14,10},{15,11},{20,16},{21,... | collective-permute-start | bytes 202760 | tf_op jit(solution)/shard_map/ppermute | solution.py:594
  89.0 1.5 %collective-permute-start.7 = (bf16[264,128]{1,0:T(8,128)(2,1)S(1)}, bf16[264,128]{1,0:T(8,128)(2,1)S(1)}, u32[]{:S(2)}, u32[]{:S(2)}) collective-permute-start(bf16[264,128]{1,0:T(8,128)(2,1)S(1)} %shard_map.94), channel_id=1, source_target_pairs={{6,0},{7,1},{14,8},{15,9},{22,16},{23,17},{30,24},{31,25},{38,32},... | collective-permute-start | bytes 202760 | tf_op jit(solution)/shard_map/ppermute | solution.py:594
  90.5 8.7 %shard_map.93 = (f32[640,512]{1,0:T(8,128)S(1)}, f32[640,512]{1,0:T(8,128)S(1)}, f32[640,512]{1,0:T(8,128)S(1)}) custom-call(s32[2]{0:T(128)S(1)} %pad_add_fusion.info, bf16[640,512]{1,0:T(8,128)(2,1)S(1)} %get-tuple-element.41.q8, bf16[640,512]{1,0:T(8,128)(2,1)} %get-tuple-element.47.keys_in, bf16[640,512]{1,0:T(8,128)(2,1)} %get-tuple-element.48.values_in, ...), custom_call_target="tpu_custom_call" | custom-call | tf_op jit(solution)/shard_map/pallas_call | solution.py:43
  99.2 4.4 %shard_map.95 = bf16[2560,128]{1,0:T(8,128)(2,1)} custom-call(s32[2]{0:T(128)S(1)} %pad_add_fusion.info, f32[640,512]{1,0:T(8,128)S(1)} %get-tuple-element.53.partial, f32[640,512]{1,0:T(8,128)S(1)} %get-tuple-element.54.grad_keys, f32[640,512]{1,0:T(8,128)S(1)} %get-tuple-element.55.grad_values, bf16[640,512]{1,0:T(8,128)(2,1)} %get-tuple-element.47.keys_in, ...), custom_call_target="tpu_custom_call" | custom-call | tf_op jit(solution)/shard_map/pallas_call | solution.py:43
  103.7 9.9 %all-to-all-start.3 = ((bf16[32,80,128]{2,1,0:T(8,128)(2,1)}), bf16[32,80,128]{2,1,0:T(8,128)(2,1)S(1)}, u32[]{:S(2)}, u32[]{:S(2)}) async-start(bf16[32,80,128]{2,1,0:T(8,128)(2,1)} %bitcast.13), calls=%async_computation.3 | async-start | bytes 1310720 | tf_op jit(solution)/shard_map/all_to_all | solution.py:602
  113.6 1.7 %shard_map.92 = bf16[512,512]{1,0:T(8,128)(2,1)} custom-call(bf16[512,640]{1,0:T(8,128)(2,1)S(1)} %copy-done, bf16[32,80,128]{2,1,0:T(8,128)(2,1)S(1)} %all-to-all-done.2.message), custom_call_target="tpu_custom_call" | custom-call | tf_op jit(solution)/shard_map/pallas_call | solution.py:43
  115.3 18.3 %all-to-all-done.3.message = bf16[32,80,128]{2,1,0:T(8,128)(2,1)S(1)} async-done(((bf16[32,80,128]{2,1,0:T(8,128)(2,1)}), bf16[32,80,128]{2,1,0:T(8,128)(2,1)S(1)}, u32[]{:S(2)}, u32[]{:S(2)}) %all-to-all-start.3) | async-done | bytes 655392 | tf_op jit(solution)/shard_map/all_to_all | solution.py:602
  133.6 1.7 %shard_map.96 = bf16[512,512]{1,0:T(8,128)(2,1)} custom-call(bf16[512,640]{1,0:T(8,128)(2,1)S(1)} %copy-done, bf16[32,80,128]{2,1,0:T(8,128)(2,1)S(1)} %all-to-all-done.3.message), custom_call_target="tpu_custom_call" | custom-call | tf_op jit(solution)/shard_map/pallas_call | solution.py:43
  (20 shorter events, 2.6 us)
Async XLA Ops:
  0.6 14.7 %copy-start.1 = (bf16[1,1,512,512]{3,2,1,0:T(8,128)(2,1)S(1)}, bf16[1,1,512,512]{3,2,1,0:T(8,128)(2,1)}, u32[]{:S(2)}) copy-start(bf16[1,1,512,512]{3,2,1,0:T(8,128)(2,1)} %param.13) | copy-start | bytes 1572868
  3.9 33.0 %all-to-all-start = ((bf16[32,88,128]{2,1,0:T(8,128)(2,1)}), bf16[32,88,128]{2,1,0:T(8,128)(2,1)S(1)}, u32[]{:S(2)}, u32[]{:S(2)}) async-start(bf16[32,88,128]{2,1,0:T(8,128)(2,1)} %get-tuple-element.32), calls=%async_computation | async-start | bytes 1441792 | tf_op jit(solution)/shard_map/all_to_all | solution.py:602
  15.2 27.5 %copy-start.2 = (f32[4,8]{1,0:T(4,128)S(1)}, f32[4,8]{1,0:T(4,128)}, u32[]{:S(2)}) copy-start(f32[4,8]{1,0:T(4,128)} %rates.1) | copy-start | bytes 388
  36.8 0.9 copy-start.3
  37.7 24.3 %all-to-all-start.1 = ((bf16[32,80,128]{2,1,0:T(8,128)(2,1)}), bf16[32,80,128]{2,1,0:T(8,128)(2,1)S(1)}, u32[]{:S(2)}, u32[]{:S(2)}) async-start(bf16[32,80,128]{2,1,0:T(8,128)(2,1)} %bitcast.15), calls=%async_computation.1 | async-start | bytes 1310720 | tf_op jit(solution)/shard_map/all_to_all | solution.py:602
  47.7 1.3 collective-permute-start
  49.8 12.2 %collective-permute-start.1 = (bf16[264,128]{1,0:T(8,128)(2,1)S(1)}, bf16[264,128]{1,0:T(8,128)(2,1)S(1)}, u32[]{:S(2)}, u32[]{:S(2)}) collective-permute-start(bf16[264,128]{1,0:T(8,128)(2,1)S(1)} %shard_map.90), channel_id=1, source_target_pairs={{0,2},{1,3},{2,4},{3,5},{4,6},{5,7},{8,10},{9,11},{10,12},{11,13},... | collective-permute-start | bytes 202760 | tf_op jit(solution)/shard_map/ppermute | solution.py:594
  51.1 10.9 %collective-permute-start.2 = (bf16[264,128]{1,0:T(8,128)(2,1)S(1)}, bf16[264,128]{1,0:T(8,128)(2,1)S(1)}, u32[]{:S(2)}, u32[]{:S(2)}) collective-permute-start(bf16[264,128]{1,0:T(8,128)(2,1)S(1)} %shard_map.90), channel_id=1, source_target_pairs={{0,4},{1,5},{2,6},{3,7},{8,12},{9,13},{10,14},{11,15},{16,20},{17,... | collective-permute-start | bytes 202760 | tf_op jit(solution)/shard_map/ppermute | solution.py:594
  52.4 9.6 %collective-permute-start.3 = (bf16[264,128]{1,0:T(8,128)(2,1)S(1)}, bf16[264,128]{1,0:T(8,128)(2,1)S(1)}, u32[]{:S(2)}, u32[]{:S(2)}) collective-permute-start(bf16[264,128]{1,0:T(8,128)(2,1)S(1)} %shard_map.90), channel_id=1, source_target_pairs={{0,6},{1,7},{8,14},{9,15},{16,22},{17,23},{24,30},{25,31},{32,38},... | collective-permute-start | bytes 202760 | tf_op jit(solution)/shard_map/ppermute | solution.py:594
  67.8 35.9 %all-to-all-start.2 = ((bf16[32,80,128]{2,1,0:T(8,128)(2,1)}), bf16[32,80,128]{2,1,0:T(8,128)(2,1)S(1)}, u32[]{:S(2)}, u32[]{:S(2)}) async-start(bf16[32,80,128]{2,1,0:T(8,128)(2,1)} %bitcast.14), calls=%async_computation.2 | async-start | bytes 1310720 | tf_op jit(solution)/shard_map/all_to_all | solution.py:602
  77.4 1.3 collective-permute-start.4
  79.4 19.8 %collective-permute-start.5 = (bf16[264,128]{1,0:T(8,128)(2,1)S(1)}, bf16[264,128]{1,0:T(8,128)(2,1)S(1)}, u32[]{:S(2)}, u32[]{:S(2)}) collective-permute-start(bf16[264,128]{1,0:T(8,128)(2,1)S(1)} %shard_map.94), channel_id=1, source_target_pairs={{2,0},{3,1},{4,2},{5,3},{6,4},{7,5},{10,8},{11,9},{12,10},{13,11},... | collective-permute-start | bytes 202760 | tf_op jit(solution)/shard_map/ppermute | solution.py:594
  81.7 17.5 %collective-permute-start.6 = (bf16[264,128]{1,0:T(8,128)(2,1)S(1)}, bf16[264,128]{1,0:T(8,128)(2,1)S(1)}, u32[]{:S(2)}, u32[]{:S(2)}) collective-permute-start(bf16[264,128]{1,0:T(8,128)(2,1)S(1)} %shard_map.94), channel_id=1, source_target_pairs={{4,0},{5,1},{6,2},{7,3},{12,8},{13,9},{14,10},{15,11},{20,16},{21,... | collective-permute-start | bytes 202760 | tf_op jit(solution)/shard_map/ppermute | solution.py:594
  89.0 10.2 %collective-permute-start.7 = (bf16[264,128]{1,0:T(8,128)(2,1)S(1)}, bf16[264,128]{1,0:T(8,128)(2,1)S(1)}, u32[]{:S(2)}, u32[]{:S(2)}) collective-permute-start(bf16[264,128]{1,0:T(8,128)(2,1)S(1)} %shard_map.94), channel_id=1, source_target_pairs={{6,0},{7,1},{14,8},{15,9},{22,16},{23,17},{30,24},{31,25},{38,32},... | collective-permute-start | bytes 202760 | tf_op jit(solution)/shard_map/ppermute | solution.py:594
  103.7 9.9 %copy-start = (bf16[512,640]{1,0:T(8,128)(2,1)S(1)}, bf16[512,640]{1,0:T(8,128)(2,1)}, u32[]{:S(2)}) copy-start(bf16[512,640]{1,0:T(8,128)(2,1)} %get-tuple-element.31.back) | copy-start | bytes 1966084
  103.7 29.9 %all-to-all-start.3 = ((bf16[32,80,128]{2,1,0:T(8,128)(2,1)}), bf16[32,80,128]{2,1,0:T(8,128)(2,1)S(1)}, u32[]{:S(2)}, u32[]{:S(2)}) async-start(bf16[32,80,128]{2,1,0:T(8,128)(2,1)} %bitcast.13), calls=%async_computation.3 | async-start | bytes 1310720 | tf_op jit(solution)/shard_map/all_to_all | solution.py:602

commit v4 on v3

--- a/solution.py
+++ b/solution.py
@@ -32,7 +32,6 @@
 VMEM = pl.BlockSpec(memory_space=pltpu.VMEM)
 SMEM = pl.BlockSpec(memory_space=pltpu.SMEM)
 HBM = pl.BlockSpec(memory_space=pltpu.HBM)
-ANY = pl.BlockSpec(memory_space=pl.ANY)
 
 
 def call(body, outs, ins, scratch=(), spaces=None, out_hbm=()):
@@ -53,14 +52,16 @@
     )(*ins)
 
 
-def write_rows(scratch, rows_of, parts):
+def write_rows(scratch, tile_of, parts):
     count = scratch.shape[0] // parts
-    for j in range(parts):
-        scratch[pl.ds(j, count, stride=parts), :] = rows_of(j)
-
-
-def write_message(message, scratch, rows_of, width):
-    write_rows(scratch, rows_of, width // 128)
+    for j in range(0, parts, 2):
+        tile = tile_of(slice(128 * j, 128 * j + WIDE))
+        scratch[pl.ds(j, count, stride=parts), :] = tile[:, 0:128]
+        scratch[pl.ds(j + 1, count, stride=parts), :] = tile[:, 128:WIDE]
+
+
+def write_message(message, scratch, tile_of, width):
+    write_rows(scratch, tile_of, width // 128)
     owners = message.shape[0]
     per = scratch.shape[0] // owners
     message[:, 0:per, :] = scratch[...].reshape(owners, per, 128).astype(bf16)
@@ -158,7 +159,7 @@
     write_message(
         message,
         scratch,
-        lambda j: dot(place[...], events[:, 128 * j : 128 * (j + 1)]),
+        lambda cols: dot(place[...], events[:, cols]),
         width,
     )
     lanes = iota((128, rows), 0)
@@ -179,7 +180,7 @@
     rows, width = grads.shape
     slots = turned.shape[1]
     place = ones_where(iota((slots, rows), 0) == spots[1:2, :])
-    write_rows(scratch, lambda j: dot(place, grads[:, 128 * j : 128 * (j + 1)]), width // 128)
+    write_rows(scratch, lambda cols: dot(place, grads[:, cols]), width // 128)
     narrow[...] = scratch[...].astype(bf16)
     copies = [fetched(narrow, message, sems.at[0])]
     same = ones_where(iota((rows, rows), 0) == iota((rows, rows), 1))
@@ -198,8 +199,10 @@
 
 def unpack_rows(back, message, out, scratch):
     width = out.shape[1]
-    for j, part in enumerate(read_message(message, scratch, width)):
-        out[:, 128 * j : 128 * (j + 1)] = dot(back[...], part.astype(bf16)).astype(bf16)
+    parts = read_message(message, scratch, width)
+    for j in range(0, len(parts), 2):
+        both = jnp.concatenate([parts[j], parts[j + 1]], axis=1).astype(bf16)
+        out[:, 128 * j : 128 * j + WIDE] = dot(back[...], both).astype(bf16)
 
 
 def halves():
@@ -236,6 +239,21 @@
     return jnp.where(mask, jnp.concatenate([half, half], axis=0), 0.0)
 
 
+def set_states(states, arrived):
+    mask = block_mask()
+    none = jnp.zeros((128, 128), f32)
+    for n in range(states.shape[0]):
+        first = jnp.concatenate([unfolded(arrived[2 * n], mask), none], axis=1)
+        second = jnp.concatenate([none, unfolded(arrived[2 * n + 1], mask)], axis=1)
+        states[n] = jnp.concatenate([first, second], axis=0).astype(bf16)
+
+
+def set_memory(memory, both, n):
+    mask = block_mask()
+    memory[2 * n] = jnp.where(mask, both[0:128, 0:128], 0.0)
+    memory[2 * n + 1] = jnp.where(mask, both[128:WIDE, 128:WIDE], 0.0)
+
+
 def write_state(send, state, last, pairs):
     for p in range(pairs):
         send[64 * p : 64 * (p + 1), :] = folded(state[p]).astype(bf16)
@@ -304,11 +322,10 @@
 
 
 def forward_state(
-    info, rates, message_in, weights, expand, own_lanes,
+    info, rates, message, weights, expand, own_lanes,
     x_out, keys, values, keys_out, values_out, fade, fade_t, marks, fall, send,
-    scratch, memory, message, mine, x, sems,
+    scratch, memory, mine, x, sems,
 ):
-    arrival = fetched(message_in, message, sems.at[0])
     fetch = fetched(weights.at[info[0], pl.ds(1, 2)], mine, sems.at[1])
     slots, width = x.shape
     pairs = width // 128
@@ -316,7 +333,6 @@
     owners = message.shape[0]
     cap = slots // owners
     per = cap * pairs
-    arrival.wait()
     for j, part in enumerate(read_message(message, scratch, width)):
         x[:, 128 * j : 128 * (j + 1)] = part.astype(bf16)
     stores = [fetched(x, x_out, sems.at[2])]
@@ -351,16 +367,15 @@
                 marks[j, p : p + 1, :] = wide_ends[j - 1 : j, cols]
     fall[...] = parts_of(jnp.exp(start - fade[...]), 2)
     fetch.wait()
-    mask = block_mask()
     for n in range(0, width, WIDE):
         cols = slice(n, n + WIDE)
         keys[:, cols] = dot(x[...], mine[0, :, cols]).astype(bf16)
         values[:, cols] = dot(x[...], mine[1, :, cols]).astype(bf16)
     hot = spread_all(2, width)
-    for p in range(pairs):
-        cols = slice(128 * p, 128 * (p + 1))
+    for n in range(pairs // 2):
+        cols = slice(WIDE * n, WIDE * (n + 1))
         kf = (keys[:, cols].astype(f32) * dot(fall[...], hot[:, cols])).astype(bf16)
-        memory[p] = jnp.where(mask, dot(kf, values[:, cols], TN), 0.0)
+        set_memory(memory, dot(kf, values[:, cols], TN), n)
     stores.append(fetched(keys, keys_out, sems.at[3]))
     stores.append(fetched(values, values_out, sems.at[4]))
     write_state(send, memory, fade_t[blocks - 1][:, CH - 1 : CH], pairs)
@@ -413,25 +428,23 @@
         rows_copy(attended, attended_out, sems, j).wait()
 
 
-def turn(info, q8, lift, fade_t, attended_in, x_in, weights, message_in, partner, *rest):
-    received = rest[:-20]
+def turn(info, q8, lift, fade_t, attended_in, x_in, weights, message, partner, *rest):
+    received = rest[:-19]
     (
         encoded, grads_out, grad_full, incoming, send,
-        scratch, message, mine, x, attended, grads, grad_normed, normed, lifts,
+        scratch, mine, x, attended, grads, grad_normed, normed, lifts,
         wide, narrow, states, memory, sems, out_sems,
-    ) = rest[-20:]
-    arrival = fetched(message_in, message, sems.at[2])
+    ) = rest[-19:]
     fetch = fetched(weights.at[info[0], 3], mine, sems.at[0])
     rows_in = fetched(x_in, x, sems.at[1])
     attended_here = fetched(attended_in, attended, sems.at[3])
     slots, width = x.shape
     pairs = width // 128
     blocks = slots // CH
-    mask = block_mask()
-    for p, state in enumerate(gathered_state(info[1].astype(f32), partner, received, pairs)):
-        incoming[p] = state
-        states[p] = unfolded(state, mask).astype(bf16)
-    arrival.wait()
+    arrived = gathered_state(info[1].astype(f32), partner, received, pairs)
+    for p in range(pairs):
+        incoming[p] = arrived[p]
+    set_states(states, arrived)
     for j, part in enumerate(read_message(message, scratch, width)):
         grads[:, 128 * j : 128 * (j + 1)] = part.astype(bf16)
     store = fetched(grads, grads_out, sems.at[4])
@@ -448,11 +461,11 @@
         factors = dot(lift[rows, :], hot)
         values = []
         square = jnp.zeros((CH, 1), f32)
-        for p in range(pairs):
-            cols = slice(128 * p, 128 * (p + 1))
+        for n in range(pairs // 2):
+            cols = slice(WIDE * n, WIDE * (n + 1))
             lifted = (q8[rows, cols].astype(f32) * factors[:, cols]).astype(bf16)
             lifts[rows, cols] = lifted
-            value = attended[rows, cols] + dot(lifted, states[p])
+            value = attended[rows, cols] + dot(lifted, states[n])
             values.append(value)
             square += jnp.sum(value * value, axis=1, keepdims=True)
         here = jnp.concatenate(values, axis=1)
@@ -464,9 +477,9 @@
         return carry
 
     lax.fori_loop(0, blocks, block, 0, unroll=True)
-    for p in range(pairs):
-        cols = slice(128 * p, 128 * (p + 1))
-        memory[p] = jnp.where(mask, dot(lifts[:, cols], grad_full[:, cols], TN), 0.0)
+    for n in range(pairs // 2):
+        cols = slice(WIDE * n, WIDE * (n + 1))
+        set_memory(memory, dot(lifts[:, cols], grad_full[:, cols], TN), n)
     write_state(send, memory, fade_t[blocks - 1][:, CH - 1 : CH], pairs)
     rows_in.wait()
     for n in range(0, width, WIDE):
@@ -554,20 +567,16 @@
     slots, width = partial.shape
     pairs = width // 128
     blocks = slots // CH
-    mask = block_mask()
-    arrived = gathered_state((1 - info[1]).astype(f32), partner, received, pairs)
-    for p, state in enumerate(arrived):
-        states[p] = unfolded(state, mask).astype(bf16)
+    set_states(states, gathered_state((1 - info[1]).astype(f32), partner, received, pairs))
     hot = spread_all(2, width)
     keys_here.wait()
     values_here.wait()
-    for p in range(pairs):
-        cols = slice(128 * p, 128 * (p + 1))
+    for n in range(pairs // 2):
+        cols = slice(WIDE * n, WIDE * (n + 1))
         factor = dot(fall[...], hot[:, cols])
         kf = (keys[:, cols].astype(f32) * factor).astype(bf16)
-        state = states[p]
-        gk[:, cols] = (grad_keys[:, cols] + factor * dot(values[:, cols], state, NT)).astype(bf16)
-        gv[:, cols] = (grad_values[:, cols] + dot(kf, state)).astype(bf16)
+        gk[:, cols] = (grad_keys[:, cols] + factor * dot(values[:, cols], states[n], NT)).astype(bf16)
+        gv[:, cols] = (grad_values[:, cols] + dot(kf, states[n])).astype(bf16)
     fetch.wait()
     for n in range(0, width, WIDE):
         cols = slice(n, n + WIDE)
@@ -658,7 +667,7 @@
     block_wide = pltpu.VMEM((CH * pairs, 128), f32)
     flat_narrow = pltpu.VMEM(*flat_msg)
     rows16, rows32 = pltpu.VMEM(*wide16), pltpu.VMEM(*wide32)
-    narrow_states = pltpu.VMEM((pairs, 128, 128), bf16)
+    narrow_states = pltpu.VMEM((pairs // 2, WIDE, WIDE), bf16)
     x, keys, values, keys_far, values_far, fade, fade_t, marks, fall, send = call(
         forward_state,
         [
@@ -666,8 +675,8 @@
             ((blocks, 2 * pairs, 128), f32), ((slots, 128), bf16), state_msg,
         ],
         [info, decay_rates, events_in, weights, expand, own_lanes],
-        [flat, state_vmem, pltpu.VMEM((owners, per + 8, 128), bf16), two, rows16, sem((5,))],
-        {0: SMEM, 1: SMEM, 2: HBM, 3: HBM},
+        [flat, state_vmem, two, rows16, sem((5,))],
+        {0: SMEM, 1: SMEM, 3: HBM},
         (0, 3, 4),
     )
     partner = swapped(send, "ctx")
@@ -686,10 +695,10 @@
         [flat_msg, wide16, wide16, half_states, state_msg],
         [info, q8, lift, fade_t, attended, x, weights, grads_in, partner, *received],
         [
-            flat, pltpu.VMEM((owners, per, 128), bf16), one, rows16, rows32, rows16, rows16, rows16,
+            flat, one, rows16, rows32, rows16, rows16, rows16,
             rows16, block_wide, flat_narrow, narrow_states, state_vmem, sem((5,)), sem((blocks,)),
         ],
-        {0: SMEM, 4: HBM, 5: HBM, 6: HBM, 7: ANY},
+        {0: SMEM, 4: HBM, 5: HBM, 6: HBM},
         (0, 1),
     )
     partner = swapped(send, "ctx")

time: 136 us -> 133 us (0.978)
  Pallas kernels: 41.2 us -> 39 us
    pallas_call x11, Pallas kernels: 41.2 us -> 39 us  [call(): pl.pallas_call(body, out_shape=[pltpu.HBM(s, d) if i in out_hbm else jax....]
  transfers between devices with their start and end apart: 12 -> 12, of which waited for: 5 -> 5; matrix products, arithmetic and copies ran while one was open for 0% -> 0% of each run, Pallas kernels for 23% -> 22%
where the time goes in v4:
time: 133 us
  starting transfers between devices  50.2 us (38%)
  waiting for transfers between devices  42.5 us (32%)
  Pallas kernels  39 us (29%)
    all_to_all x4, waiting for transfers between devices, regroup(): return lax.all_to_all(value, 'log', split_axis=0, concat_axis=0, tiled=True)  40 us
    pallas_call x11, Pallas kernels, call(): pl.pallas_call(body, out_shape=[pltpu.HBM(s, d) if i in out_hbm else jax....  39 us
    all_to_all x4, starting transfers between devices, regroup(): return lax.all_to_all(value, 'log', split_axis=0, concat_axis=0, tiled=True)  35.3 us
    ppermute x6, starting transfers between devices, exchange(): lax.ppermute(value, axis, [(i, i + sign * k) for i in range(count) if 0 <...  14.5 us
  transfers between devices with their start and end apart: 12, of which 5 were waited for; matrix products, arithmetic and copies ran while one was open for 0% of the time, Pallas kernels for 22%

profile of v4, /device:TPU:24, one launch (start us, length us, event | category | flops | bytes accessed | tf_op | source)
XLA Modules:
  0.0 132.6 jit_solution(724109424475524152)
XLA Ops:
  0.6 2.9 %shard_map.86 = (bf16[32,88,128]{2,1,0:T(8,128)(2,1)}, s32[2,512]{1,0:T(2,128)S(1)}) custom-call(s32[1,512]{1,0:T(1,128)} %bitcast.19, bf16[512,512]{1,0:T(8,128)(2,1)} %bitcast.18, f32[1,512]{1,0:T(1,128)} %bitcast.20, f32[1,512]{1,0:T(1,128)} %bitcast.21), custom_call_target="tpu_custom_call" | custom-call | tf_op jit(solution)/shard_map/pallas_call | solution.py:42
  3.6 11.3 %all-to-all-start = ((bf16[32,88,128]{2,1,0:T(8,128)(2,1)}), bf16[32,88,128]{2,1,0:T(8,128)(2,1)S(1)}, u32[]{:S(2)}, u32[]{:S(2)}) async-start(bf16[32,88,128]{2,1,0:T(8,128)(2,1)} %get-tuple-element.32), calls=%async_computation | async-start | bytes 1441792 | tf_op jit(solution)/shard_map/all_to_all | solution.py:611
  15.0 2.7 %shard_map.87 = (bf16[2560,128]{1,0:T(8,128)(2,1)}, bf16[512,640]{1,0:T(8,128)(2,1)}, bf16[640,256]{1,0:T(8,128)(2,1)S(1)}, bf16[640,128]{1,0:T(8,128)(2,1)S(1)}) custom-call(s32[2]{0:T(128)S(1)} %pad_add_fusion.info, s32[2,512]{1,0:T(2,128)S(1)} %get-tuple-element.30.spots, bf16[512,512]{1,0:T(8,128)(2,1)S(1)} %bitcast.12), custom_call_target="tpu_custom_call" | custom-call | tf_op jit(solution)/shard_map/pallas_call | solution.py:42
  17.7 18.8 %all-to-all-done.message = bf16[32,88,128]{2,1,0:T(8,128)(2,1)S(1)} async-done(((bf16[32,88,128]{2,1,0:T(8,128)(2,1)}), bf16[32,88,128]{2,1,0:T(8,128)(2,1)S(1)}, u32[]{:S(2)}, u32[]{:S(2)}) %all-to-all-start) | async-done | bytes 720928 | tf_op jit(solution)/shard_map/all_to_all | solution.py:611
  36.5 5.0 %all-to-all-start.1 = ((bf16[32,80,128]{2,1,0:T(8,128)(2,1)}), bf16[32,80,128]{2,1,0:T(8,128)(2,1)S(1)}, u32[]{:S(2)}, u32[]{:S(2)}) async-start(bf16[32,80,128]{2,1,0:T(8,128)(2,1)} %bitcast.15), calls=%async_computation.1 | async-start | bytes 1310720 | tf_op jit(solution)/shard_map/all_to_all | solution.py:611
  41.5 4.5 %shard_map.88 = (bf16[640,512]{1,0:T(8,128)(2,1)}, bf16[640,512]{1,0:T(8,128)(2,1)S(1)}, bf16[640,512]{1,0:T(8,128)(2,1)S(1)}, bf16[640,512]{1,0:T(8,128)(2,1)},...) custom-call(s32[2]{0:T(128)S(1)} %pad_add_fusion.info, ...), custom_call_target="tpu_custom_call" | custom-call | tf_op jit(solution)/shard_map/pallas_call | solution.py:42
  46.1 1.2 collective-permute-done.other.partner
  48.1 1.3 collective-permute-start.1
  49.4 1.3 collective-permute-start.2
  50.7 1.3 collective-permute-start.3
  52.0 6.3 %shard_map.89 = (bf16[640,512]{1,0:T(8,128)(2,1)S(1)}, f32[640,512]{1,0:T(8,128)}, bf16[5,4,64,128]{3,2,1,0:T(8,128)(2,1)S(1)}, bf16[640,128]{1,0:T(8,128)(2,1)S(1)}) custom-call(s32[2]{0:T(128)S(1)} %pad_add_fusion.info, bf16[640,512]{1,0:T(8,128)(2,1)} %get-tuple-element.35.x_in, bf16[4,4,512,512]{3,2,1,0:T(8,128)(2,1)} %weights.9, ...), custom_call_target="tpu_custom_call" | custom-call | tf_op jit(solution)/shard_map/pallas_call | solution.py:42
  58.2 2.6 %all-to-all-done.1.message = bf16[32,80,128]{2,1,0:T(8,128)(2,1)S(1)} async-done(((bf16[32,80,128]{2,1,0:T(8,128)(2,1)}), bf16[32,80,128]{2,1,0:T(8,128)(2,1)S(1)}, u32[]{:S(2)}, u32[]{:S(2)}) %all-to-all-start.1) | async-done | bytes 655392 | tf_op jit(solution)/shard_map/all_to_all | solution.py:611
  60.8 5.3 %shard_map.91 = (bf16[2560,128]{1,0:T(8,128)(2,1)}, bf16[640,512]{1,0:T(8,128)(2,1)}, bf16[640,512]{1,0:T(8,128)(2,1)S(1)}, f32[4,64,128]{2,1,0:T(8,128)S(1)}, bf16[264,128]{1,0:T(8,128)(2,1)S(1)}) custom-call(s32[2]{0:T(128)S(1)} %pad_add_fusion.info, bf16[640,512]{1,0:T(8,128)(2,1)S(1)} %get-tuple-element.41.q8, ...), custom_call_target="tpu_custom_call" | custom-call | tf_op jit(solution)/shard_map/pallas_call | solution.py:42
  66.1 9.1 %all-to-all-start.2 = ((bf16[32,80,128]{2,1,0:T(8,128)(2,1)}), bf16[32,80,128]{2,1,0:T(8,128)(2,1)S(1)}, u32[]{:S(2)}, u32[]{:S(2)}) async-start(bf16[32,80,128]{2,1,0:T(8,128)(2,1)} %bitcast.14), calls=%async_computation.2 | async-start | bytes 1310720 | tf_op jit(solution)/shard_map/all_to_all | solution.py:611
  75.5 1.2 collective-permute-done.4.other.partner
  77.5 2.1 %collective-permute-start.5 = (bf16[264,128]{1,0:T(8,128)(2,1)S(1)}, bf16[264,128]{1,0:T(8,128)(2,1)S(1)}, u32[]{:S(2)}, u32[]{:S(2)}) collective-permute-start(bf16[264,128]{1,0:T(8,128)(2,1)S(1)} %shard_map.94), channel_id=1, source_target_pairs={{2,0},{3,1},{4,2},{5,3},{6,4},{7,5},{10,8},{11,9},{12,10},{13,11},... | collective-permute-start | bytes 202760 | tf_op jit(solution)/shard_map/ppermute | solution.py:603
  79.5 7.3 %collective-permute-start.6 = (bf16[264,128]{1,0:T(8,128)(2,1)S(1)}, bf16[264,128]{1,0:T(8,128)(2,1)S(1)}, u32[]{:S(2)}, u32[]{:S(2)}) collective-permute-start(bf16[264,128]{1,0:T(8,128)(2,1)S(1)} %shard_map.94), channel_id=1, source_target_pairs={{4,0},{5,1},{6,2},{7,3},{12,8},{13,9},{14,10},{15,11},{20,16},{21,... | collective-permute-start | bytes 202760 | tf_op jit(solution)/shard_map/ppermute | solution.py:603
  86.8 1.3 collective-permute-start.7
  88.1 8.7 %shard_map.93 = (f32[640,512]{1,0:T(8,128)S(1)}, f32[640,512]{1,0:T(8,128)S(1)}, f32[640,512]{1,0:T(8,128)S(1)}) custom-call(s32[2]{0:T(128)S(1)} %pad_add_fusion.info, bf16[640,512]{1,0:T(8,128)(2,1)S(1)} %get-tuple-element.41.q8, bf16[640,512]{1,0:T(8,128)(2,1)} %get-tuple-element.47.keys_in, bf16[640,512]{1,0:T(8,128)(2,1)} %get-tuple-element.48.values_in, ...), custom_call_target="tpu_custom_call" | custom-call | tf_op jit(solution)/shard_map/pallas_call | solution.py:42
  96.8 4.5 %shard_map.95 = bf16[2560,128]{1,0:T(8,128)(2,1)} custom-call(s32[2]{0:T(128)S(1)} %pad_add_fusion.info, f32[640,512]{1,0:T(8,128)S(1)} %get-tuple-element.53.partial, f32[640,512]{1,0:T(8,128)S(1)} %get-tuple-element.54.grad_keys, f32[640,512]{1,0:T(8,128)S(1)} %get-tuple-element.55.grad_values, bf16[640,512]{1,0:T(8,128)(2,1)} %get-tuple-element.47.keys_in, ...), custom_call_target="tpu_custom_call" | custom-call | tf_op jit(solution)/shard_map/pallas_call | solution.py:42
  101.3 9.9 %all-to-all-start.3 = ((bf16[32,80,128]{2,1,0:T(8,128)(2,1)}), bf16[32,80,128]{2,1,0:T(8,128)(2,1)S(1)}, u32[]{:S(2)}, u32[]{:S(2)}) async-start(bf16[32,80,128]{2,1,0:T(8,128)(2,1)} %bitcast.13), calls=%async_computation.3 | async-start | bytes 1310720 | tf_op jit(solution)/shard_map/all_to_all | solution.py:611
  111.3 1.4 %shard_map.92 = bf16[512,512]{1,0:T(8,128)(2,1)} custom-call(bf16[512,640]{1,0:T(8,128)(2,1)S(1)} %copy-done, bf16[32,80,128]{2,1,0:T(8,128)(2,1)S(1)} %all-to-all-done.2.message), custom_call_target="tpu_custom_call" | custom-call | tf_op jit(solution)/shard_map/pallas_call | solution.py:42
  112.7 18.5 %all-to-all-done.3.message = bf16[32,80,128]{2,1,0:T(8,128)(2,1)S(1)} async-done(((bf16[32,80,128]{2,1,0:T(8,128)(2,1)}), bf16[32,80,128]{2,1,0:T(8,128)(2,1)S(1)}, u32[]{:S(2)}, u32[]{:S(2)}) %all-to-all-start.3) | async-done | bytes 655392 | tf_op jit(solution)/shard_map/all_to_all | solution.py:611
  131.2 1.4 %shard_map.96 = bf16[512,512]{1,0:T(8,128)(2,1)} custom-call(bf16[512,640]{1,0:T(8,128)(2,1)S(1)} %copy-done, bf16[32,80,128]{2,1,0:T(8,128)(2,1)S(1)} %all-to-all-done.3.message), custom_call_target="tpu_custom_call" | custom-call | tf_op jit(solution)/shard_map/pallas_call | solution.py:42
  (18 shorter events, 1.9 us)
Async XLA Ops:
  0.6 14.4 %copy-start.1 = (bf16[1,1,512,512]{3,2,1,0:T(8,128)(2,1)S(1)}, bf16[1,1,512,512]{3,2,1,0:T(8,128)(2,1)}, u32[]{:S(2)}) copy-start(bf16[1,1,512,512]{3,2,1,0:T(8,128)(2,1)} %param.13) | copy-start | bytes 1572868
  3.6 33.0 %all-to-all-start = ((bf16[32,88,128]{2,1,0:T(8,128)(2,1)}), bf16[32,88,128]{2,1,0:T(8,128)(2,1)S(1)}, u32[]{:S(2)}, u32[]{:S(2)}) async-start(bf16[32,88,128]{2,1,0:T(8,128)(2,1)} %get-tuple-element.32), calls=%async_computation | async-start | bytes 1441792 | tf_op jit(solution)/shard_map/all_to_all | solution.py:611
  14.9 26.6 %copy-start.2 = (f32[4,8]{1,0:T(4,128)S(1)}, f32[4,8]{1,0:T(4,128)}, u32[]{:S(2)}) copy-start(f32[4,8]{1,0:T(4,128)} %rates.1) | copy-start | bytes 388
  36.5 24.3 %all-to-all-start.1 = ((bf16[32,80,128]{2,1,0:T(8,128)(2,1)}), bf16[32,80,128]{2,1,0:T(8,128)(2,1)S(1)}, u32[]{:S(2)}, u32[]{:S(2)}) async-start(bf16[32,80,128]{2,1,0:T(8,128)(2,1)} %bitcast.15), calls=%async_computation.1 | async-start | bytes 1310720 | tf_op jit(solution)/shard_map/all_to_all | solution.py:611
  46.0 1.3 %collective-permute-start = (bf16[264,128]{1,0:T(8,128)(2,1)S(1)}, bf16[264,128]{1,0:T(8,128)(2,1)S(1)}, u32[]{:S(2)}, u32[]{:S(2)}) collective-permute-start(bf16[264,128]{1,0:T(8,128)(2,1)S(1)} %get-tuple-element.45.own), channel_id=1, source_target_pairs={{0,1},{1,0},{2,3},{3,2},{4,5},{5,4},{6,7},{7,6},{8,9},{9,8},{10,11... | collective-permute-start | bytes 202760 | tf_op jit(solution)/shard_map/ppermute | solution.py:597
  48.1 12.8 %collective-permute-start.1 = (bf16[264,128]{1,0:T(8,128)(2,1)S(1)}, bf16[264,128]{1,0:T(8,128)(2,1)S(1)}, u32[]{:S(2)}, u32[]{:S(2)}) collective-permute-start(bf16[264,128]{1,0:T(8,128)(2,1)S(1)} %shard_map.90), channel_id=1, source_target_pairs={{0,2},{1,3},{2,4},{3,5},{4,6},{5,7},{8,10},{9,11},{10,12},{11,13},... | collective-permute-start | bytes 202760 | tf_op jit(solution)/shard_map/ppermute | solution.py:603
  49.4 11.5 %collective-permute-start.2 = (bf16[264,128]{1,0:T(8,128)(2,1)S(1)}, bf16[264,128]{1,0:T(8,128)(2,1)S(1)}, u32[]{:S(2)}, u32[]{:S(2)}) collective-permute-start(bf16[264,128]{1,0:T(8,128)(2,1)S(1)} %shard_map.90), channel_id=1, source_target_pairs={{0,4},{1,5},{2,6},{3,7},{8,12},{9,13},{10,14},{11,15},{16,20},{17,... | collective-permute-start | bytes 202760 | tf_op jit(solution)/shard_map/ppermute | solution.py:603
  50.7 10.2 %collective-permute-start.3 = (bf16[264,128]{1,0:T(8,128)(2,1)S(1)}, bf16[264,128]{1,0:T(8,128)(2,1)S(1)}, u32[]{:S(2)}, u32[]{:S(2)}) collective-permute-start(bf16[264,128]{1,0:T(8,128)(2,1)S(1)} %shard_map.90), channel_id=1, source_target_pairs={{0,6},{1,7},{8,14},{9,15},{16,22},{17,23},{24,30},{25,31},{32,38},... | collective-permute-start | bytes 202760 | tf_op jit(solution)/shard_map/ppermute | solution.py:603
  66.1 35.2 %all-to-all-start.2 = ((bf16[32,80,128]{2,1,0:T(8,128)(2,1)}), bf16[32,80,128]{2,1,0:T(8,128)(2,1)S(1)}, u32[]{:S(2)}, u32[]{:S(2)}) async-start(bf16[32,80,128]{2,1,0:T(8,128)(2,1)} %bitcast.14), calls=%async_computation.2 | async-start | bytes 1310720 | tf_op jit(solution)/shard_map/all_to_all | solution.py:611
  75.2 1.5 %collective-permute-start.4 = (bf16[264,128]{1,0:T(8,128)(2,1)S(1)}, bf16[264,128]{1,0:T(8,128)(2,1)S(1)}, u32[]{:S(2)}, u32[]{:S(2)}) collective-permute-start(bf16[264,128]{1,0:T(8,128)(2,1)S(1)} %get-tuple-element.57.own), channel_id=1, source_target_pairs={{0,1},{1,0},{2,3},{3,2},{4,5},{5,4},{6,7},{7,6},{8,9},{9,8},{10,11... | collective-permute-start | bytes 202760 | tf_op jit(solution)/shard_map/ppermute | solution.py:597
  77.5 19.3 %collective-permute-start.5 = (bf16[264,128]{1,0:T(8,128)(2,1)S(1)}, bf16[264,128]{1,0:T(8,128)(2,1)S(1)}, u32[]{:S(2)}, u32[]{:S(2)}) collective-permute-start(bf16[264,128]{1,0:T(8,128)(2,1)S(1)} %shard_map.94), channel_id=1, source_target_pairs={{2,0},{3,1},{4,2},{5,3},{6,4},{7,5},{10,8},{11,9},{12,10},{13,11},... | collective-permute-start | bytes 202760 | tf_op jit(solution)/shard_map/ppermute | solution.py:603
  79.5 17.3 %collective-permute-start.6 = (bf16[264,128]{1,0:T(8,128)(2,1)S(1)}, bf16[264,128]{1,0:T(8,128)(2,1)S(1)}, u32[]{:S(2)}, u32[]{:S(2)}) collective-permute-start(bf16[264,128]{1,0:T(8,128)(2,1)S(1)} %shard_map.94), channel_id=1, source_target_pairs={{4,0},{5,1},{6,2},{7,3},{12,8},{13,9},{14,10},{15,11},{20,16},{21,... | collective-permute-start | bytes 202760 | tf_op jit(solution)/shard_map/ppermute | solution.py:603
  86.8 10.0 %collective-permute-start.7 = (bf16[264,128]{1,0:T(8,128)(2,1)S(1)}, bf16[264,128]{1,0:T(8,128)(2,1)S(1)}, u32[]{:S(2)}, u32[]{:S(2)}) collective-permute-start(bf16[264,128]{1,0:T(8,128)(2,1)S(1)} %shard_map.94), channel_id=1, source_target_pairs={{6,0},{7,1},{14,8},{15,9},{22,16},{23,17},{30,24},{31,25},{38,32},... | collective-permute-start | bytes 202760 | tf_op jit(solution)/shard_map/ppermute | solution.py:603
  101.3 10.0 %copy-start = (bf16[512,640]{1,0:T(8,128)(2,1)S(1)}, bf16[512,640]{1,0:T(8,128)(2,1)}, u32[]{:S(2)}) copy-start(bf16[512,640]{1,0:T(8,128)(2,1)} %get-tuple-element.31.back) | copy-start | bytes 1966084
  101.3 29.9 %all-to-all-start.3 = ((bf16[32,80,128]{2,1,0:T(8,128)(2,1)}), bf16[32,80,128]{2,1,0:T(8,128)(2,1)S(1)}, u32[]{:S(2)}, u32[]{:S(2)}) async-start(bf16[32,80,128]{2,1,0:T(8,128)(2,1)} %bitcast.13), calls=%async_computation.3 | async-start | bytes 1310720 | tf_op jit(solution)/shard_map/all_to_all | solution.py:611

commit v5 on v4

--- a/solution.py
+++ b/solution.py
@@ -428,16 +428,15 @@
         rows_copy(attended, attended_out, sems, j).wait()
 
 
-def turn(info, q8, lift, fade_t, attended_in, x_in, weights, message, partner, *rest):
-    received = rest[:-19]
+def encode(info, q8, lift, attended_in, x_in, weights, partner, *rest):
+    received = rest[:-12]
     (
-        encoded, grads_out, grad_full, incoming, send,
-        scratch, mine, x, attended, grads, grad_normed, normed, lifts,
-        wide, narrow, states, memory, sems, out_sems,
-    ) = rest[-19:]
-    fetch = fetched(weights.at[info[0], 3], mine, sems.at[0])
-    rows_in = fetched(x_in, x, sems.at[1])
-    attended_here = fetched(attended_in, attended, sems.at[3])
+        encoded, full_out, incoming,
+        mine, x, attended, normed, wide, narrow, states, sems, full_sems,
+    ) = rest[-12:]
+    attended_here = fetched(attended_in, attended, sems.at[0])
+    fetch = fetched(weights.at[info[0], 3], mine, sems.at[1])
+    rows_in = fetched(x_in, x, sems.at[2])
     slots, width = x.shape
     pairs = width // 128
     blocks = slots // CH
@@ -445,16 +444,8 @@
     for p in range(pairs):
         incoming[p] = arrived[p]
     set_states(states, arrived)
-    for j, part in enumerate(read_message(message, scratch, width)):
-        grads[:, 128 * j : 128 * (j + 1)] = part.astype(bf16)
-    store = fetched(grads, grads_out, sems.at[4])
-    fetch.wait()
-    for n in range(0, width, WIDE):
-        cols = slice(n, n + WIDE)
-        grad_normed[:, cols] = dot(grads[...], mine[cols, :], NT).astype(bf16)
+    hot = spread_all(2, width)
     attended_here.wait()
-
-    hot = spread_all(2, width)
 
     def block(j, carry):
         rows = pl.ds(pl.multiple_of(j * CH, CH), CH)
@@ -464,13 +455,60 @@
         for n in range(pairs // 2):
             cols = slice(WIDE * n, WIDE * (n + 1))
             lifted = (q8[rows, cols].astype(f32) * factors[:, cols]).astype(bf16)
-            lifts[rows, cols] = lifted
             value = attended[rows, cols] + dot(lifted, states[n])
+            attended[rows, cols] = value
             values.append(value)
             square += jnp.sum(value * value, axis=1, keepdims=True)
-        here = jnp.concatenate(values, axis=1)
         scale = lax.rsqrt(square * (1.0 / width) + 1e-06)
-        normed[rows, :] = (here * scale).astype(bf16)
+        normed[rows, :] = (jnp.concatenate(values, axis=1) * scale).astype(bf16)
+        rows_copy(attended, full_out, full_sems, j).start()
+        return carry
+
+    lax.fori_loop(0, blocks, block, 0, unroll=True)
+    rows_in.wait()
+    fetch.wait()
+    halves_out = [
+        x[:, n : n + WIDE].astype(f32) + dot(normed[...], mine[:, n : n + WIDE])
+        for n in range(0, width, WIDE)
+    ]
+    for n, half in enumerate(halves_out):
+        wide[pl.ds(2 * n, slots, stride=pairs), :] = half[:, 0:128]
+        wide[pl.ds(2 * n + 1, slots, stride=pairs), :] = half[:, 128:WIDE]
+    narrow[...] = wide[...].astype(bf16)
+    out = fetched(narrow, encoded, sems.at[3])
+    for j in range(blocks):
+        rows_copy(attended, full_out, full_sems, j).wait()
+    out.wait()
+
+
+def turn(
+    info, q8, lift, fade_t, full_in, weights, message,
+    grads_out, grad_full, send,
+    scratch, mine, full, grads, grad_normed, lifts, memory, sems,
+):
+    full_here = fetched(full_in, full, sems.at[0])
+    fetch = fetched(weights.at[info[0], 3], mine, sems.at[1])
+    slots, width = full.shape
+    pairs = width // 128
+    blocks = slots // CH
+    for j, part in enumerate(read_message(message, scratch, width)):
+        grads[:, 128 * j : 128 * (j + 1)] = part.astype(bf16)
+    store = fetched(grads, grads_out, sems.at[2])
+    fetch.wait()
+    for n in range(0, width, WIDE):
+        cols = slice(n, n + WIDE)
+        grad_normed[:, cols] = dot(grads[...], mine[cols, :], NT).astype(bf16)
+    hot = spread_all(2, width)
+    for n in range(0, width, WIDE):
+        cols = slice(n, n + WIDE)
+        factors = dot(lift[...], hot[:, cols])
+        lifts[:, cols] = (q8[:, cols].astype(f32) * factors).astype(bf16)
+    full_here.wait()
+
+    def block(j, carry):
+        rows = pl.ds(pl.multiple_of(j * CH, CH), CH)
+        here = full[rows, :]
+        scale = lax.rsqrt(jnp.mean(here * here, axis=1, keepdims=True) + 1e-06)
         grad = grad_normed[rows, :].astype(f32)
         along = jnp.mean(here * grad, axis=1, keepdims=True)
         grad_full[rows, :] = (scale * grad - here * (scale * scale * scale * along)).astype(bf16)
@@ -481,32 +519,17 @@
         cols = slice(WIDE * n, WIDE * (n + 1))
         set_memory(memory, dot(lifts[:, cols], grad_full[:, cols], TN), n)
     write_state(send, memory, fade_t[blocks - 1][:, CH - 1 : CH], pairs)
-    rows_in.wait()
-    for n in range(0, width, WIDE):
-        cols = slice(n, n + WIDE)
-        attended[:, cols] = x[:, cols].astype(f32) + dot(normed[...], mine[:, cols])
-    sender = Sender(encoded, wide, narrow, out_sems, pairs)
-
-    def put(j, carry):
-        sender.put(j, attended[pl.ds(pl.multiple_of(j * CH, CH), CH), :])
-        return carry
-
-    lax.fori_loop(0, blocks, put, 0)
-    sender.finish(blocks)
     store.wait()
 
 
 def backward_local(
-    info, q8, keys_in, values_in, fade, fade_t, marks, grad_full, states, incoming,
-    grads_in, weights,
-    grad_keys, grad_values, partial,
-    memory, grad_q, grads, mine, keys, values, sems, key_sems, value_sems,
+    q8, keys_in, values_in, fade, fade_t, marks, grad_full, states, incoming,
+    grad_q, grad_keys, grad_values,
+    memory, keys, values, key_sems, value_sems,
 ):
     for j in reversed(range(q8.shape[0] // CH)):
         rows_copy(keys_in, keys, key_sems, j).start()
         rows_copy(values_in, values, value_sems, j).start()
-    arrival = fetched(grads_in, grads, sems.at[0])
-    fetch = fetched(weights.at[info[0], 0], mine, sems.at[1])
     slots, width = q8.shape
     pairs = width // 128
     blocks = slots // CH
@@ -549,9 +572,14 @@
         return carry
 
     lax.fori_loop(0, blocks, block, 0, unroll=True)
+
+
+def project_back(info, grads_in, grad_q, weights, partial, mine, grads, sems):
+    arrival = fetched(grads_in, grads, sems.at[0])
+    fetch = fetched(weights.at[info[0], 0], mine, sems.at[1])
+    fetch.wait()
     arrival.wait()
-    fetch.wait()
-    for n in range(0, width, WIDE):
+    for n in range(0, grads.shape[1], WIDE):
         cols = slice(n, n + WIDE)
         partial[:, cols] = grads[:, cols].astype(f32) + dot(grad_q[...], mine[cols, :], NT)
 
@@ -690,34 +718,43 @@
         {0: SMEM, 1: HBM, 2: HBM},
         (1,),
     )
-    message, grads, grad_full, incoming, send = call(
-        turn,
-        [flat_msg, wide16, wide16, half_states, state_msg],
-        [info, q8, lift, fade_t, attended, x, weights, grads_in, partner, *received],
+    message, full, incoming = call(
+        encode,
+        [flat_msg, wide32, half_states],
+        [info, q8, lift, attended, x, weights, partner, *received],
         [
-            flat, one, rows16, rows32, rows16, rows16, rows16,
-            rows16, block_wide, flat_narrow, narrow_states, state_vmem, sem((5,)), sem((blocks,)),
-        ],
-        {0: SMEM, 4: HBM, 5: HBM, 6: HBM},
-        (0, 1),
-    )
-    partner = swapped(send, "ctx")
-    encoded_in = regroup(message.reshape(owners, per, 128))
-    grad_keys, grad_values, partial = call(
-        backward_local,
-        [wide32, wide32, wide32],
-        [
-            info, q8, keys_far, values_far, fade, fade_t, marks, grad_full, kept, incoming, grads,
-            weights,
-        ],
-        [
-            state_vmem, rows16, rows16, one, rows16, rows16, sem((2,)), sem((blocks,)),
+            one, rows16, rows32, rows16, flat, flat_narrow, narrow_states, sem((4,)),
             sem((blocks,)),
         ],
-        {0: SMEM, 2: HBM, 3: HBM, 10: HBM, 11: HBM},
+        {0: SMEM, 3: HBM, 4: HBM, 5: HBM},
+        (0, 1),
+    )
+    encoded_in = regroup(message.reshape(owners, per, 128))
+    grads, grad_full, send = call(
+        turn,
+        [wide16, wide16, state_msg],
+        [info, q8, lift, fade_t, full, weights, grads_in],
+        [flat, one, rows32, rows16, rows16, rows16, state_vmem, sem((3,))],
+        {0: SMEM, 4: HBM, 5: HBM},
+        (0,),
+    )
+    partner = swapped(send, "ctx")
+    grad_q, grad_keys, grad_values = call(
+        backward_local,
+        [wide16, wide32, wide32],
+        [q8, keys_far, values_far, fade, fade_t, marks, grad_full, kept, incoming],
+        [state_vmem, rows16, rows16, sem((blocks,)), sem((blocks,))],
+        {1: HBM, 2: HBM},
     )
     (joined,) = call(join_back, [state_msg], [info, send, partner], (), {0: SMEM})
     received = exchange(joined, "ctx", -1)
+    (partial,) = call(
+        project_back,
+        [wide32],
+        [info, grads, grad_q, weights],
+        [one, rows16, sem((2,))],
+        {0: SMEM, 1: HBM, 3: HBM},
+    )
     (message,) = call(
         backward_finish,
         [flat_msg],

time: 133 us -> 137 us (1.030)
  Pallas kernels: 39 us -> 43.1 us
    pallas_call x11 -> x13, Pallas kernels: 39 us -> 43.1 us  [call(): pl.pallas_call(body, out_shape=[pltpu.HBM(s, d) if i in out_hbm else jax....]
    all_to_all x4, waiting for transfers between devices: 40 us -> 37.4 us  [regroup(): return lax.all_to_all(value, 'log', split_axis=0, concat_axis=0, tiled=True)]
    ppermute x6, waiting for transfers between devices: 0.02 us -> 1.89 us  [exchange(): lax.ppermute(value, axis, [(i, i + sign * k) for i in range(count) if 0 <...]
  transfers between devices with their start and end apart: 12 -> 12, of which waited for: 5 -> 5; matrix products, arithmetic and copies ran while one was open for 0% -> 0% of each run, Pallas kernels for 22% -> 28%
where the time goes in v5:
time: 137 us
  starting transfers between devices  50.7 us (37%)
  Pallas kernels  43.1 us (31%)
  waiting for transfers between devices  41.8 us (31%)
    pallas_call x13, Pallas kernels, call(): pl.pallas_call(body, out_shape=[pltpu.HBM(s, d) if i in out_hbm else jax....  43.1 us
    all_to_all x4, waiting for transfers between devices, regroup(): return lax.all_to_all(value, 'log', split_axis=0, concat_axis=0, tiled=True)  37.4 us
    all_to_all x4, starting transfers between devices, regroup(): return lax.all_to_all(value, 'log', split_axis=0, concat_axis=0, tiled=True)  36 us
    ppermute x6, starting transfers between devices, exchange(): lax.ppermute(value, axis, [(i, i + sign * k) for i in range(count) if 0 <...  14.5 us
  transfers between devices with their start and end apart: 12, of which 5 were waited for; matrix products, arithmetic and copies ran while one was open for 0% of the time, Pallas kernels for 28%

profile of v5, /device:TPU:24, one launch (start us, length us, event | category | flops | bytes accessed | tf_op | source)
XLA Modules:
  0.0 136.7 jit_solution(3373457461037363686)
XLA Ops:
  0.6 2.9 %shard_map.86 = (bf16[32,88,128]{2,1,0:T(8,128)(2,1)}, s32[2,512]{1,0:T(2,128)S(1)}) custom-call(s32[1,512]{1,0:T(1,128)} %bitcast.19, bf16[512,512]{1,0:T(8,128)(2,1)} %bitcast.18, f32[1,512]{1,0:T(1,128)} %bitcast.20, f32[1,512]{1,0:T(1,128)} %bitcast.21), custom_call_target="tpu_custom_call" | custom-call | tf_op jit(solution)/shard_map/pallas_call | solution.py:42
  3.5 11.3 %all-to-all-start = ((bf16[32,88,128]{2,1,0:T(8,128)(2,1)}), bf16[32,88,128]{2,1,0:T(8,128)(2,1)S(1)}, u32[]{:S(2)}, u32[]{:S(2)}) async-start(bf16[32,88,128]{2,1,0:T(8,128)(2,1)} %get-tuple-element.33), calls=%async_computation | async-start | bytes 1441792 | tf_op jit(solution)/shard_map/all_to_all | solution.py:639
  15.0 2.6 %shard_map.87 = (bf16[2560,128]{1,0:T(8,128)(2,1)}, bf16[512,640]{1,0:T(8,128)(2,1)}, bf16[640,256]{1,0:T(8,128)(2,1)S(1)}, bf16[640,128]{1,0:T(8,128)(2,1)S(1)}) custom-call(s32[2]{0:T(128)S(1)} %pad_add_fusion.info, s32[2,512]{1,0:T(2,128)S(1)} %get-tuple-element.31.spots, bf16[512,512]{1,0:T(8,128)(2,1)S(1)} %bitcast.12), custom_call_target="tpu_custom_call" | custom-call | tf_op jit(solution)/shard_map/pallas_call | solution.py:42
  17.6 18.9 %all-to-all-done.message = bf16[32,88,128]{2,1,0:T(8,128)(2,1)S(1)} async-done(((bf16[32,88,128]{2,1,0:T(8,128)(2,1)}), bf16[32,88,128]{2,1,0:T(8,128)(2,1)S(1)}, u32[]{:S(2)}, u32[]{:S(2)}) %all-to-all-start) | async-done | bytes 720928 | tf_op jit(solution)/shard_map/all_to_all | solution.py:639
  36.5 5.0 %all-to-all-start.2 = ((bf16[32,80,128]{2,1,0:T(8,128)(2,1)}), bf16[32,80,128]{2,1,0:T(8,128)(2,1)S(1)}, u32[]{:S(2)}, u32[]{:S(2)}) async-start(bf16[32,80,128]{2,1,0:T(8,128)(2,1)} %bitcast.15), calls=%async_computation.2 | async-start | bytes 1310720 | tf_op jit(solution)/shard_map/all_to_all | solution.py:639
  41.5 4.5 %shard_map.88 = (bf16[640,512]{1,0:T(8,128)(2,1)}, bf16[640,512]{1,0:T(8,128)(2,1)S(1)}, bf16[640,512]{1,0:T(8,128)(2,1)S(1)}, bf16[640,512]{1,0:T(8,128)(2,1)},...) custom-call(s32[2]{0:T(128)S(1)} %pad_add_fusion.info, ...), custom_call_target="tpu_custom_call" | custom-call | tf_op jit(solution)/shard_map/pallas_call | solution.py:42
  48.1 1.3 collective-permute-start.1
  49.4 1.3 collective-permute-start.2
  50.7 1.3 collective-permute-start.3
  52.0 6.3 %shard_map.89 = (bf16[640,512]{1,0:T(8,128)(2,1)S(1)}, f32[640,512]{1,0:T(8,128)}, bf16[5,4,64,128]{3,2,1,0:T(8,128)(2,1)S(1)}, bf16[640,128]{1,0:T(8,128)(2,1)S(1)}) custom-call(s32[2]{0:T(128)S(1)} %pad_add_fusion.info, bf16[640,512]{1,0:T(8,128)(2,1)} %get-tuple-element.36.x_in, bf16[4,4,512,512]{3,2,1,0:T(8,128)(2,1)} %weights.11, ...), custom_call_target="tpu_custom_call" | custom-call | tf_op jit(solution)/shard_map/pallas_call | solution.py:42
  58.3 1.9 %collective-permute-done.3.rest_2_ = bf16[264,128]{1,0:T(8,128)(2,1)S(1)} collective-permute-done((bf16[264,128]{1,0:T(8,128)(2,1)S(1)}, bf16[264,128]{1,0:T(8,128)(2,1)S(1)}, u32[]{:S(2)}, u32[]{:S(2)}) %collective-permute-start.3) | collective-permute-done | bytes 67616 | tf_op jit(solution)/shard_map/ppermute | solution.py:631
  60.1 4.4 %shard_map.91 = (bf16[2560,128]{1,0:T(8,128)(2,1)}, f32[640,512]{1,0:T(8,128)}, f32[4,64,128]{2,1,0:T(8,128)S(1)}) custom-call(s32[2]{0:T(128)S(1)} %pad_add_fusion.info, bf16[640,512]{1,0:T(8,128)(2,1)S(1)} %get-tuple-element.42.q8, bf16[640,128]{1,0:T(8,128)(2,1)S(1)} %get-tuple-element.43.lift, f32[640,512]{1,0:T(8,128)} %get-tuple-element.44.attended_in, ...), custom_call_target="tpu_custom_call" | custom-call | tf_op jit(solution)/shard_map/pallas_call | solution.py:42
  64.6 10.0 %all-to-all-start.1 = ((bf16[32,80,128]{2,1,0:T(8,128)(2,1)}), bf16[32,80,128]{2,1,0:T(8,128)(2,1)S(1)}, u32[]{:S(2)}, u32[]{:S(2)}) async-start(bf16[32,80,128]{2,1,0:T(8,128)(2,1)} %bitcast.14), calls=%async_computation.1 | async-start | bytes 1310720 | tf_op jit(solution)/shard_map/all_to_all | solution.py:639
  74.6 3.8 %shard_map.93 = (bf16[640,512]{1,0:T(8,128)(2,1)}, bf16[640,512]{1,0:T(8,128)(2,1)S(1)}, bf16[264,128]{1,0:T(8,128)(2,1)S(1)}) custom-call(s32[2]{0:T(128)S(1)} %pad_add_fusion.info, bf16[640,512]{1,0:T(8,128)(2,1)S(1)} %get-tuple-element.42.q8, bf16[640,128]{1,0:T(8,128)(2,1)S(1)} %get-tuple-element.43.lift, f32[5,8,128]{2,1,0:T(8,128)S(1)} %get-tuple-element.40.fade_t, ...), custom_call_target="tpu_custom_call" | custom-call | tf_op jit(solution)/shard_map/pallas_call | solution.py:42
  80.4 2.1 %collective-permute-start.5 = (bf16[264,128]{1,0:T(8,128)(2,1)S(1)}, bf16[264,128]{1,0:T(8,128)(2,1)S(1)}, u32[]{:S(2)}, u32[]{:S(2)}) collective-permute-start(bf16[264,128]{1,0:T(8,128)(2,1)S(1)} %shard_map.96), channel_id=1, source_target_pairs={{2,0},{3,1},{4,2},{5,3},{6,4},{7,5},{10,8},{11,9},{12,10},{13,11},... | collective-permute-start | bytes 202760 | tf_op jit(solution)/shard_map/ppermute | solution.py:631
  82.5 7.3 %collective-permute-start.6 = (bf16[264,128]{1,0:T(8,128)(2,1)S(1)}, bf16[264,128]{1,0:T(8,128)(2,1)S(1)}, u32[]{:S(2)}, u32[]{:S(2)}) collective-permute-start(bf16[264,128]{1,0:T(8,128)(2,1)S(1)} %shard_map.96), channel_id=1, source_target_pairs={{4,0},{5,1},{6,2},{7,3},{12,8},{13,9},{14,10},{15,11},{20,16},{21,... | collective-permute-start | bytes 202760 | tf_op jit(solution)/shard_map/ppermute | solution.py:631
  89.8 1.3 collective-permute-start.7
  91.1 7.6 %shard_map.94 = (bf16[640,512]{1,0:T(8,128)(2,1)S(1)}, f32[640,512]{1,0:T(8,128)S(1)}, f32[640,512]{1,0:T(8,128)S(1)}) custom-call(bf16[640,512]{1,0:T(8,128)(2,1)S(1)} %get-tuple-element.42.q8, bf16[640,512]{1,0:T(8,128)(2,1)} %get-tuple-element.50.keys_in, bf16[640,512]{1,0:T(8,128)(2,1)} %get-tuple-element.51.values_in, ...), custom_call_target="tpu_custom_call" | custom-call | tf_op jit(solution)/shard_map/pallas_call | solution.py:42
  98.7 2.3 %shard_map.95.partial = f32[640,512]{1,0:T(8,128)S(1)} custom-call(s32[2]{0:T(128)S(1)} %pad_add_fusion.info, bf16[640,512]{1,0:T(8,128)(2,1)} %get-tuple-element.49.grads_in, bf16[640,512]{1,0:T(8,128)(2,1)S(1)} %get-tuple-element.55.grad_q, bf16[4,4,512,512]{3,2,1,0:T(8,128)(2,1)} %weights.11), custom_call_target="tpu_custom_call" | custom-call | tf_op jit(solution)/shard_map/pallas_call | solution.py:42
  101.1 4.4 %shard_map.97 = bf16[2560,128]{1,0:T(8,128)(2,1)} custom-call(s32[2]{0:T(128)S(1)} %pad_add_fusion.info, f32[640,512]{1,0:T(8,128)S(1)} %shard_map.95.partial, f32[640,512]{1,0:T(8,128)S(1)} %get-tuple-element.56.grad_keys, f32[640,512]{1,0:T(8,128)S(1)} %get-tuple-element.57.grad_values, bf16[640,512]{1,0:T(8,128)(2,1)} %get-tuple-element.50.keys_in, ...), custom_call_target="tpu_custom_call" | custom-call | tf_op jit(solution)/shard_map/pallas_call | solution.py:42
  105.5 9.8 %all-to-all-start.3 = ((bf16[32,80,128]{2,1,0:T(8,128)(2,1)}), bf16[32,80,128]{2,1,0:T(8,128)(2,1)S(1)}, u32[]{:S(2)}, u32[]{:S(2)}) async-start(bf16[32,80,128]{2,1,0:T(8,128)(2,1)} %bitcast.13), calls=%async_computation.3 | async-start | bytes 1310720 | tf_op jit(solution)/shard_map/all_to_all | solution.py:639
  115.3 1.4 %shard_map.92 = bf16[512,512]{1,0:T(8,128)(2,1)} custom-call(bf16[512,640]{1,0:T(8,128)(2,1)S(1)} %copy-done, bf16[32,80,128]{2,1,0:T(8,128)(2,1)S(1)} %all-to-all-done.1.message), custom_call_target="tpu_custom_call" | custom-call | tf_op jit(solution)/shard_map/pallas_call | solution.py:42
  116.7 18.6 %all-to-all-done.3.message = bf16[32,80,128]{2,1,0:T(8,128)(2,1)S(1)} async-done(((bf16[32,80,128]{2,1,0:T(8,128)(2,1)}), bf16[32,80,128]{2,1,0:T(8,128)(2,1)S(1)}, u32[]{:S(2)}, u32[]{:S(2)}) %all-to-all-start.3) | async-done | bytes 655392 | tf_op jit(solution)/shard_map/all_to_all | solution.py:639
  135.3 1.4 %shard_map.98 = bf16[512,512]{1,0:T(8,128)(2,1)} custom-call(bf16[512,640]{1,0:T(8,128)(2,1)S(1)} %copy-done, bf16[32,80,128]{2,1,0:T(8,128)(2,1)S(1)} %all-to-all-done.3.message), custom_call_target="tpu_custom_call" | custom-call | tf_op jit(solution)/shard_map/pallas_call | solution.py:42
  (20 shorter events, 4.2 us)
Async XLA Ops:
  0.6 14.4 %copy-start.1 = (bf16[1,1,512,512]{3,2,1,0:T(8,128)(2,1)S(1)}, bf16[1,1,512,512]{3,2,1,0:T(8,128)(2,1)}, u32[]{:S(2)}) copy-start(bf16[1,1,512,512]{3,2,1,0:T(8,128)(2,1)} %param.13) | copy-start | bytes 1572868
  3.5 33.0 %all-to-all-start = ((bf16[32,88,128]{2,1,0:T(8,128)(2,1)}), bf16[32,88,128]{2,1,0:T(8,128)(2,1)S(1)}, u32[]{:S(2)}, u32[]{:S(2)}) async-start(bf16[32,88,128]{2,1,0:T(8,128)(2,1)} %get-tuple-element.33), calls=%async_computation | async-start | bytes 1441792 | tf_op jit(solution)/shard_map/all_to_all | solution.py:639
  14.9 26.6 %copy-start.2 = (f32[4,8]{1,0:T(4,128)S(1)}, f32[4,8]{1,0:T(4,128)}, u32[]{:S(2)}) copy-start(f32[4,8]{1,0:T(4,128)} %rates.1) | copy-start | bytes 388
  36.5 28.1 %all-to-all-start.2 = ((bf16[32,80,128]{2,1,0:T(8,128)(2,1)}), bf16[32,80,128]{2,1,0:T(8,128)(2,1)S(1)}, u32[]{:S(2)}, u32[]{:S(2)}) async-start(bf16[32,80,128]{2,1,0:T(8,128)(2,1)} %bitcast.15), calls=%async_computation.2 | async-start | bytes 1310720 | tf_op jit(solution)/shard_map/all_to_all | solution.py:639
  46.0 1.3 collective-permute-start
  48.1 10.2 %collective-permute-start.1 = (bf16[264,128]{1,0:T(8,128)(2,1)S(1)}, bf16[264,128]{1,0:T(8,128)(2,1)S(1)}, u32[]{:S(2)}, u32[]{:S(2)}) collective-permute-start(bf16[264,128]{1,0:T(8,128)(2,1)S(1)} %shard_map.90), channel_id=1, source_target_pairs={{0,2},{1,3},{2,4},{3,5},{4,6},{5,7},{8,10},{9,11},{10,12},{11,13},... | collective-permute-start | bytes 202760 | tf_op jit(solution)/shard_map/ppermute | solution.py:631
  49.4 8.9 %collective-permute-start.2 = (bf16[264,128]{1,0:T(8,128)(2,1)S(1)}, bf16[264,128]{1,0:T(8,128)(2,1)S(1)}, u32[]{:S(2)}, u32[]{:S(2)}) collective-permute-start(bf16[264,128]{1,0:T(8,128)(2,1)S(1)} %shard_map.90), channel_id=1, source_target_pairs={{0,4},{1,5},{2,6},{3,7},{8,12},{9,13},{10,14},{11,15},{16,20},{17,... | collective-permute-start | bytes 202760 | tf_op jit(solution)/shard_map/ppermute | solution.py:631
  50.7 9.5 %collective-permute-start.3 = (bf16[264,128]{1,0:T(8,128)(2,1)S(1)}, bf16[264,128]{1,0:T(8,128)(2,1)S(1)}, u32[]{:S(2)}, u32[]{:S(2)}) collective-permute-start(bf16[264,128]{1,0:T(8,128)(2,1)S(1)} %shard_map.90), channel_id=1, source_target_pairs={{0,6},{1,7},{8,14},{9,15},{16,22},{17,23},{24,30},{25,31},{32,38},... | collective-permute-start | bytes 202760 | tf_op jit(solution)/shard_map/ppermute | solution.py:631
  64.6 40.9 %all-to-all-start.1 = ((bf16[32,80,128]{2,1,0:T(8,128)(2,1)}), bf16[32,80,128]{2,1,0:T(8,128)(2,1)S(1)}, u32[]{:S(2)}, u32[]{:S(2)}) async-start(bf16[32,80,128]{2,1,0:T(8,128)(2,1)} %bitcast.14), calls=%async_computation.1 | async-start | bytes 1310720 | tf_op jit(solution)/shard_map/all_to_all | solution.py:639
  78.4 1.3 collective-permute-start.4
  80.4 20.6 %collective-permute-start.5 = (bf16[264,128]{1,0:T(8,128)(2,1)S(1)}, bf16[264,128]{1,0:T(8,128)(2,1)S(1)}, u32[]{:S(2)}, u32[]{:S(2)}) collective-permute-start(bf16[264,128]{1,0:T(8,128)(2,1)S(1)} %shard_map.96), channel_id=1, source_target_pairs={{2,0},{3,1},{4,2},{5,3},{6,4},{7,5},{10,8},{11,9},{12,10},{13,11},... | collective-permute-start | bytes 202760 | tf_op jit(solution)/shard_map/ppermute | solution.py:631
  82.5 18.5 %collective-permute-start.6 = (bf16[264,128]{1,0:T(8,128)(2,1)S(1)}, bf16[264,128]{1,0:T(8,128)(2,1)S(1)}, u32[]{:S(2)}, u32[]{:S(2)}) collective-permute-start(bf16[264,128]{1,0:T(8,128)(2,1)S(1)} %shard_map.96), channel_id=1, source_target_pairs={{4,0},{5,1},{6,2},{7,3},{12,8},{13,9},{14,10},{15,11},{20,16},{21,... | collective-permute-start | bytes 202760 | tf_op jit(solution)/shard_map/ppermute | solution.py:631
  89.8 11.3 %collective-permute-start.7 = (bf16[264,128]{1,0:T(8,128)(2,1)S(1)}, bf16[264,128]{1,0:T(8,128)(2,1)S(1)}, u32[]{:S(2)}, u32[]{:S(2)}) collective-permute-start(bf16[264,128]{1,0:T(8,128)(2,1)S(1)} %shard_map.96), channel_id=1, source_target_pairs={{6,0},{7,1},{14,8},{15,9},{22,16},{23,17},{30,24},{31,25},{38,32},... | collective-permute-start | bytes 202760 | tf_op jit(solution)/shard_map/ppermute | solution.py:631
  105.5 9.8 %copy-start = (bf16[512,640]{1,0:T(8,128)(2,1)S(1)}, bf16[512,640]{1,0:T(8,128)(2,1)}, u32[]{:S(2)}) copy-start(bf16[512,640]{1,0:T(8,128)(2,1)} %get-tuple-element.32.back) | copy-start | bytes 1966084
  105.5 29.7 %all-to-all-start.3 = ((bf16[32,80,128]{2,1,0:T(8,128)(2,1)}), bf16[32,80,128]{2,1,0:T(8,128)(2,1)S(1)}, u32[]{:S(2)}, u32[]{:S(2)}) async-start(bf16[32,80,128]{2,1,0:T(8,128)(2,1)} %bitcast.13), calls=%async_computation.3 | async-start | bytes 1310720 | tf_op jit(solution)/shard_map/all_to_all | solution.py:639

commit v6 on v4

--- a/solution.py
+++ b/solution.py
@@ -126,7 +126,7 @@
 
 def pack_events(
     owner_in, events_in, elapsed_in, resets_in, message, spots,
-    scratch, place, owner, events, elapsed, resets, sems,
+    scratch, place, earlier, owner, events, elapsed, resets, sems,
 ):
     copies = [
         pltpu.make_async_copy(source, target, sems.at[i])
@@ -141,15 +141,15 @@
     ]
     for copy in copies:
         copy.start()
+    rows, width = events.shape
+    earlier[...] = ones_where(iota((rows, rows), 0) < iota((rows, rows), 1))
     copies[0].wait()
-    rows, width = events.shape
     owners = message.shape[0]
     slots = place.shape[0]
     cap = slots // owners
     own = owner[...]
     hit = iota((owners, rows), 0) == own
-    earlier = ones_where(iota((rows, rows), 0) < iota((rows, rows), 1))
-    before = dot(ones_where(hit), earlier)
+    before = dot(ones_where(hit), earlier[...])
     rank = jnp.sum(jnp.where(hit, before, 0.0), axis=0, keepdims=True).astype(jnp.int32)
     spots[0:1, :] = own
     spots[1:2, :] = own * cap + rank
@@ -323,8 +323,8 @@
 
 def forward_state(
     info, rates, message, weights, expand, own_lanes,
-    x_out, keys, values, keys_out, values_out, fade, fade_t, marks, fall, send,
-    scratch, memory, mine, x, sems,
+    x_out, keys, values, keys_out, values_out, fade, fade_t, marks, fall, send, x,
+    scratch, memory, mine, sems,
 ):
     fetch = fetched(weights.at[info[0], pl.ds(1, 2)], mine, sems.at[1])
     slots, width = x.shape
@@ -384,14 +384,12 @@
 
 
 def attend(
-    info, x_in, weights, keys, values, fade, fade_t, marks,
+    info, x, weights, keys, values, fade, fade_t, marks,
     q8, attended_out, states, lift,
-    memory, attended, x, mine, in_sems, sems,
+    memory, attended, mine, in_sem, sems,
 ):
-    arrival = fetched(x_in, x, in_sems.at[0])
-    fetch = fetched(weights.at[info[0], 0], mine, in_sems.at[1])
+    fetch = fetched(weights.at[info[0], 0], mine, in_sem)
     lift[...] = parts_of(jnp.exp(fade[...]), 2)
-    arrival.wait()
     fetch.wait()
     for n in range(0, x.shape[1], WIDE):
         cols = slice(n, n + WIDE)
@@ -640,6 +638,7 @@
         [
             flat,
             pltpu.VMEM((slots, rows), bf16),
+            pltpu.VMEM((rows, rows), bf16),
             pltpu.VMEM((1, rows), jnp.int32),
             pltpu.VMEM((rows, width), bf16),
             pltpu.VMEM((1, rows), f32),
@@ -668,14 +667,15 @@
     flat_narrow = pltpu.VMEM(*flat_msg)
     rows16, rows32 = pltpu.VMEM(*wide16), pltpu.VMEM(*wide32)
     narrow_states = pltpu.VMEM((pairs // 2, WIDE, WIDE), bf16)
-    x, keys, values, keys_far, values_far, fade, fade_t, marks, fall, send = call(
+    x, keys, values, keys_far, values_far, fade, fade_t, marks, fall, send, x_near = call(
         forward_state,
         [
             wide16, wide16, wide16, wide16, wide16, ((slots, 128), f32), ((blocks, 8, 128), f32),
             ((blocks, 2 * pairs, 128), f32), ((slots, 128), bf16), state_msg,
+            wide16,
         ],
         [info, decay_rates, events_in, weights, expand, own_lanes],
-        [flat, state_vmem, two, rows16, sem((5,))],
+        [flat, state_vmem, two, sem((5,))],
         {0: SMEM, 1: SMEM, 3: HBM},
         (0, 3, 4),
     )
@@ -685,9 +685,9 @@
     q8, attended, kept, lift = call(
         attend,
         [wide16, wide32, ((blocks, pairs, 64, 128), bf16), ((slots, 128), bf16)],
-        [info, x, weights, keys, values, fade, fade_t, marks],
-        [state_vmem, rows32, rows16, one, sem((2,)), sem((blocks,))],
-        {0: SMEM, 1: HBM, 2: HBM},
+        [info, x_near, weights, keys, values, fade, fade_t, marks],
+        [state_vmem, rows32, one, sem, sem((blocks,))],
+        {0: SMEM, 2: HBM},
         (1,),
     )
     message, grads, grad_full, incoming, send = call(

time: 133 us -> 133 us (level)
  no operation moved by 1% of the time
where the time goes in v6:
time: 133 us; the launch traced here: 132 us
  starting transfers between devices  49.3 us (37%)
  waiting for transfers between devices  43.2 us (32%)
  Pallas kernels  38.3 us (29%)
    all_to_all x4, waiting for transfers between devices, regroup(): return lax.all_to_all(value, 'log', split_axis=0, concat_axis=0, tiled=True)  40.7 us
    pallas_call x11, Pallas kernels, call(): pl.pallas_call(body, out_shape=[pltpu.HBM(s, d) if i in out_hbm else jax....  38.3 us
    all_to_all x4, starting transfers between devices, regroup(): return lax.all_to_all(value, 'log', split_axis=0, concat_axis=0, tiled=True)  34.8 us
    ppermute x6, starting transfers between devices, exchange(): lax.ppermute(value, axis, [(i, i + sign * k) for i in range(count) if 0 <...  14.3 us
  transfers between devices with their start and end apart: 12, of which 5 were waited for; matrix products, arithmetic and copies ran while one was open for 0% of the time, Pallas kernels for 22%

profile of v6, /device:TPU:24, one launch (start us, length us, event | category | flops | bytes accessed | tf_op | source)
XLA Modules:
  0.0 131.8 jit_solution(15839282214543053911)
XLA Ops:
  0.6 2.9 %shard_map.86 = (bf16[32,88,128]{2,1,0:T(8,128)(2,1)}, s32[2,512]{1,0:T(2,128)S(1)}) custom-call(s32[1,512]{1,0:T(1,128)} %bitcast.19, bf16[512,512]{1,0:T(8,128)(2,1)} %bitcast.18, f32[1,512]{1,0:T(1,128)} %bitcast.20, f32[1,512]{1,0:T(1,128)} %bitcast.21), custom_call_target="tpu_custom_call" | custom-call | tf_op jit(solution)/shard_map/pallas_call | solution.py:42
  3.6 11.3 %all-to-all-start = ((bf16[32,88,128]{2,1,0:T(8,128)(2,1)}), bf16[32,88,128]{2,1,0:T(8,128)(2,1)S(1)}, u32[]{:S(2)}, u32[]{:S(2)}) async-start(bf16[32,88,128]{2,1,0:T(8,128)(2,1)} %get-tuple-element.33), calls=%async_computation | async-start | bytes 1441792 | tf_op jit(solution)/shard_map/all_to_all | solution.py:609
  15.0 2.7 %shard_map.87 = (bf16[2560,128]{1,0:T(8,128)(2,1)}, bf16[512,640]{1,0:T(8,128)(2,1)}, bf16[640,256]{1,0:T(8,128)(2,1)S(1)}, bf16[640,128]{1,0:T(8,128)(2,1)S(1)}) custom-call(s32[2]{0:T(128)S(1)} %pad_add_fusion.info, s32[2,512]{1,0:T(2,128)S(1)} %get-tuple-element.31.spots, bf16[512,512]{1,0:T(8,128)(2,1)S(1)} %bitcast.12), custom_call_target="tpu_custom_call" | custom-call | tf_op jit(solution)/shard_map/pallas_call | solution.py:42
  17.7 18.8 %all-to-all-done.message = bf16[32,88,128]{2,1,0:T(8,128)(2,1)S(1)} async-done(((bf16[32,88,128]{2,1,0:T(8,128)(2,1)}), bf16[32,88,128]{2,1,0:T(8,128)(2,1)S(1)}, u32[]{:S(2)}, u32[]{:S(2)}) %all-to-all-start) | async-done | bytes 720928 | tf_op jit(solution)/shard_map/all_to_all | solution.py:609
  36.5 5.0 %all-to-all-start.1 = ((bf16[32,80,128]{2,1,0:T(8,128)(2,1)}), bf16[32,80,128]{2,1,0:T(8,128)(2,1)S(1)}, u32[]{:S(2)}, u32[]{:S(2)}) async-start(bf16[32,80,128]{2,1,0:T(8,128)(2,1)} %bitcast.15), calls=%async_computation.1 | async-start | bytes 1310720 | tf_op jit(solution)/shard_map/all_to_all | solution.py:609
  41.5 4.0 %shard_map.88 = (bf16[640,512]{1,0:T(8,128)(2,1)}, bf16[640,512]{1,0:T(8,128)(2,1)S(1)}, bf16[640,512]{1,0:T(8,128)(2,1)S(1)}, bf16[640,512]{1,0:T(8,128)(2,1)},...) custom-call(s32[2]{0:T(128)S(1)} %pad_add_fusion.info, ...), custom_call_target="tpu_custom_call" | custom-call | tf_op jit(solution)/shard_map/pallas_call | solution.py:42
  45.6 1.2 collective-permute-done.other.partner
  47.6 1.3 collective-permute-start.1
  48.9 1.3 collective-permute-start.2
  50.2 1.3 collective-permute-start.3
  51.5 6.1 %shard_map.89 = (bf16[640,512]{1,0:T(8,128)(2,1)S(1)}, f32[640,512]{1,0:T(8,128)}, bf16[5,4,64,128]{3,2,1,0:T(8,128)(2,1)S(1)}, bf16[640,128]{1,0:T(8,128)(2,1)S(1)}) custom-call(s32[2]{0:T(128)S(1)} %pad_add_fusion.info, bf16[640,512]{1,0:T(8,128)(2,1)S(1)} %get-tuple-element.36.x, bf16[4,4,512,512]{3,2,1,0:T(8,128)(2,1)} %weights.9, ...), custom_call_target="tpu_custom_call" | custom-call | tf_op jit(solution)/shard_map/pallas_call | solution.py:42
  57.5 3.3 %all-to-all-done.1.message = bf16[32,80,128]{2,1,0:T(8,128)(2,1)S(1)} async-done(((bf16[32,80,128]{2,1,0:T(8,128)(2,1)}), bf16[32,80,128]{2,1,0:T(8,128)(2,1)S(1)}, u32[]{:S(2)}, u32[]{:S(2)}) %all-to-all-start.1) | async-done | bytes 655392 | tf_op jit(solution)/shard_map/all_to_all | solution.py:609
  60.8 5.3 %shard_map.91 = (bf16[2560,128]{1,0:T(8,128)(2,1)}, bf16[640,512]{1,0:T(8,128)(2,1)}, bf16[640,512]{1,0:T(8,128)(2,1)S(1)}, f32[4,64,128]{2,1,0:T(8,128)S(1)}, bf16[264,128]{1,0:T(8,128)(2,1)S(1)}) custom-call(s32[2]{0:T(128)S(1)} %pad_add_fusion.info, bf16[640,512]{1,0:T(8,128)(2,1)S(1)} %get-tuple-element.42.q8, ...), custom_call_target="tpu_custom_call" | custom-call | tf_op jit(solution)/shard_map/pallas_call | solution.py:42
  66.1 8.8 %all-to-all-start.2 = ((bf16[32,80,128]{2,1,0:T(8,128)(2,1)}), bf16[32,80,128]{2,1,0:T(8,128)(2,1)S(1)}, u32[]{:S(2)}, u32[]{:S(2)}) async-start(bf16[32,80,128]{2,1,0:T(8,128)(2,1)} %bitcast.14), calls=%async_computation.2 | async-start | bytes 1310720 | tf_op jit(solution)/shard_map/all_to_all | solution.py:609
  75.0 1.2 collective-permute-done.4.other.partner
  76.9 1.9 %collective-permute-start.5 = (bf16[264,128]{1,0:T(8,128)(2,1)S(1)}, bf16[264,128]{1,0:T(8,128)(2,1)S(1)}, u32[]{:S(2)}, u32[]{:S(2)}) collective-permute-start(bf16[264,128]{1,0:T(8,128)(2,1)S(1)} %shard_map.94), channel_id=1, source_target_pairs={{2,0},{3,1},{4,2},{5,3},{6,4},{7,5},{10,8},{11,9},{12,10},{13,11},... | collective-permute-start | bytes 202760 | tf_op jit(solution)/shard_map/ppermute | solution.py:601
  78.8 7.3 %collective-permute-start.6 = (bf16[264,128]{1,0:T(8,128)(2,1)S(1)}, bf16[264,128]{1,0:T(8,128)(2,1)S(1)}, u32[]{:S(2)}, u32[]{:S(2)}) collective-permute-start(bf16[264,128]{1,0:T(8,128)(2,1)S(1)} %shard_map.94), channel_id=1, source_target_pairs={{4,0},{5,1},{6,2},{7,3},{12,8},{13,9},{14,10},{15,11},{20,16},{21,... | collective-permute-start | bytes 202760 | tf_op jit(solution)/shard_map/ppermute | solution.py:601
  86.1 1.3 collective-permute-start.7
  87.4 8.7 %shard_map.93 = (f32[640,512]{1,0:T(8,128)S(1)}, f32[640,512]{1,0:T(8,128)S(1)}, f32[640,512]{1,0:T(8,128)S(1)}) custom-call(s32[2]{0:T(128)S(1)} %pad_add_fusion.info, bf16[640,512]{1,0:T(8,128)(2,1)S(1)} %get-tuple-element.42.q8, bf16[640,512]{1,0:T(8,128)(2,1)} %get-tuple-element.49.keys_in, bf16[640,512]{1,0:T(8,128)(2,1)} %get-tuple-element.50.values_in, ...), custom_call_target="tpu_custom_call" | custom-call | tf_op jit(solution)/shard_map/pallas_call | solution.py:42
  96.1 4.5 %shard_map.95 = bf16[2560,128]{1,0:T(8,128)(2,1)} custom-call(s32[2]{0:T(128)S(1)} %pad_add_fusion.info, f32[640,512]{1,0:T(8,128)S(1)} %get-tuple-element.55.partial, f32[640,512]{1,0:T(8,128)S(1)} %get-tuple-element.56.grad_keys, f32[640,512]{1,0:T(8,128)S(1)} %get-tuple-element.57.grad_values, bf16[640,512]{1,0:T(8,128)(2,1)} %get-tuple-element.49.keys_in, ...), custom_call_target="tpu_custom_call" | custom-call | tf_op jit(solution)/shard_map/pallas_call | solution.py:42
  100.6 9.7 %all-to-all-start.3 = ((bf16[32,80,128]{2,1,0:T(8,128)(2,1)}), bf16[32,80,128]{2,1,0:T(8,128)(2,1)S(1)}, u32[]{:S(2)}, u32[]{:S(2)}) async-start(bf16[32,80,128]{2,1,0:T(8,128)(2,1)} %bitcast.13), calls=%async_computation.3 | async-start | bytes 1310720 | tf_op jit(solution)/shard_map/all_to_all | solution.py:609
  110.4 1.4 %shard_map.92 = bf16[512,512]{1,0:T(8,128)(2,1)} custom-call(bf16[512,640]{1,0:T(8,128)(2,1)S(1)} %copy-done, bf16[32,80,128]{2,1,0:T(8,128)(2,1)S(1)} %all-to-all-done.2.message), custom_call_target="tpu_custom_call" | custom-call | tf_op jit(solution)/shard_map/pallas_call | solution.py:42
  111.8 18.5 %all-to-all-done.3.message = bf16[32,80,128]{2,1,0:T(8,128)(2,1)S(1)} async-done(((bf16[32,80,128]{2,1,0:T(8,128)(2,1)}), bf16[32,80,128]{2,1,0:T(8,128)(2,1)S(1)}, u32[]{:S(2)}, u32[]{:S(2)}) %all-to-all-start.3) | async-done | bytes 655392 | tf_op jit(solution)/shard_map/all_to_all | solution.py:609
  130.3 1.4 %shard_map.96 = bf16[512,512]{1,0:T(8,128)(2,1)} custom-call(bf16[512,640]{1,0:T(8,128)(2,1)S(1)} %copy-done, bf16[32,80,128]{2,1,0:T(8,128)(2,1)S(1)} %all-to-all-done.3.message), custom_call_target="tpu_custom_call" | custom-call | tf_op jit(solution)/shard_map/pallas_call | solution.py:42
  (18 shorter events, 1.7 us)
Async XLA Ops:
  0.6 14.4 %copy-start.1 = (bf16[1,1,512,512]{3,2,1,0:T(8,128)(2,1)S(1)}, bf16[1,1,512,512]{3,2,1,0:T(8,128)(2,1)}, u32[]{:S(2)}) copy-start(bf16[1,1,512,512]{3,2,1,0:T(8,128)(2,1)} %param.13) | copy-start | bytes 1572868
  3.6 33.0 %all-to-all-start = ((bf16[32,88,128]{2,1,0:T(8,128)(2,1)}), bf16[32,88,128]{2,1,0:T(8,128)(2,1)S(1)}, u32[]{:S(2)}, u32[]{:S(2)}) async-start(bf16[32,88,128]{2,1,0:T(8,128)(2,1)} %get-tuple-element.33), calls=%async_computation | async-start | bytes 1441792 | tf_op jit(solution)/shard_map/all_to_all | solution.py:609
  14.9 26.6 %copy-start.2 = (f32[4,8]{1,0:T(4,128)S(1)}, f32[4,8]{1,0:T(4,128)}, u32[]{:S(2)}) copy-start(f32[4,8]{1,0:T(4,128)} %rates.1) | copy-start | bytes 388
  36.5 24.3 %all-to-all-start.1 = ((bf16[32,80,128]{2,1,0:T(8,128)(2,1)}), bf16[32,80,128]{2,1,0:T(8,128)(2,1)S(1)}, u32[]{:S(2)}, u32[]{:S(2)}) async-start(bf16[32,80,128]{2,1,0:T(8,128)(2,1)} %bitcast.15), calls=%async_computation.1 | async-start | bytes 1310720 | tf_op jit(solution)/shard_map/all_to_all | solution.py:609
  45.5 1.3 %collective-permute-start = (bf16[264,128]{1,0:T(8,128)(2,1)S(1)}, bf16[264,128]{1,0:T(8,128)(2,1)S(1)}, u32[]{:S(2)}, u32[]{:S(2)}) collective-permute-start(bf16[264,128]{1,0:T(8,128)(2,1)S(1)} %get-tuple-element.47.own), channel_id=1, source_target_pairs={{0,1},{1,0},{2,3},{3,2},{4,5},{5,4},{6,7},{7,6},{8,9},{9,8},{10,11... | collective-permute-start | bytes 202760 | tf_op jit(solution)/shard_map/ppermute | solution.py:595
  47.6 13.3 %collective-permute-start.1 = (bf16[264,128]{1,0:T(8,128)(2,1)S(1)}, bf16[264,128]{1,0:T(8,128)(2,1)S(1)}, u32[]{:S(2)}, u32[]{:S(2)}) collective-permute-start(bf16[264,128]{1,0:T(8,128)(2,1)S(1)} %shard_map.90), channel_id=1, source_target_pairs={{0,2},{1,3},{2,4},{3,5},{4,6},{5,7},{8,10},{9,11},{10,12},{11,13},... | collective-permute-start | bytes 202760 | tf_op jit(solution)/shard_map/ppermute | solution.py:601
  48.9 12.0 %collective-permute-start.2 = (bf16[264,128]{1,0:T(8,128)(2,1)S(1)}, bf16[264,128]{1,0:T(8,128)(2,1)S(1)}, u32[]{:S(2)}, u32[]{:S(2)}) collective-permute-start(bf16[264,128]{1,0:T(8,128)(2,1)S(1)} %shard_map.90), channel_id=1, source_target_pairs={{0,4},{1,5},{2,6},{3,7},{8,12},{9,13},{10,14},{11,15},{16,20},{17,... | collective-permute-start | bytes 202760 | tf_op jit(solution)/shard_map/ppermute | solution.py:601
  50.2 10.7 %collective-permute-start.3 = (bf16[264,128]{1,0:T(8,128)(2,1)S(1)}, bf16[264,128]{1,0:T(8,128)(2,1)S(1)}, u32[]{:S(2)}, u32[]{:S(2)}) collective-permute-start(bf16[264,128]{1,0:T(8,128)(2,1)S(1)} %shard_map.90), channel_id=1, source_target_pairs={{0,6},{1,7},{8,14},{9,15},{16,22},{17,23},{24,30},{25,31},{32,38},... | collective-permute-start | bytes 202760 | tf_op jit(solution)/shard_map/ppermute | solution.py:601
  66.1 34.5 %all-to-all-start.2 = ((bf16[32,80,128]{2,1,0:T(8,128)(2,1)}), bf16[32,80,128]{2,1,0:T(8,128)(2,1)S(1)}, u32[]{:S(2)}, u32[]{:S(2)}) async-start(bf16[32,80,128]{2,1,0:T(8,128)(2,1)} %bitcast.14), calls=%async_computation.2 | async-start | bytes 1310720 | tf_op jit(solution)/shard_map/all_to_all | solution.py:609
  74.9 1.3 %collective-permute-start.4 = (bf16[264,128]{1,0:T(8,128)(2,1)S(1)}, bf16[264,128]{1,0:T(8,128)(2,1)S(1)}, u32[]{:S(2)}, u32[]{:S(2)}) collective-permute-start(bf16[264,128]{1,0:T(8,128)(2,1)S(1)} %get-tuple-element.59.own), channel_id=1, source_target_pairs={{0,1},{1,0},{2,3},{3,2},{4,5},{5,4},{6,7},{7,6},{8,9},{9,8},{10,11... | collective-permute-start | bytes 202760 | tf_op jit(solution)/shard_map/ppermute | solution.py:595
  76.9 19.1 %collective-permute-start.5 = (bf16[264,128]{1,0:T(8,128)(2,1)S(1)}, bf16[264,128]{1,0:T(8,128)(2,1)S(1)}, u32[]{:S(2)}, u32[]{:S(2)}) collective-permute-start(bf16[264,128]{1,0:T(8,128)(2,1)S(1)} %shard_map.94), channel_id=1, source_target_pairs={{2,0},{3,1},{4,2},{5,3},{6,4},{7,5},{10,8},{11,9},{12,10},{13,11},... | collective-permute-start | bytes 202760 | tf_op jit(solution)/shard_map/ppermute | solution.py:601
  78.8 17.3 %collective-permute-start.6 = (bf16[264,128]{1,0:T(8,128)(2,1)S(1)}, bf16[264,128]{1,0:T(8,128)(2,1)S(1)}, u32[]{:S(2)}, u32[]{:S(2)}) collective-permute-start(bf16[264,128]{1,0:T(8,128)(2,1)S(1)} %shard_map.94), channel_id=1, source_target_pairs={{4,0},{5,1},{6,2},{7,3},{12,8},{13,9},{14,10},{15,11},{20,16},{21,... | collective-permute-start | bytes 202760 | tf_op jit(solution)/shard_map/ppermute | solution.py:601
  86.1 10.0 %collective-permute-start.7 = (bf16[264,128]{1,0:T(8,128)(2,1)S(1)}, bf16[264,128]{1,0:T(8,128)(2,1)S(1)}, u32[]{:S(2)}, u32[]{:S(2)}) collective-permute-start(bf16[264,128]{1,0:T(8,128)(2,1)S(1)} %shard_map.94), channel_id=1, source_target_pairs={{6,0},{7,1},{14,8},{15,9},{22,16},{23,17},{30,24},{31,25},{38,32},... | collective-permute-start | bytes 202760 | tf_op jit(solution)/shard_map/ppermute | solution.py:601
  100.6 9.8 %copy-start = (bf16[512,640]{1,0:T(8,128)(2,1)S(1)}, bf16[512,640]{1,0:T(8,128)(2,1)}, u32[]{:S(2)}) copy-start(bf16[512,640]{1,0:T(8,128)(2,1)} %get-tuple-element.32.back) | copy-start | bytes 1966084
  100.6 29.7 %all-to-all-start.3 = ((bf16[32,80,128]{2,1,0:T(8,128)(2,1)}), bf16[32,80,128]{2,1,0:T(8,128)(2,1)S(1)}, u32[]{:S(2)}, u32[]{:S(2)}) async-start(bf16[32,80,128]{2,1,0:T(8,128)(2,1)} %bitcast.13), calls=%async_computation.3 | async-start | bytes 1310720 | tf_op jit(solution)/shard_map/all_to_all | solution.py:609
